TPU v7x, 32 devices: a whole 2x2x4 slice. The times are simulated.
32 devices in a mesh: dp: 2 (over x), ctx: 8 (over z, y), fsdp: 2 (over core).
Axes of the slice: x: 2, y: 2, z: 4, core: 2. Of those that a mesh axis runs over, the one named last changes fastest.
Arguments:
- tokens: bfloat16 [8, 1024, 1024], P(('dp', 'fsdp'), 'ctx'), may hold values from -6 to 6
- query_key_value_weight: bfloat16 [1024, 3072], P('fsdp'), may hold values from -0.1875 to 0.1875
- bias_query: bfloat16 [1024], P('fsdp'), may hold values from -4 to 4
- bias_value: bfloat16 [1024], P('fsdp'), may hold values from -0.3125 to 0.3125
- attention_out_weight: bfloat16 [1024, 1024], P('fsdp'), may hold values from -3.5 to 3.5
- attention_out_bias: bfloat16 [1024], P('fsdp'), may hold values from -4 to 4
- gain_one: bfloat16 [1024], P('fsdp'), may hold values from 0.5 to 1.5
- shift_one: bfloat16 [1024], P('fsdp'), may hold values from -4 to 4
- feedforward_in_weight: bfloat16 [1024, 4096], P('fsdp'), may hold values from -0.1875 to 0.1875
- feedforward_in_bias: bfloat16 [4096], P('fsdp'), may hold values from -4 to 4
- feedforward_out_weight: bfloat16 [4096, 1024], P('fsdp'), may hold values from -0.09375 to 0.09375
- feedforward_out_bias: bfloat16 [1024], P('fsdp'), may hold values from -4 to 4
- gain_two: bfloat16 [1024], P('fsdp'), may hold values from 0.5 to 1.5
- shift_two: bfloat16 [1024], P('fsdp'), may hold values from -4 to 4
- d_out: bfloat16 [8, 1024, 1024], P(('dp', 'fsdp'), 'ctx'), may hold values from -6 to 6
Outputs:
- output: bfloat16 [8, 1024, 1024], P(('dp', 'fsdp'), 'ctx')
- grad_tokens: float32 [8, 1024, 1024], P(('dp', 'fsdp'), 'ctx')
- grad_qkv: float32 [1024, 3072], P('fsdp')
- grad_bias_query: float32 [1024], P('fsdp')
- grad_bias_value: float32 [1024], P('fsdp')
- grad_out: float32 [1024, 1024], P('fsdp')
- grad_bias_out: float32 [1024], P('fsdp')
- grad_gain_one: float32 [1024], P('fsdp')
- grad_shift_one: float32 [1024], P('fsdp')
- grad_in: float32 [1024, 4096], P('fsdp')
- grad_bias_in: float32 [4096], P('fsdp')
- grad_back: float32 [4096, 1024], P('fsdp')
- grad_bias_back: float32 [1024], P('fsdp')
- grad_gain_two: float32 [1024], P('fsdp')
- grad_shift_two: float32 [1024], P('fsdp')
All inputs are finite; a program needn't handle non-finite values.
Results may differ from a plain program's by a relative error of at most 0.025.
Values may be sent and summed in bfloat16 or wider, within the bound.
No kernel may reach another device: no remote copies, remote signals or barrier semaphores. Data moves between devices by JAX's collectives and lax.ppermute only.
A program may use at most 192 MiB of HBM per device.

v0:
```python
from functools import partial

import jax
import jax.numpy as jnp
from jax import lax
from jax.sharding import PartitionSpec as P

HEADS = 16
HEAD_DIM = 64


EPSILON = 1e-06


def from_behind(block, axis, distance):
    devices = range(lax.axis_size(axis))
    route = [((i - distance) % len(devices), i) for i in devices]
    return lax.ppermute(block, axis, route)


def norm_apply(values, gain_vec, shift_vec):
    centre = jnp.mean(values, axis=-1, keepdims=True)
    centred = values - centre
    variance = jnp.mean(centred * centred, axis=-1, keepdims=True)
    return centred * lax.rsqrt(variance + EPSILON) * gain_vec + shift_vec


def lowered(values):
    return values.astype(jnp.bfloat16)


def widened(values):
    return values.astype(jnp.float32)


def project(left_operand_rows, right_operand_matrix):
    return jnp.einsum(
        "ugj,jn->ugn", left_operand_rows, right_operand_matrix, preferred_element_type=jnp.float32
    )


def weight_grad(left_operand_rows, gradient_row_block):
    return jnp.einsum(
        "xrb,xrw->bw", left_operand_rows, gradient_row_block, preferred_element_type=jnp.float32
    )


def back_project(gradient_row_block, right_operand_matrix):
    return jnp.einsum(
        "wkb,fb->wkf", gradient_row_block, right_operand_matrix, preferred_element_type=jnp.float32
    )


def column_sum(values):
    return jnp.sum(widened(values), axis=(0, 1))


def split_heads(values):
    return values.reshape(values.shape[0], values.shape[1], HEADS, HEAD_DIM)


def merge_heads(values):
    return values.reshape(values.shape[0], values.shape[1], HEADS * HEAD_DIM)


def split_blocks(values, block_rows):
    seq_count = values.shape[0]
    blocks = values.shape[1] // block_rows
    return jnp.moveaxis(values.reshape(seq_count, blocks, block_rows, values.shape[2]), 1, 0)


def block_scores(query_rows, key_rows):
    scores = jnp.einsum(
        "sqhd,skhd->shqk",
        split_heads(query_rows),
        split_heads(key_rows),
        preferred_element_type=jnp.float32,
    )
    return scores * HEAD_DIM ** (-0.5)


def fold_block(state_now, key_block, value_block, query_rows):
    running_max, running_sum, running_acc = state_now
    scores = block_scores(query_rows, key_block)
    new_max = jnp.maximum(running_max, jnp.max(scores, axis=-1))
    rescale = jnp.exp(running_max - new_max)
    weights = jnp.exp(scores - new_max[..., None])
    new_sum = running_sum * rescale + jnp.sum(weights, axis=-1)
    product = jnp.einsum(
        "shqk,skhd->shqd",
        lowered(weights),
        split_heads(value_block),
        preferred_element_type=jnp.float32,
    )
    return (new_max, new_sum, running_acc * rescale[..., None] + product)


def attend_forward(query_rows, key_rows, value_rows):
    seq_count = query_rows.shape[0]
    block_rows = query_rows.shape[1]
    initial = (
        jnp.full((seq_count, HEADS, block_rows), -1e30, jnp.float32),
        jnp.zeros((seq_count, HEADS, block_rows), jnp.float32),
        jnp.zeros((seq_count, HEADS, block_rows, HEAD_DIM), jnp.float32),
    )
    kept = None
    key_part = lax.all_gather(key_rows, "ctx", axis=1, tiled=True)
    value_part = lax.all_gather(value_rows, "ctx", axis=1, tiled=True)

    def one_block(state_in, block_pair):
        return (fold_block(state_in, block_pair[0], block_pair[1], query_rows), None)

    state_out, unused = lax.scan(
        one_block,
        initial,
        (split_blocks(key_part, block_rows), split_blocks(value_part, block_rows)),
    )
    running_max, running_sum, running_acc = state_out
    attention_result = running_acc / running_sum[..., None]
    attention_result = jnp.transpose(attention_result, (0, 2, 1, 3)).reshape(
        seq_count, block_rows, HEADS * HEAD_DIM
    )
    log_total = running_max + jnp.log(running_sum)
    return (attention_result, log_total, kept)


def attend_back(query_rows, gradient_row_block, log_total, row_inner, key_rows, value_rows):
    score_scale = HEAD_DIM ** (-0.5)
    scores = block_scores(query_rows, key_rows)
    probabilities = jnp.exp(scores - log_total[..., None])
    value_grad = jnp.einsum(
        "shqk,sqhd->skhd",
        lowered(probabilities),
        split_heads(gradient_row_block),
        preferred_element_type=jnp.float32,
    )
    prob_grad = jnp.einsum(
        "sqhd,skhd->shqk",
        split_heads(gradient_row_block),
        split_heads(value_rows),
        preferred_element_type=jnp.float32,
    )
    score_grad = lowered(probabilities * (prob_grad - row_inner[..., None]))
    query_grad = (
        jnp.einsum(
            "shqk,skhd->sqhd", score_grad, split_heads(key_rows), preferred_element_type=jnp.float32
        )
        * score_scale
    )
    key_grad = (
        jnp.einsum(
            "shqk,sqhd->skhd",
            score_grad,
            split_heads(query_rows),
            preferred_element_type=jnp.float32,
        )
        * score_scale
    )
    return (merge_heads(query_grad), merge_heads(key_grad), merge_heads(value_grad))


def attend_backward(query_rows, gradient_row_block, log_total, row_inner, key_rows, value_rows):
    zero_rows = jnp.zeros(query_rows.shape, jnp.float32)
    turn_count = lax.axis_size("ctx") // 2

    def turn_keys(turn_index, carried):
        moving_key, moving_value, key_acc, value_acc, query_acc = carried
        for half_step in range(2):
            pieces = attend_back(
                query_rows, gradient_row_block, log_total, row_inner, moving_key, moving_value
            )
            query_acc = query_acc + pieces[0]
            key_acc = key_acc + pieces[1]
            value_acc = value_acc + pieces[2]
            moving_key, moving_value = from_behind((moving_key, moving_value), "ctx", 1)
            key_acc, value_acc = (
                from_behind(key_acc.astype(jnp.bfloat16), "ctx", 1).astype(key_acc.dtype),
                from_behind(value_acc.astype(jnp.bfloat16), "ctx", 1).astype(value_acc.dtype),
            )
        return (moving_key, moving_value, key_acc, value_acc, query_acc)

    finished = lax.fori_loop(
        0, turn_count, turn_keys, (key_rows, value_rows, zero_rows, zero_rows, zero_rows)
    )
    return (finished[4], finished[2], finished[3])


def on_device(
    tokens,
    query_key_value_weight,
    bias_query,
    bias_value,
    attention_out_weight,
    attention_out_bias,
    gain_one,
    shift_one,
    feedforward_in_weight,
    feedforward_in_bias,
    feedforward_out_weight,
    feedforward_out_bias,
    gain_two,
    shift_two,
    d_out,
):
    attn_full = (
        lax.all_gather(query_key_value_weight, "fsdp", axis=0, tiled=True),
        lax.all_gather(attention_out_weight, "fsdp", axis=0, tiled=True),
        lax.all_gather(bias_query, "fsdp", axis=0, tiled=True),
        lax.all_gather(bias_value, "fsdp", axis=0, tiled=True),
        lax.all_gather(attention_out_bias, "fsdp", axis=0, tiled=True),
        lax.all_gather(gain_one, "fsdp", axis=0, tiled=True),
        lax.all_gather(shift_one, "fsdp", axis=0, tiled=True),
    )
    qkv_full, out_full, query_bias, value_bias, out_bias, gain_first, shift_first = attn_full
    model_width = out_full.shape[0]
    projected_rows = project(tokens, qkv_full) + jnp.concatenate(
        [widened(query_bias), jnp.zeros((model_width,), jnp.float32), widened(value_bias)]
    )
    projected_low = lowered(projected_rows)
    query_rows = projected_low[..., :model_width]
    key_rows = projected_low[..., model_width : 2 * model_width]
    value_rows = projected_low[..., 2 * model_width :]
    attention_result, log_total, kept = attend_forward(query_rows, key_rows, value_rows)
    attended_low = lowered(attention_result)
    attention_branch = project(attended_low, out_full) + widened(out_bias)
    summed_one = widened(tokens) + attention_branch
    first_normalized, pull_one = jax.vjp(
        norm_apply, summed_one, widened(gain_first), widened(shift_first)
    )
    normed_low = lowered(first_normalized)
    ffn_full = (
        lax.all_gather(feedforward_in_weight, "fsdp", axis=0, tiled=True),
        lax.all_gather(feedforward_out_weight, "fsdp", axis=0, tiled=True),
        lax.all_gather(feedforward_in_bias, "fsdp", axis=0, tiled=True),
        lax.all_gather(feedforward_out_bias, "fsdp", axis=0, tiled=True),
        lax.all_gather(gain_two, "fsdp", axis=0, tiled=True),
        lax.all_gather(shift_two, "fsdp", axis=0, tiled=True),
    )
    in_full, back_full, inner_bias, back_bias, gain_second, shift_second = ffn_full
    hidden_before_gelu = project(normed_low, in_full) + widened(inner_bias)
    active_low = lowered(jax.nn.gelu(hidden_before_gelu, approximate=False))
    feedforward_branch = project(active_low, back_full) + widened(back_bias)

    def second_norm(residual_in, branch_in, gain_vec, shift_vec):
        return norm_apply(residual_in + branch_in, gain_vec, shift_vec)

    result, pull_two = jax.vjp(
        second_norm,
        first_normalized,
        feedforward_branch,
        widened(gain_second),
        widened(shift_second),
    )
    output = lowered(result)
    first_grad_res, second_grad, gain_two_grad, shift_two_grad = pull_two(widened(d_out))
    in_full, back_full = (
        lax.all_gather(feedforward_in_weight, "fsdp", axis=0, tiled=True),
        lax.all_gather(feedforward_out_weight, "fsdp", axis=0, tiled=True),
    )
    second_low = lowered(second_grad)
    back_grad = weight_grad(active_low, second_low)
    back_bias_grad = column_sum(second_low)
    active_grad = back_project(second_low, back_full)
    gelu_pull = jax.vjp(partial(jax.nn.gelu, approximate=False), hidden_before_gelu)[1]
    hidden_low = lowered(gelu_pull(active_grad)[0])
    in_grad = weight_grad(normed_low, hidden_low)
    in_bias_grad = column_sum(hidden_low)
    first_grad = first_grad_res + back_project(hidden_low, in_full)
    ffn_grads = (
        lax.psum_scatter(
            in_grad.astype(jnp.bfloat16), "fsdp", scatter_dimension=0, tiled=True
        ).astype(jnp.float32),
        lax.psum_scatter(
            in_bias_grad.astype(jnp.bfloat16), "fsdp", scatter_dimension=0, tiled=True
        ).astype(jnp.float32),
        lax.psum_scatter(
            back_grad.astype(jnp.bfloat16), "fsdp", scatter_dimension=0, tiled=True
        ).astype(jnp.float32),
        lax.psum_scatter(
            back_bias_grad.astype(jnp.bfloat16), "fsdp", scatter_dimension=0, tiled=True
        ).astype(jnp.float32),
        lax.psum_scatter(
            gain_two_grad.astype(jnp.bfloat16), "fsdp", scatter_dimension=0, tiled=True
        ).astype(jnp.float32),
        lax.psum_scatter(
            shift_two_grad.astype(jnp.bfloat16), "fsdp", scatter_dimension=0, tiled=True
        ).astype(jnp.float32),
    )
    ffn_grads = lax.psum(
        (ffn_grads[0], ffn_grads[1], ffn_grads[2], ffn_grads[3], ffn_grads[4], ffn_grads[5]),
        ("dp", "ctx"),
    )
    summed_grad, gain_one_grad, shift_one_grad = pull_one(first_grad)
    qkv_full, out_full = (
        lax.all_gather(query_key_value_weight, "fsdp", axis=0, tiled=True),
        lax.all_gather(attention_out_weight, "fsdp", axis=0, tiled=True),
    )
    branch_low = lowered(summed_grad)
    out_grad = weight_grad(attended_low, branch_low)
    out_bias_grad = column_sum(branch_low)
    attended_grad_low = lowered(back_project(branch_low, out_full))
    row_inner = jnp.sum(
        split_heads(widened(attended_grad_low)) * split_heads(attention_result), axis=-1
    )
    row_inner = jnp.transpose(row_inner, (0, 2, 1))
    query_grad, key_grad, value_grad = attend_backward(
        query_rows, attended_grad_low, log_total, row_inner, key_rows, value_rows
    )
    mixed_grad = lowered(jnp.concatenate([query_grad, key_grad, value_grad], axis=-1))
    qkv_grad = weight_grad(tokens, mixed_grad)
    bias_grads = column_sum(mixed_grad)
    query_bias_grad = bias_grads[:model_width]
    value_bias_grad = bias_grads[2 * model_width :]
    token_grad = summed_grad + back_project(mixed_grad, qkv_full)
    attn_grads = (
        lax.psum_scatter(
            qkv_grad.astype(jnp.bfloat16), "fsdp", scatter_dimension=0, tiled=True
        ).astype(jnp.float32),
        lax.psum_scatter(
            query_bias_grad.astype(jnp.bfloat16), "fsdp", scatter_dimension=0, tiled=True
        ).astype(jnp.float32),
        lax.psum_scatter(
            value_bias_grad.astype(jnp.bfloat16), "fsdp", scatter_dimension=0, tiled=True
        ).astype(jnp.float32),
        lax.psum_scatter(
            out_grad.astype(jnp.bfloat16), "fsdp", scatter_dimension=0, tiled=True
        ).astype(jnp.float32),
        lax.psum_scatter(
            out_bias_grad.astype(jnp.bfloat16), "fsdp", scatter_dimension=0, tiled=True
        ).astype(jnp.float32),
        lax.psum_scatter(
            gain_one_grad.astype(jnp.bfloat16), "fsdp", scatter_dimension=0, tiled=True
        ).astype(jnp.float32),
        lax.psum_scatter(
            shift_one_grad.astype(jnp.bfloat16), "fsdp", scatter_dimension=0, tiled=True
        ).astype(jnp.float32),
    )
    attn_grads = lax.psum(
        (
            attn_grads[0],
            attn_grads[1],
            attn_grads[2],
            attn_grads[3],
            attn_grads[4],
            attn_grads[5],
            attn_grads[6],
        ),
        ("dp", "ctx"),
    )
    return (
        output,
        token_grad,
        attn_grads[0],
        attn_grads[1],
        attn_grads[2],
        attn_grads[3],
        attn_grads[4],
        attn_grads[5],
        attn_grads[6],
        ffn_grads[0],
        ffn_grads[1],
        ffn_grads[2],
        ffn_grads[3],
        ffn_grads[4],
        ffn_grads[5],
    )


def solution(mesh):
    in_specs = (
        P(("dp", "fsdp"), "ctx", None),
        P("fsdp", None),
        P("fsdp"),
        P("fsdp"),
        P("fsdp", None),
        P("fsdp"),
        P("fsdp"),
        P("fsdp"),
        P("fsdp", None),
        P("fsdp"),
        P("fsdp", None),
        P("fsdp"),
        P("fsdp"),
        P("fsdp"),
        P(("dp", "fsdp"), "ctx", None),
    )
    out_specs = (
        P(("dp", "fsdp"), "ctx", None),
        P(("dp", "fsdp"), "ctx", None),
        P("fsdp", None),
        P("fsdp"),
        P("fsdp"),
        P("fsdp", None),
        P("fsdp"),
        P("fsdp"),
        P("fsdp"),
        P("fsdp", None),
        P("fsdp"),
        P("fsdp", None),
        P("fsdp"),
        P("fsdp"),
        P("fsdp"),
    )
    return jax.shard_map(
        on_device, mesh=mesh, in_specs=in_specs, out_specs=out_specs, check_vma=False
    )
```

profile of v0, /device:TPU:0, one launch (start us, length us, event | category | flops | bytes accessed | tf_op | source)
XLA Modules:
  0.0 1763.5 jit_solution(14789245049256892644)
XLA Ops:
  13.0 16.0 all-gather.15.cloned.1.call-done
  29.0 4.8 fusion.51
  53.1 56.5 %all-gather.19.cloned.1.call-done = bf16[2,1024,1024]{2,1,0:T(8,128)(2,1)} async-done(((bf16[2,128,1024]{2,1,0:T(8,128)(2,1)}), bf16[2,1024,1024]{2,1,0:T(8,128)(2,1)}) %all-gather.19.cloned.1.call-update) | async-done | bytes 4194320 | tf_op jit(solution)/shard_map/all_gather | solution.py:108
  109.7 6.4 copy.66
  116.1 68.0 %all-gather.17.cloned.1.call-done = bf16[2,1024,1024]{2,1,0:T(8,128)(2,1)} async-done(((bf16[2,128,1024]{2,1,0:T(8,128)(2,1)}), bf16[2,1024,1024]{2,1,0:T(8,128)(2,1)}) %all-gather.17.cloned.1.call-update) | async-done | bytes 4194320 | tf_op jit(solution)/shard_map/all_gather | solution.py:107
  184.1 6.4 copy.65
  190.5 24.1 %while.34 = (s32[]{:T(128)}, f32[2,16,128]{2,1,0:T(8,128)S(1)}, f32[2,16,128]{2,1,0:T(8,128)S(1)}, f32[2,16,128,64]{2,3,1,0:T(8,128)S(1)}, bf16[8,2,128,1024]{2,...) while((s32[]{:T(128)}, f32[2,16,128]{2,1,0:T(8,128)S(1)}, ...), condition=%wide.region_3.4_spmd.clone, body=%wide.region_0.3_spmd.clone.sunk | while | flops 139218944 | bytes 12320885 | solution.py:113
  214.8 2.7 fusion.99
  217.8 7.2 fusion.85
  227.1 10.8 multiply_convert_fusion.2
  239.3 6.6 fusion.100
  248.3 7.5 fusion.101
  255.8 7.0 multiply_reduce_fusion
  267.5 3.1 bitcast_convert_fusion.3
  272.3 378.4 %while.35 = (s32[]{:T(128)}, bf16[2,128,1024]{1,2,0:T(8,128)(2,1)}, bf16[2,128,1024]{1,2,0:T(8,128)(2,1)}, f32[2,128,1024]{1,2,0:T(8,128)}, f32[2,128,1024]{1,2,...) while((s32[]{:T(128)}, bf16[2,128,1024]{1,2,0:T(8,128)(2,1)}, ...), condition=%wide.region_14.15_spmd.clone, body=%wide.region_13.14_spmd.clone.sunk | while | flops 684982272 | bytes 82936368 | solution.py:182
  277.2 2.6 multiply_convert_fusion.6
  292.4 9.0 collective-permute-done.2
  301.4 2.6 multiply_convert_fusion.5
  304.4 8.2 collective-permute-done.4
  315.0 8.7 collective-permute-done.6
  328.2 6.8 collective-permute-done.5
  336.0 10.2 collective-permute-done.7
  347.3 10.3 collective-permute-done.1
  357.6 10.7 collective-permute-done.3
  371.2 2.6 multiply_convert_fusion.6
  376.1 2.6 fusion.199
  387.7 9.7 collective-permute-done.2
  397.4 2.6 multiply_convert_fusion.5
  400.4 8.2 collective-permute-done.4
  411.0 8.7 collective-permute-done.6
  422.3 8.7 collective-permute-done.5
  432.0 10.2 collective-permute-done.7
  443.3 10.3 collective-permute-done.1
  453.6 9.8 collective-permute-done.3
  469.9 2.6 fusion.199
  478.3 2.9 collective-permute-done
  482.8 9.7 collective-permute-done.2
  492.5 2.6 multiply_convert_fusion.5
  495.5 8.2 collective-permute-done.4
  506.1 8.7 collective-permute-done.6
  517.4 8.7 collective-permute-done.5
  527.1 10.2 collective-permute-done.7
  538.4 10.3 collective-permute-done.1
  548.6 8.9 collective-permute-done.3
  559.1 2.6 multiply_convert_fusion.6
  564.0 2.6 fusion.199
  570.6 4.8 collective-permute-done
  576.9 9.7 collective-permute-done.2
  586.6 2.6 multiply_convert_fusion.5
  589.6 8.2 collective-permute-done.4
  600.2 8.7 collective-permute-done.6
  611.5 8.7 collective-permute-done.5
  621.3 10.2 collective-permute-done.7
  632.5 10.3 collective-permute-done.1
  642.8 7.9 collective-permute-done.3
  656.3 4.5 fusion.39
  662.8 7.0 bitcast_convert_fusion.1
  671.6 5.8 bitcast_convert_fusion
  680.2 3.4 all-reduce.10
  683.9 6.9 fusion.64
  690.9 2.7 reduce-scatter.9.cloned.1.call-done
  693.6 20.9 %reduce-scatter.11.cloned.1.call-done = bf16[2048,1024]{1,0:T(8,128)(2,1)} async-done(((bf16[4096,1024]{1,0:T(8,128)(2,1)}), bf16[2048,1024]{1,0:T(8,128)(2,1)}) %reduce-scatter.11.cloned.1.call-update) | async-done | bytes 4194320 | tf_op jit(solution)/shard_map/reduce_scatter | solution.py:276
  714.5 1035.3 %all-reduce.12 = (f32[512,3072]{0,1:T(8,128)}, f32[512]{0:T(512)}, f32[512]{0:T(512)}, f32[512,1024]{1,0:T(8,128)}, f32[512]{0:T(512)}, /*index=5*/f32[512]{0:T(...) all-reduce(bf16[512,3072]{0,1:T(8,128)(2,1)} %reduce-scatter.5.clon, ...), channel_id=1, replica_groups=mesh['dp'=2,'ctx'=8,'fsdp'=2] {'dp','ctx'}, use_global_device_ids=true, to_apply=%region_16.17 | all-reduce | flops 6297600 | bytes 37797888 | tf_op jit(solution)/shard_map/psum | solution.py:338
  1749.9 6.6 copy.80
  (341 shorter events, 158.4 us)
Async XLA Ops:
  7.2 21.9 %all-gather.15.cloned.1.call-start = ((), (), s32[]{:S(2)}) async-start(), calls=%async_computation.4 | async-start | bytes 9437184 | tf_op jit(solution)/shard_map/all_gather | solution.py:206
  7.9 101.7 %all-gather.19.cloned.1.call-start = ((), (), s32[]{:S(2)}) async-start(), calls=%async_computation.6 | async-start | bytes 4718592 | tf_op jit(solution)/shard_map/all_gather | solution.py:108
  34.9 149.1 %all-gather.17.cloned.1.call-start = ((), (), s32[]{:S(2)}) async-start(), calls=%async_computation.5 | async-start | bytes 4718592 | tf_op jit(solution)/shard_map/all_gather | solution.py:107
  35.7 179.1 %all-gather.21.cloned.1.call-start = ((), (), s32[]{:S(2)}) async-start(), calls=%async_computation.7 | async-start | bytes 3145728 | tf_op jit(solution)/shard_map/all_gather | solution.py:207
  36.3 6.8 copy-start.34
  36.3 8.6 copy-start.35
  36.3 10.4 copy-start.36
  36.3 12.2 copy-start.30
  36.3 14.5 copy-start.11
  36.4 15.5 copy-start.10
  36.4 181.4 %all-gather.23.cloned.1.call-start = ((), (), s32[]{:S(2)}) async-start(), calls=%async_computation.8 | async-start | bytes 12582912 | tf_op jit(solution)/shard_map/all_gather | solution.py:232
  37.0 202.3 %all-gather.25.cloned.1.call-start = ((), (), s32[]{:S(2)}) async-start(), calls=%async_computation.9 | async-start | bytes 12582912 | tf_op jit(solution)/shard_map/all_gather | solution.py:233
  37.5 653.4 %reduce-scatter.7.cloned.1.call-start = ((), (), s32[]{:S(2)}) async-start(), calls=%async_computation.11 | async-start | bytes 3145728 | tf_op jit(solution)/shard_map/reduce_scatter | solution.py:325
  214.8 10.2 copy-start.7
  217.5 45.4 %copy-start.4 = (f32[2,128,1024]{2,1,0:T(8,128)}, f32[2,128,1024]{2,1,0:T(8,128)S(1)}, u32[]{:S(2)}) copy-start(f32[2,128,1024]{2,1,0:T(8,128)S(1)} %get-tuple-element.356) | copy-start | bytes 3145732
  239.3 6.6 copy-start.9
  239.3 8.9 copy-start.16
  248.2 7.5 copy-start.17
  255.8 7.0 copy-start.19
  272.3 418.6 %reduce-scatter.5.cloned.1.call-start = ((), (), s32[]{:S(2)}) async-start(), calls=%async_computation.10 | async-start | bytes 9437184 | tf_op jit(solution)/shard_map/reduce_scatter | solution.py:316
  272.4 18.5 %collective-permute-start = (bf16[2,128,1024]{1,2,0:T(8,128)(2,1)}, bf16[2,128,1024]{1,2,0:T(8,128)(2,1)}, u32[]{:S(2)}, u32[]{:S(2)}) collective-permute-start(bf16[2,128,1024]{1,2,0:T(8,128)(2,1)} %get-tuple-element.527), channel_id=1, source_target_pairs={{14,0},{0,2},{2,4},{4,6},{6,8},{8,10},{10,12},{12,14},{15,1},{1,3}... | collective-permute-start | bytes 1572872 | tf_op jit(solution)/shard_map/while/body/eval_jaxpr/ppermute | solution.py:18
  274.2 27.2 %collective-permute-start.2 = (bf16[2,128,1024]{1,2,0:T(8,128)(2,1)}, bf16[2,128,1024]{1,2,0:T(8,128)(2,1)}, u32[]{:S(2)}, u32[]{:S(2)}) collective-permute-start(bf16[2,128,1024]{1,2,0:T(8,128)(2,1)} %get-tuple-element.528), channel_id=1, source_target_pairs={{14,0},{0,2},{2,4},{4,6},{6,8},{8,10},{10,12},{12,14},{15,1},{1,3}... | collective-permute-start | bytes 1572872 | tf_op jit(solution)/shard_map/while/body/eval_jaxpr/ppermute | solution.py:18
  284.5 28.1 %collective-permute-start.4 = (bf16[2,128,1024]{1,2,0:T(8,128)(2,1)}, bf16[2,128,1024]{1,2,0:T(8,128)(2,1)}, u32[]{:S(2)}, u32[]{:S(2)}) collective-permute-start(bf16[2,128,1024]{1,2,0:T(8,128)(2,1)} %fusion.199), channel_id=1, source_target_pairs={{14,0},{0,2},{2,4},{4,6},{6,8},{8,10},{10,12},{12,14},{15,1},{1,3}... | collective-permute-start | bytes 1572872 | tf_op jit(solution)/shard_map/while/body/eval_jaxpr/ppermute | solution.py:18
  287.2 36.6 %collective-permute-start.6 = (bf16[2,128,1024]{1,2,0:T(8,128)(2,1)S(1)}, bf16[2,128,1024]{1,2,0:T(8,128)(2,1)S(1)}, u32[]{:S(2)}, u32[]{:S(2)}) collective-permute-start(bf16[2,128,1024]{1,2,0:T(8,128)(2,1)S(1)} %fusion.203), channel_id=1, source_target_pairs={{14,0},{0,2},{2,4},{4,6},{6,8},{8,10},{10,12},{12,14},{15,1},{1,3}... | collective-permute-start | bytes 1572872 | tf_op jit(solution)/shard_map/while/body/eval_jaxpr/ppermute | solution.py:18
  313.9 14.0 copy-start.1
  313.9 21.1 %collective-permute-start.5 = (bf16[2,128,1024]{1,2,0:T(8,128)(2,1)S(1)}, bf16[2,128,1024]{1,2,0:T(8,128)(2,1)S(1)}, u32[]{:S(2)}, u32[]{:S(2)}) collective-permute-start(bf16[2,128,1024]{1,2,0:T(8,128)(2,1)S(1)} %fusion.200), channel_id=1, source_target_pairs={{14,0},{0,2},{2,4},{4,6},{6,8},{8,10},{10,12},{12,14},{15,1},{1,3}... | collective-permute-start | bytes 1572872 | tf_op jit(solution)/shard_map/while/body/eval_jaxpr/ppermute | solution.py:18
  323.9 22.3 %collective-permute-start.7 = (bf16[2,128,1024]{1,2,0:T(8,128)(2,1)S(1)}, bf16[2,128,1024]{1,2,0:T(8,128)(2,1)S(1)}, u32[]{:S(2)}, u32[]{:S(2)}) collective-permute-start(bf16[2,128,1024]{1,2,0:T(8,128)(2,1)S(1)} %fusion.204), channel_id=1, source_target_pairs={{14,0},{0,2},{2,4},{4,6},{6,8},{8,10},{10,12},{12,14},{15,1},{1,3}... | collective-permute-start | bytes 1572872 | tf_op jit(solution)/shard_map/while/body/eval_jaxpr/ppermute | solution.py:18
  324.0 33.6 %collective-permute-start.1 = (bf16[2,128,1024]{1,2,0:T(8,128)(2,1)}, bf16[2,128,1024]{1,2,0:T(8,128)(2,1)}, u32[]{:S(2)}, u32[]{:S(2)}) collective-permute-start(bf16[2,128,1024]{1,2,0:T(8,128)(2,1)} %collective-permute-done), channel_id=1, source_target_pairs={{14,0},{0,2},{2,4},{4,6},{6,8},{8,10},{10,12},{12,14},{15,1},{1,3}... | collective-permute-start | bytes 1572872 | tf_op jit(solution)/shard_map/while/body/eval_jaxpr/ppermute | solution.py:18
  325.4 42.9 %collective-permute-start.3 = (bf16[2,128,1024]{1,2,0:T(8,128)(2,1)}, bf16[2,128,1024]{1,2,0:T(8,128)(2,1)}, u32[]{:S(2)}, u32[]{:S(2)}) collective-permute-start(bf16[2,128,1024]{1,2,0:T(8,128)(2,1)} %collective-permute-done.2), channel_id=1, source_target_pairs={{14,0},{0,2},{2,4},{4,6},{6,8},{8,10},{10,12},{12,14},{15,1},{1,3}... | collective-permute-start | bytes 1572872 | tf_op jit(solution)/shard_map/while/body/eval_jaxpr/ppermute | solution.py:18
  328.1 40.1 %copy-start.2 = (f32[2,128,1024]{1,2,0:T(8,128)}, f32[2,128,1024]{1,2,0:T(8,128)S(1)}, u32[]{:S(2)}) copy-start(f32[2,128,1024]{1,2,0:T(8,128)S(1)} %bitcast_add_fusion.7) | copy-start | bytes 3145732 | tf_op jit(solution)/shard_map/while
  368.3 17.9 %collective-permute-start = (bf16[2,128,1024]{1,2,0:T(8,128)(2,1)}, bf16[2,128,1024]{1,2,0:T(8,128)(2,1)}, u32[]{:S(2)}, u32[]{:S(2)}) collective-permute-start(bf16[2,128,1024]{1,2,0:T(8,128)(2,1)} %get-tuple-element.527), channel_id=1, source_target_pairs={{14,0},{0,2},{2,4},{4,6},{6,8},{8,10},{10,12},{12,14},{15,1},{1,3}... | collective-permute-start | bytes 1572872 | tf_op jit(solution)/shard_map/while/body/eval_jaxpr/ppermute | solution.py:18
  368.3 29.1 %collective-permute-start.2 = (bf16[2,128,1024]{1,2,0:T(8,128)(2,1)}, bf16[2,128,1024]{1,2,0:T(8,128)(2,1)}, u32[]{:S(2)}, u32[]{:S(2)}) collective-permute-start(bf16[2,128,1024]{1,2,0:T(8,128)(2,1)} %get-tuple-element.528), channel_id=1, source_target_pairs={{14,0},{0,2},{2,4},{4,6},{6,8},{8,10},{10,12},{12,14},{15,1},{1,3}... | collective-permute-start | bytes 1572872 | tf_op jit(solution)/shard_map/while/body/eval_jaxpr/ppermute | solution.py:18
  378.8 29.9 %collective-permute-start.4 = (bf16[2,128,1024]{1,2,0:T(8,128)(2,1)}, bf16[2,128,1024]{1,2,0:T(8,128)(2,1)}, u32[]{:S(2)}, u32[]{:S(2)}) collective-permute-start(bf16[2,128,1024]{1,2,0:T(8,128)(2,1)} %fusion.199), channel_id=1, source_target_pairs={{14,0},{0,2},{2,4},{4,6},{6,8},{8,10},{10,12},{12,14},{15,1},{1,3}... | collective-permute-start | bytes 1572872 | tf_op jit(solution)/shard_map/while/body/eval_jaxpr/ppermute | solution.py:18
  380.5 39.2 %collective-permute-start.6 = (bf16[2,128,1024]{1,2,0:T(8,128)(2,1)S(1)}, bf16[2,128,1024]{1,2,0:T(8,128)(2,1)S(1)}, u32[]{:S(2)}, u32[]{:S(2)}) collective-permute-start(bf16[2,128,1024]{1,2,0:T(8,128)(2,1)S(1)} %fusion.203), channel_id=1, source_target_pairs={{14,0},{0,2},{2,4},{4,6},{6,8},{8,10},{10,12},{12,14},{15,1},{1,3}... | collective-permute-start | bytes 1572872 | tf_op jit(solution)/shard_map/while/body/eval_jaxpr/ppermute | solution.py:18
  409.8 12.1 copy-start.1
  409.8 21.1 %collective-permute-start.5 = (bf16[2,128,1024]{1,2,0:T(8,128)(2,1)S(1)}, bf16[2,128,1024]{1,2,0:T(8,128)(2,1)S(1)}, u32[]{:S(2)}, u32[]{:S(2)}) collective-permute-start(bf16[2,128,1024]{1,2,0:T(8,128)(2,1)S(1)} %fusion.200), channel_id=1, source_target_pairs={{14,0},{0,2},{2,4},{4,6},{6,8},{8,10},{10,12},{12,14},{15,1},{1,3}... | collective-permute-start | bytes 1572872 | tf_op jit(solution)/shard_map/while/body/eval_jaxpr/ppermute | solution.py:18
  419.9 22.3 %collective-permute-start.7 = (bf16[2,128,1024]{1,2,0:T(8,128)(2,1)S(1)}, bf16[2,128,1024]{1,2,0:T(8,128)(2,1)S(1)}, u32[]{:S(2)}, u32[]{:S(2)}) collective-permute-start(bf16[2,128,1024]{1,2,0:T(8,128)(2,1)S(1)} %fusion.204), channel_id=1, source_target_pairs={{14,0},{0,2},{2,4},{4,6},{6,8},{8,10},{10,12},{12,14},{15,1},{1,3}... | collective-permute-start | bytes 1572872 | tf_op jit(solution)/shard_map/while/body/eval_jaxpr/ppermute | solution.py:18
  419.9 33.6 %collective-permute-start.1 = (bf16[2,128,1024]{1,2,0:T(8,128)(2,1)}, bf16[2,128,1024]{1,2,0:T(8,128)(2,1)}, u32[]{:S(2)}, u32[]{:S(2)}) collective-permute-start(bf16[2,128,1024]{1,2,0:T(8,128)(2,1)} %collective-permute-done), channel_id=1, source_target_pairs={{14,0},{0,2},{2,4},{4,6},{6,8},{8,10},{10,12},{12,14},{15,1},{1,3}... | collective-permute-start | bytes 1572872 | tf_op jit(solution)/shard_map/while/body/eval_jaxpr/ppermute | solution.py:18
  420.0 43.3 %collective-permute-start.3 = (bf16[2,128,1024]{1,2,0:T(8,128)(2,1)}, bf16[2,128,1024]{1,2,0:T(8,128)(2,1)}, u32[]{:S(2)}, u32[]{:S(2)}) collective-permute-start(bf16[2,128,1024]{1,2,0:T(8,128)(2,1)} %collective-permute-done.2), channel_id=1, source_target_pairs={{14,0},{0,2},{2,4},{4,6},{6,8},{8,10},{10,12},{12,14},{15,1},{1,3}... | collective-permute-start | bytes 1572872 | tf_op jit(solution)/shard_map/while/body/eval_jaxpr/ppermute | solution.py:18
  422.3 41.1 %copy-start.2 = (f32[2,128,1024]{1,2,0:T(8,128)}, f32[2,128,1024]{1,2,0:T(8,128)S(1)}, u32[]{:S(2)}) copy-start(f32[2,128,1024]{1,2,0:T(8,128)S(1)} %bitcast_add_fusion.7) | copy-start | bytes 3145732 | tf_op jit(solution)/shard_map/while
  463.3 17.9 %collective-permute-start = (bf16[2,128,1024]{1,2,0:T(8,128)(2,1)}, bf16[2,128,1024]{1,2,0:T(8,128)(2,1)}, u32[]{:S(2)}, u32[]{:S(2)}) collective-permute-start(bf16[2,128,1024]{1,2,0:T(8,128)(2,1)} %get-tuple-element.527), channel_id=1, source_target_pairs={{14,0},{0,2},{2,4},{4,6},{6,8},{8,10},{10,12},{12,14},{15,1},{1,3}... | collective-permute-start | bytes 1572872 | tf_op jit(solution)/shard_map/while/body/eval_jaxpr/ppermute | solution.py:18
  463.3 29.1 %collective-permute-start.2 = (bf16[2,128,1024]{1,2,0:T(8,128)(2,1)}, bf16[2,128,1024]{1,2,0:T(8,128)(2,1)}, u32[]{:S(2)}, u32[]{:S(2)}) collective-permute-start(bf16[2,128,1024]{1,2,0:T(8,128)(2,1)} %get-tuple-element.528), channel_id=1, source_target_pairs={{14,0},{0,2},{2,4},{4,6},{6,8},{8,10},{10,12},{12,14},{15,1},{1,3}... | collective-permute-start | bytes 1572872 | tf_op jit(solution)/shard_map/while/body/eval_jaxpr/ppermute | solution.py:18
  472.5 31.2 %collective-permute-start.4 = (bf16[2,128,1024]{1,2,0:T(8,128)(2,1)}, bf16[2,128,1024]{1,2,0:T(8,128)(2,1)}, u32[]{:S(2)}, u32[]{:S(2)}) collective-permute-start(bf16[2,128,1024]{1,2,0:T(8,128)(2,1)} %fusion.199), channel_id=1, source_target_pairs={{14,0},{0,2},{2,4},{4,6},{6,8},{8,10},{10,12},{12,14},{15,1},{1,3}... | collective-permute-start | bytes 1572872 | tf_op jit(solution)/shard_map/while/body/eval_jaxpr/ppermute | solution.py:18
  473.7 41.1 %collective-permute-start.6 = (bf16[2,128,1024]{1,2,0:T(8,128)(2,1)S(1)}, bf16[2,128,1024]{1,2,0:T(8,128)(2,1)S(1)}, u32[]{:S(2)}, u32[]{:S(2)}) collective-permute-start(bf16[2,128,1024]{1,2,0:T(8,128)(2,1)S(1)} %fusion.203), channel_id=1, source_target_pairs={{14,0},{0,2},{2,4},{4,6},{6,8},{8,10},{10,12},{12,14},{15,1},{1,3}... | collective-permute-start | bytes 1572872 | tf_op jit(solution)/shard_map/while/body/eval_jaxpr/ppermute | solution.py:18
  504.9 12.1 copy-start.1
  504.9 21.1 %collective-permute-start.5 = (bf16[2,128,1024]{1,2,0:T(8,128)(2,1)S(1)}, bf16[2,128,1024]{1,2,0:T(8,128)(2,1)S(1)}, u32[]{:S(2)}, u32[]{:S(2)}) collective-permute-start(bf16[2,128,1024]{1,2,0:T(8,128)(2,1)S(1)} %fusion.200), channel_id=1, source_target_pairs={{14,0},{0,2},{2,4},{4,6},{6,8},{8,10},{10,12},{12,14},{15,1},{1,3}... | collective-permute-start | bytes 1572872 | tf_op jit(solution)/shard_map/while/body/eval_jaxpr/ppermute | solution.py:18
  515.0 22.3 %collective-permute-start.7 = (bf16[2,128,1024]{1,2,0:T(8,128)(2,1)S(1)}, bf16[2,128,1024]{1,2,0:T(8,128)(2,1)S(1)}, u32[]{:S(2)}, u32[]{:S(2)}) collective-permute-start(bf16[2,128,1024]{1,2,0:T(8,128)(2,1)S(1)} %fusion.204), channel_id=1, source_target_pairs={{14,0},{0,2},{2,4},{4,6},{6,8},{8,10},{10,12},{12,14},{15,1},{1,3}... | collective-permute-start | bytes 1572872 | tf_op jit(solution)/shard_map/while/body/eval_jaxpr/ppermute | solution.py:18
  515.0 33.6 %collective-permute-start.1 = (bf16[2,128,1024]{1,2,0:T(8,128)(2,1)}, bf16[2,128,1024]{1,2,0:T(8,128)(2,1)}, u32[]{:S(2)}, u32[]{:S(2)}) collective-permute-start(bf16[2,128,1024]{1,2,0:T(8,128)(2,1)} %collective-permute-done), channel_id=1, source_target_pairs={{14,0},{0,2},{2,4},{4,6},{6,8},{8,10},{10,12},{12,14},{15,1},{1,3}... | collective-permute-start | bytes 1572872 | tf_op jit(solution)/shard_map/while/body/eval_jaxpr/ppermute | solution.py:18
  515.1 42.4 %collective-permute-start.3 = (bf16[2,128,1024]{1,2,0:T(8,128)(2,1)}, bf16[2,128,1024]{1,2,0:T(8,128)(2,1)}, u32[]{:S(2)}, u32[]{:S(2)}) collective-permute-start(bf16[2,128,1024]{1,2,0:T(8,128)(2,1)} %collective-permute-done.2), channel_id=1, source_target_pairs={{14,0},{0,2},{2,4},{4,6},{6,8},{8,10},{10,12},{12,14},{15,1},{1,3}... | collective-permute-start | bytes 1572872 | tf_op jit(solution)/shard_map/while/body/eval_jaxpr/ppermute | solution.py:18
  517.3 40.2 %copy-start.2 = (f32[2,128,1024]{1,2,0:T(8,128)}, f32[2,128,1024]{1,2,0:T(8,128)S(1)}, u32[]{:S(2)}) copy-start(f32[2,128,1024]{1,2,0:T(8,128)S(1)} %bitcast_add_fusion.7) | copy-start | bytes 3145732 | tf_op jit(solution)/shard_map/while
  557.5 17.9 %collective-permute-start = (bf16[2,128,1024]{1,2,0:T(8,128)(2,1)}, bf16[2,128,1024]{1,2,0:T(8,128)(2,1)}, u32[]{:S(2)}, u32[]{:S(2)}) collective-permute-start(bf16[2,128,1024]{1,2,0:T(8,128)(2,1)} %get-tuple-element.527), channel_id=1, source_target_pairs={{14,0},{0,2},{2,4},{4,6},{6,8},{8,10},{10,12},{12,14},{15,1},{1,3}... | collective-permute-start | bytes 1572872 | tf_op jit(solution)/shard_map/while/body/eval_jaxpr/ppermute | solution.py:18
  557.5 29.1 %collective-permute-start.2 = (bf16[2,128,1024]{1,2,0:T(8,128)(2,1)}, bf16[2,128,1024]{1,2,0:T(8,128)(2,1)}, u32[]{:S(2)}, u32[]{:S(2)}) collective-permute-start(bf16[2,128,1024]{1,2,0:T(8,128)(2,1)} %get-tuple-element.528), channel_id=1, source_target_pairs={{14,0},{0,2},{2,4},{4,6},{6,8},{8,10},{10,12},{12,14},{15,1},{1,3}... | collective-permute-start | bytes 1572872 | tf_op jit(solution)/shard_map/while/body/eval_jaxpr/ppermute | solution.py:18
  566.6 31.2 %collective-permute-start.4 = (bf16[2,128,1024]{1,2,0:T(8,128)(2,1)}, bf16[2,128,1024]{1,2,0:T(8,128)(2,1)}, u32[]{:S(2)}, u32[]{:S(2)}) collective-permute-start(bf16[2,128,1024]{1,2,0:T(8,128)(2,1)} %fusion.199), channel_id=1, source_target_pairs={{14,0},{0,2},{2,4},{4,6},{6,8},{8,10},{10,12},{12,14},{15,1},{1,3}... | collective-permute-start | bytes 1572872 | tf_op jit(solution)/shard_map/while/body/eval_jaxpr/ppermute | solution.py:18
  567.9 41.1 %collective-permute-start.6 = (bf16[2,128,1024]{1,2,0:T(8,128)(2,1)S(1)}, bf16[2,128,1024]{1,2,0:T(8,128)(2,1)S(1)}, u32[]{:S(2)}, u32[]{:S(2)}) collective-permute-start(bf16[2,128,1024]{1,2,0:T(8,128)(2,1)S(1)} %fusion.203), channel_id=1, source_target_pairs={{14,0},{0,2},{2,4},{4,6},{6,8},{8,10},{10,12},{12,14},{15,1},{1,3}... | collective-permute-start | bytes 1572872 | tf_op jit(solution)/shard_map/while/body/eval_jaxpr/ppermute | solution.py:18
  599.1 12.1 copy-start.1
  599.1 21.1 %collective-permute-start.5 = (bf16[2,128,1024]{1,2,0:T(8,128)(2,1)S(1)}, bf16[2,128,1024]{1,2,0:T(8,128)(2,1)S(1)}, u32[]{:S(2)}, u32[]{:S(2)}) collective-permute-start(bf16[2,128,1024]{1,2,0:T(8,128)(2,1)S(1)} %fusion.200), channel_id=1, source_target_pairs={{14,0},{0,2},{2,4},{4,6},{6,8},{8,10},{10,12},{12,14},{15,1},{1,3}... | collective-permute-start | bytes 1572872 | tf_op jit(solution)/shard_map/while/body/eval_jaxpr/ppermute | solution.py:18
  609.1 22.3 %collective-permute-start.7 = (bf16[2,128,1024]{1,2,0:T(8,128)(2,1)S(1)}, bf16[2,128,1024]{1,2,0:T(8,128)(2,1)S(1)}, u32[]{:S(2)}, u32[]{:S(2)}) collective-permute-start(bf16[2,128,1024]{1,2,0:T(8,128)(2,1)S(1)} %fusion.204), channel_id=1, source_target_pairs={{14,0},{0,2},{2,4},{4,6},{6,8},{8,10},{10,12},{12,14},{15,1},{1,3}... | collective-permute-start | bytes 1572872 | tf_op jit(solution)/shard_map/while/body/eval_jaxpr/ppermute | solution.py:18
  609.2 33.6 %collective-permute-start.1 = (bf16[2,128,1024]{1,2,0:T(8,128)(2,1)}, bf16[2,128,1024]{1,2,0:T(8,128)(2,1)}, u32[]{:S(2)}, u32[]{:S(2)}) collective-permute-start(bf16[2,128,1024]{1,2,0:T(8,128)(2,1)} %collective-permute-done), channel_id=1, source_target_pairs={{14,0},{0,2},{2,4},{4,6},{6,8},{8,10},{10,12},{12,14},{15,1},{1,3}... | collective-permute-start | bytes 1572872 | tf_op jit(solution)/shard_map/while/body/eval_jaxpr/ppermute | solution.py:18
  609.3 41.5 %collective-permute-start.3 = (bf16[2,128,1024]{1,2,0:T(8,128)(2,1)}, bf16[2,128,1024]{1,2,0:T(8,128)(2,1)}, u32[]{:S(2)}, u32[]{:S(2)}) collective-permute-start(bf16[2,128,1024]{1,2,0:T(8,128)(2,1)} %collective-permute-done.2), channel_id=1, source_target_pairs={{14,0},{0,2},{2,4},{4,6},{6,8},{8,10},{10,12},{12,14},{15,1},{1,3}... | collective-permute-start | bytes 1572872 | tf_op jit(solution)/shard_map/while/body/eval_jaxpr/ppermute | solution.py:18
  611.5 39.2 %copy-start.2 = (f32[2,128,1024]{1,2,0:T(8,128)}, f32[2,128,1024]{1,2,0:T(8,128)S(1)}, u32[]{:S(2)}) copy-start(f32[2,128,1024]{1,2,0:T(8,128)S(1)} %bitcast_add_fusion.7) | copy-start | bytes 3145732 | tf_op jit(solution)/shard_map/while
  650.7 5.6 copy-start.29
  660.9 32.7 %reduce-scatter.9.cloned.1.call-start = ((), (), s32[]{:S(2)}) async-start(), calls=%async_computation.12 | async-start | bytes 12582912 | tf_op jit(solution)/shard_map/reduce_scatter | solution.py:270
  669.8 44.7 %reduce-scatter.11.cloned.1.call-start = ((), (), s32[]{:S(2)}) async-start(), calls=%async_computation.13 | async-start | bytes 12582912 | tf_op jit(solution)/shard_map/reduce_scatter | solution.py:276
  677.4 6.6 copy-start.13
  (28 other events, 63.6 us)
Sparse Core Ops, SparseCore 0:
  9.6 19.4 all-gather.14
  35.1 74.5 all-gather.18
  112.4 71.6 all-gather.16
  185.5 8.8 all-gather.20
  195.8 21.0 all-gather.22
  218.2 21.0 all-gather.24
  272.4 10.8 reduce-scatter.6
  661.0 11.6 reduce-scatter.4
  675.6 17.9 reduce-scatter.8
  696.4 18.0 reduce-scatter.10
where the time goes:
time: 1770 us; the launch traced here: 1760 us
  blocking collectives  1060 us (60%)
  waiting for transfers between devices  435 us (25%)
  matrix products  138 us (8%)
  local copies, waits for them, and re-layouts  54.6 us (3%)
  other arithmetic  45.7 us (3%)
    psum x1, blocking collectives, on_device(): lax.psum((attn_grads[0], attn_grads[1], attn_grads[2], attn_grads[3], att...  1040 us
    ppermute x32, waiting for transfers between devices, from_behind(): return lax.ppermute(block, axis, route)  267 us
    all_gather x1, waiting for transfers between devices, attend_forward(): key_part = lax.all_gather(key_rows, 'ctx', axis=1, tiled=True)  68 us
    all_gather x1, waiting for transfers between devices, attend_forward(): value_part = lax.all_gather(value_rows, 'ctx', axis=1, tiled=True)  56.5 us
  transfers between devices with their start and end apart: 42, of which 37 were waited for; matrix products, arithmetic and copies ran while one was open for 10% of the time, Pallas kernels for 0%

commit v1 on v0

--- a/solution.py
+++ b/solution.py
@@ -3,6 +3,8 @@
 import jax
 import jax.numpy as jnp
 from jax import lax
+from jax.experimental import pallas as pl
+from jax.experimental.pallas import tpu as pltpu
 from jax.sharding import PartitionSpec as P
 
 HEADS = 16
@@ -185,7 +187,7 @@
     return (finished[4], finished[2], finished[3])
 
 
-def on_device(
+def ring_on_device(
     tokens,
     query_key_value_weight,
     bias_query,
@@ -366,6 +368,581 @@
     )
 
 
+def exchange(values, axis, bit):
+    count = lax.axis_size(axis)
+    return lax.ppermute(values, axis, [(i, i ^ bit) for i in range(count)])
+
+
+def bits_below(count):
+    return [1 << k for k in range(count.bit_length() - 1)]
+
+
+def reorder(pieces, index):
+    for bit in bits_below(len(pieces)):
+        taken = (index & bit) != 0
+        pieces = [jnp.where(taken, pieces[k ^ bit], pieces[k]) for k in range(len(pieces))]
+    return pieces
+
+
+def pair_join(own, other, core, axis=0):
+    first = jnp.where(core == 0, own, other)
+    second = jnp.where(core == 0, other, own)
+    return jnp.concatenate([first, second], axis=axis)
+
+
+def half_of(values, which, axis):
+    size = values.shape[axis] // 2
+    low = lax.slice_in_dim(values, 0, size, axis=axis)
+    high = lax.slice_in_dim(values, size, 2 * size, axis=axis)
+    return jnp.where(which == 0, low, high)
+
+
+def gather_blocks(block):
+    count = lax.axis_size("ctx")
+    pieces = {0: block}
+    for bit in reversed(bits_below(count)):
+        for k in list(pieces):
+            pieces[k ^ bit] = exchange(pieces[k], "ctx", bit)
+    return [pieces[k] for k in range(count)]
+
+
+def swap_blocks(pieces):
+    return [pieces[0]] + [exchange(pieces[k], "ctx", k) for k in range(1, len(pieces))]
+
+
+def head_mask(value):
+    lane = lax.broadcasted_iota(jnp.int32, (1, 2 * HEAD_DIM), 1)
+    return [
+        jnp.where(lane < HEAD_DIM, value, 0.0),
+        jnp.where(lane < HEAD_DIM, 0.0, value),
+    ]
+
+
+def contract(left, right, left_dim, right_dim):
+    return lax.dot_general(
+        left, right, (((left_dim,), (right_dim,)), ((), ())), preferred_element_type=jnp.float32
+    )
+
+
+def forward_kernel(query_ref, key_ref, value_ref, result_ref, low_ref, log_ref):
+    query = query_ref[0].astype(jnp.float32)
+    keys = key_ref[0]
+    values = value_ref[0]
+    results = []
+    logs = []
+    for mask in head_mask(HEAD_DIM ** (-0.5)):
+        scores = contract((query * mask).astype(jnp.bfloat16), keys, 1, 1)
+        row_max = jnp.max(scores, axis=-1, keepdims=True)
+        weights = jnp.exp(scores - row_max)
+        total = jnp.sum(weights, axis=-1, keepdims=True)
+        probabilities = (weights * (1.0 / total)).astype(jnp.bfloat16)
+        results.append(contract(probabilities, values, 1, 0))
+        logs.append(row_max + jnp.log(total))
+    first = lax.broadcasted_iota(jnp.int32, results[0].shape, 1) < HEAD_DIM
+    result = jnp.where(first, results[0], results[1])
+    result_ref[0] = result
+    low_ref[0] = result.astype(jnp.bfloat16)
+    log_ref[0] = jnp.where(first, logs[0], logs[1])
+
+
+def attention_forward(projected):
+    seqs, length, width = projected.shape
+    pair = width // 3
+    rows = min(256, length)
+    row_spec = pl.BlockSpec((1, rows, pair), lambda s, q: (s, q, 0))
+    return pl.pallas_call(
+        forward_kernel,
+        grid=(seqs, length // rows),
+        in_specs=[
+            row_spec,
+            pl.BlockSpec((1, length, pair), lambda s, q: (s, 0, 1)),
+            pl.BlockSpec((1, length, pair), lambda s, q: (s, 0, 2)),
+        ],
+        out_specs=[row_spec, row_spec, row_spec],
+        out_shape=[
+            jax.ShapeDtypeStruct((seqs, length, pair), jnp.float32),
+            jax.ShapeDtypeStruct((seqs, length, pair), jnp.bfloat16),
+            jax.ShapeDtypeStruct((seqs, length, pair), jnp.float32),
+        ],
+        compiler_params=pltpu.CompilerParams(vmem_limit_bytes=48 << 20),
+        name="attention_forward",
+    )(projected, projected, projected)
+
+
+def backward_kernel(
+    query_ref, key_ref, value_ref, grad_ref, result_ref, log_ref,
+    query_out, key_out, value_out, query_acc, log_rows, inner_rows,
+):
+    step = pl.program_id(1)
+
+    @pl.when(step == 0)
+    def first_step():
+        query_acc[...] = jnp.zeros_like(query_acc)
+        logs = jnp.transpose(log_ref[0])
+        inner = jnp.transpose(grad_ref[0].astype(jnp.float32) * result_ref[0])
+        for h in range(2):
+            log_rows[h] = jnp.broadcast_to(
+                logs[h * HEAD_DIM : h * HEAD_DIM + 1], log_rows.shape[1:]
+            )
+            inner_rows[h] = jnp.broadcast_to(
+                jnp.sum(inner[h * HEAD_DIM : (h + 1) * HEAD_DIM], axis=0, keepdims=True),
+                inner_rows.shape[1:],
+            )
+
+    queries = query_ref[0]
+    grads = grad_ref[0]
+    keys = key_ref[0]
+    values = value_ref[0]
+    scale = HEAD_DIM ** (-0.5)
+    query_parts = []
+    key_parts = []
+    value_parts = []
+    scaled_masks = head_mask(scale)
+    masks = head_mask(1.0)
+    for h in range(2):
+        scores = contract(
+            (keys.astype(jnp.float32) * scaled_masks[h]).astype(jnp.bfloat16), queries, 1, 1
+        )
+        probabilities = jnp.exp(scores - log_rows[h, :1])
+        prob_grad = contract(
+            (values.astype(jnp.float32) * masks[h]).astype(jnp.bfloat16), grads, 1, 1
+        )
+        score_grad = (probabilities * (prob_grad - inner_rows[h, :1])).astype(jnp.bfloat16)
+        value_parts.append(contract(probabilities.astype(jnp.bfloat16), grads, 1, 0))
+        key_parts.append(contract(score_grad, queries, 1, 0))
+        query_parts.append(contract(score_grad, keys, 0, 0))
+    first = lax.broadcasted_iota(jnp.int32, key_parts[0].shape, 1) < HEAD_DIM
+    value_out[0] = jnp.where(first, value_parts[0], value_parts[1]).astype(jnp.bfloat16)
+    key_out[0] = (jnp.where(first, key_parts[0], key_parts[1]) * scale).astype(jnp.bfloat16)
+    first = lax.broadcasted_iota(jnp.int32, query_parts[0].shape, 1) < HEAD_DIM
+    query_acc[...] += jnp.where(first, query_parts[0], query_parts[1])
+
+    @pl.when(step == pl.num_programs(1) - 1)
+    def last_step():
+        query_out[0] = (query_acc[...] * scale).astype(jnp.bfloat16)
+
+
+def attention_backward(projected, grads, result, logs):
+    seqs, length, width = projected.shape
+    pair = width // 3
+    rows = min(256, length)
+    whole = pl.BlockSpec((1, length, pair), lambda s, k: (s, 0, 0))
+    block = pl.BlockSpec((1, rows, pair), lambda s, k: (s, k, 0))
+    shape = jax.ShapeDtypeStruct((seqs, length, pair), jnp.bfloat16)
+    return pl.pallas_call(
+        backward_kernel,
+        grid=(seqs, length // rows),
+        in_specs=[
+            whole,
+            pl.BlockSpec((1, rows, pair), lambda s, k: (s, k, 1)),
+            pl.BlockSpec((1, rows, pair), lambda s, k: (s, k, 2)),
+            whole,
+            whole,
+            whole,
+        ],
+        out_specs=[whole, block, block],
+        out_shape=[shape, shape, shape],
+        scratch_shapes=[
+            pltpu.VMEM((length, pair), jnp.float32),
+            pltpu.VMEM((2, 8, length), jnp.float32),
+            pltpu.VMEM((2, 8, length), jnp.float32),
+        ],
+        compiler_params=pltpu.CompilerParams(vmem_limit_bytes=48 << 20),
+        name="attention_backward",
+    )(projected, projected, projected, grads, result, logs)
+
+
+def grad_kernel(place_ref, left_own, left_other, right_own, right_other, keep_ref, send_ref):
+    step = pl.program_id(0)
+    half = pl.num_programs(0) // 2
+    total = contract(left_own[...], right_own[...], 0, 0)
+    total = total + contract(left_other[...], right_other[...], 0, 0)
+    total = total.astype(jnp.bfloat16)
+
+    @pl.when(step < half)
+    def outgoing():
+        send_ref[0] = total
+
+    @pl.when(step >= half)
+    def kept():
+        keep_ref[0] = total
+
+
+def pair_grad(place, left_pair, right_pair, row_bits, col_bits, name):
+    tokens, width = left_pair[0].shape
+    columns = right_pair[0].shape[1]
+    rows = width >> row_bits
+    cols = columns >> col_bits
+    count = 1 << (row_bits + col_bits)
+    half = count // 2
+
+    def chunk(step):
+        return (step + half) % count
+
+    left = pl.BlockSpec((tokens, rows), lambda s, p: (0, (chunk(s) ^ p[0]) >> col_bits))
+    right = pl.BlockSpec(
+        (tokens, cols), lambda s, p: (0, (chunk(s) ^ p[0]) & ((1 << col_bits) - 1))
+    )
+    shape = jax.ShapeDtypeStruct((half, rows, cols), jnp.bfloat16)
+    return pl.pallas_call(
+        grad_kernel,
+        grid_spec=pltpu.PrefetchScalarGridSpec(
+            num_scalar_prefetch=1,
+            grid=(count,),
+            in_specs=[left, left, right, right],
+            out_specs=[
+                pl.BlockSpec((1, rows, cols), lambda s, p: (jnp.maximum(s - half, 0), 0, 0)),
+                pl.BlockSpec((1, rows, cols), lambda s, p: (jnp.minimum(s, half - 1), 0, 0)),
+            ],
+        ),
+        out_shape=[shape, shape],
+        compiler_params=pltpu.CompilerParams(vmem_limit_bytes=48 << 20),
+        name=name,
+    )(place, left_pair[0], left_pair[1], right_pair[0], right_pair[1])
+
+
+def place_of(order):
+    place = jnp.int32(0)
+    for axis, bit in order:
+        place = place * 2 + jnp.where((lax.axis_index(axis) & bit) != 0, 1, 0)
+    return place.astype(jnp.int32).reshape(1)
+
+
+def added(first, second):
+    return lowered(widened(first) + widened(second))
+
+
+def sum_to_owner(keep, send, order):
+    for step, (axis, bit) in enumerate(order):
+        arrived = exchange(send, axis, bit)
+        half = keep.shape[0] // 2
+        if step == len(order) - 1:
+            return added(keep, arrived)
+        send = added(keep[half:], arrived[half:])
+        keep = added(keep[:half], arrived[:half])
+
+
+def spread(owned, order):
+    for axis, bit in reversed(order[1:]):
+        owned = jnp.concatenate([owned, exchange(owned, axis, bit)], axis=0)
+    return owned, exchange(owned, order[0][0], order[0][1])
+
+
+def place_kernel(place_ref, near_ref, far_ref, out_ref):
+    half = pl.num_programs(0) // 2
+
+    @pl.when(pl.program_id(0) < half)
+    def from_near():
+        out_ref[...] = near_ref[0].astype(jnp.float32)
+
+    @pl.when(pl.program_id(0) >= half)
+    def from_far():
+        out_ref[...] = far_ref[0].astype(jnp.float32)
+
+
+def put_in_place(place, near, far, row_bits, col_bits, name):
+    half, rows, cols = near.shape
+    count = 2 * half
+    return pl.pallas_call(
+        place_kernel,
+        grid_spec=pltpu.PrefetchScalarGridSpec(
+            num_scalar_prefetch=1,
+            grid=(count,),
+            in_specs=[
+                pl.BlockSpec((1, rows, cols), lambda s, p: (jnp.minimum(s, half - 1), 0, 0)),
+                pl.BlockSpec((1, rows, cols), lambda s, p: (jnp.maximum(s - half, 0), 0, 0)),
+            ],
+            out_specs=pl.BlockSpec(
+                (rows, cols),
+                lambda s, p: ((s ^ p[0]) >> col_bits, (s ^ p[0]) & ((1 << col_bits) - 1)),
+            ),
+        ),
+        out_shape=jax.ShapeDtypeStruct((rows << row_bits, cols << col_bits), jnp.float32),
+        compiler_params=pltpu.CompilerParams(vmem_limit_bytes=48 << 20),
+        name=name,
+    )(place, near, far)
+
+
+def place_three_kernel(place_ref, near_ref, far_ref, out_ref):
+    half = pl.num_programs(0) // 2
+
+    @pl.when(pl.program_id(0) < half)
+    def from_near():
+        out_ref[...] = near_ref[0, 0].astype(jnp.float32)
+
+    @pl.when(pl.program_id(0) >= half)
+    def from_far():
+        out_ref[...] = far_ref[0, 0].astype(jnp.float32)
+
+
+def put_three_in_place(place, near, far, row_bits, col_bits, name):
+    half, three, rows, cols = near.shape
+    count = 2 * half
+    return pl.pallas_call(
+        place_three_kernel,
+        grid_spec=pltpu.PrefetchScalarGridSpec(
+            num_scalar_prefetch=1,
+            grid=(count, three),
+            in_specs=[
+                pl.BlockSpec(
+                    (1, 1, rows, cols),
+                    lambda s, t, p: (
+                        jnp.minimum(s, half - 1), jnp.where(s < half, t, three - 1), 0, 0
+                    ),
+                ),
+                pl.BlockSpec(
+                    (1, 1, rows, cols),
+                    lambda s, t, p: (jnp.maximum(s - half, 0), jnp.where(s < half, 0, t), 0, 0),
+                ),
+            ],
+            out_specs=pl.BlockSpec(
+                (rows, cols),
+                lambda s, t, p: (
+                    (s ^ p[0]) >> col_bits,
+                    (t << col_bits) + ((s ^ p[0]) & ((1 << col_bits) - 1)),
+                ),
+            ),
+        ),
+        out_shape=jax.ShapeDtypeStruct((rows << row_bits, three * (cols << col_bits)), jnp.float32),
+        compiler_params=pltpu.CompilerParams(vmem_limit_bytes=48 << 20),
+        name=name,
+    )(place, near, far)
+
+
+def sum_everywhere(values, axes):
+    for axis in axes:
+        for bit in bits_below(lax.axis_size(axis)):
+            values = values + exchange(values, axis, bit)
+    return values
+
+
+def on_device(
+    tokens,
+    query_key_value_weight,
+    bias_query,
+    bias_value,
+    attention_out_weight,
+    attention_out_bias,
+    gain_one,
+    shift_one,
+    feedforward_in_weight,
+    feedforward_in_bias,
+    feedforward_out_weight,
+    feedforward_out_bias,
+    gain_two,
+    shift_two,
+    d_out,
+):
+    core = lax.axis_index("fsdp")
+    ctx = lax.axis_index("ctx")
+    ctx_count = lax.axis_size("ctx")
+    seqs, block_rows, width = tokens.shape
+    pair = width // ctx_count
+    flat = seqs * block_rows
+
+    token_pieces = gather_blocks(tokens)
+
+    small = (
+        bias_query, bias_value, attention_out_bias, gain_one, shift_one,
+        feedforward_in_bias, feedforward_out_bias, gain_two, shift_two,
+    )
+    packed = jnp.concatenate(small)
+    packed_other = exchange(packed, "fsdp", 1)
+    vectors = []
+    offset = 0
+    for part in small:
+        size = part.shape[0]
+        vectors.append(widened(pair_join(part, packed_other[offset : offset + size], core)))
+        offset += size
+    (
+        query_bias, value_bias, out_bias, gain_first, shift_first,
+        inner_bias, back_bias, gain_second, shift_second,
+    ) = vectors
+    qkv_full = pair_join(
+        query_key_value_weight, exchange(query_key_value_weight, "fsdp", 1), core
+    )
+    out_full = pair_join(attention_out_weight, exchange(attention_out_weight, "fsdp", 1), core)
+    in_full = pair_join(feedforward_in_weight, exchange(feedforward_in_weight, "fsdp", 1), core)
+    back_full = pair_join(feedforward_out_weight, exchange(feedforward_out_weight, "fsdp", 1), core)
+
+    head_weight = jnp.concatenate(
+        [lax.dynamic_slice_in_dim(qkv_full, t * width + ctx * pair, pair, axis=1) for t in range(3)],
+        axis=1,
+    )
+    head_bias = jnp.concatenate(
+        [
+            lax.dynamic_slice_in_dim(query_bias, ctx * pair, pair),
+            jnp.zeros((pair,), jnp.float32),
+            lax.dynamic_slice_in_dim(value_bias, ctx * pair, pair),
+        ]
+    )
+    token_rows = jnp.concatenate(token_pieces, axis=1)
+    projected = lowered(project(token_rows, head_weight) + head_bias)
+    head_result, head_low, head_logs = attention_forward(projected)
+
+    def row_blocks(values):
+        return [
+            lax.slice_in_dim(values, k * block_rows, (k + 1) * block_rows, axis=1)
+            for k in range(ctx_count)
+        ]
+
+    attended_pieces = reorder(swap_blocks(row_blocks(head_low)), ctx)
+    attended_low = jnp.concatenate(attended_pieces, axis=-1)
+    attention_branch = project(attended_low, out_full) + out_bias
+    summed_one = widened(tokens) + attention_branch
+    first_normalized, pull_one = jax.vjp(norm_apply, summed_one, gain_first, shift_first)
+    normed_low = lowered(first_normalized)
+    hidden_before_gelu = project(normed_low, in_full) + inner_bias
+    active_low = lowered(jax.nn.gelu(hidden_before_gelu, approximate=False))
+    feedforward_branch = project(active_low, back_full) + back_bias
+
+    def second_norm(residual_in, branch_in, gain_vec, shift_vec):
+        return norm_apply(residual_in + branch_in, gain_vec, shift_vec)
+
+    result, pull_two = jax.vjp(
+        second_norm, first_normalized, feedforward_branch, gain_second, shift_second
+    )
+    output = lowered(result)
+    first_grad_res, second_grad, gain_two_grad, shift_two_grad = pull_two(widened(d_out))
+    second_low = lowered(second_grad)
+
+    def left_pair(values):
+        rows = values.reshape(flat, values.shape[2])
+        return (half_of(rows, core, 1), exchange(half_of(rows, 1 - core, 1), "fsdp", 1))
+
+    def right_pair(values):
+        rows = values.reshape(flat, values.shape[2])
+        return (rows, exchange(rows, "fsdp", 1))
+
+    ctx_bits = [("ctx", bit) for bit in bits_below(ctx_count)]
+    dp_bits = [("dp", bit) for bit in bits_below(lax.axis_size("dp"))]
+    order_x = dp_bits + ctx_bits
+    order_y = ctx_bits[:1] + dp_bits + ctx_bits[1:]
+    place_x = place_of(order_x)
+    place_y = place_of(order_y)
+    total_bits = len(order_x)
+
+    back_bits = (total_bits - 1, 1)
+    back_parts = pair_grad(
+        place_x, left_pair(active_low), right_pair(second_low), *back_bits, "grad_back"
+    )
+    back_bias_grad = column_sum(second_low)
+    active_grad = back_project(second_low, back_full)
+    gelu_pull = jax.vjp(partial(jax.nn.gelu, approximate=False), hidden_before_gelu)[1]
+    hidden_low = lowered(gelu_pull(active_grad)[0])
+    in_bits = (0, total_bits)
+    in_parts = pair_grad(
+        place_y, left_pair(normed_low), right_pair(hidden_low), *in_bits, "grad_in"
+    )
+    in_bias_grad = column_sum(hidden_low)
+    first_grad = first_grad_res + back_project(hidden_low, in_full)
+    summed_grad, gain_one_grad, shift_one_grad = pull_one(first_grad)
+    branch_low = lowered(summed_grad)
+    out_bits = (1, total_bits - 1)
+    out_parts = pair_grad(
+        place_x, left_pair(attended_low), right_pair(branch_low), *out_bits, "grad_out"
+    )
+    out_bias_grad = column_sum(branch_low)
+    attended_grad = lowered(back_project(branch_low, out_full))
+
+    column_pieces = [attended_grad[..., k * pair : (k + 1) * pair] for k in range(ctx_count)]
+    head_grad = jnp.concatenate(swap_blocks(reorder(column_pieces, ctx)), axis=1)
+    query_grad, key_grad, value_grad = attention_backward(
+        projected, head_grad, head_result, head_logs
+    )
+    head_grads = (query_grad, key_grad, value_grad)
+
+    token_flat = token_rows.reshape(-1, width)
+    qkv_part = jnp.stack(
+        [contract(token_flat, g.reshape(-1, pair), 0, 0) for g in head_grads], axis=0
+    )
+    own_rows = half_of(qkv_part, core, 1)
+    qkv_sum = own_rows + widened(exchange(lowered(half_of(qkv_part, 1 - core, 1)), "fsdp", 1))
+    order_q = dp_bits + ctx_bits
+    dp_index = lax.axis_index("dp")
+    dp_count = lax.axis_size("dp")
+    qkv_chunks = [
+        qkv_sum[:, k * (qkv_sum.shape[1] // dp_count) : (k + 1) * (qkv_sum.shape[1] // dp_count)]
+        for k in range(dp_count)
+    ]
+    qkv_chunks = reorder(qkv_chunks, dp_index)
+    while len(qkv_chunks) > 1:
+        half = len(qkv_chunks) // 2
+        arrived = [exchange(lowered(c), "dp", half) for c in qkv_chunks[half:]]
+        qkv_chunks = [c + widened(a) for c, a in zip(qkv_chunks[:half], arrived)]
+    qkv_owned = lowered(qkv_chunks[0])[None]
+    place_q = place_of(
+        [("dp", bit) for bit in reversed(bits_below(dp_count))]
+        + [("ctx", bit) for bit in reversed(bits_below(ctx_count))]
+    )
+    order_q = [("dp", bit) for bit in reversed(bits_below(dp_count))] + [
+        ("ctx", bit) for bit in reversed(bits_below(ctx_count))
+    ]
+    qkv_near, qkv_far = spread(qkv_owned, order_q)
+    qkv_grad = put_three_in_place(
+        place_q, qkv_near, qkv_far, len(dp_bits), len(ctx_bits), "place_qkv"
+    )
+
+    back_grad = put_in_place(
+        place_x, *spread(sum_to_owner(*back_parts, order_x), order_x), *back_bits, "place_back"
+    )
+    in_grad = put_in_place(
+        place_y, *spread(sum_to_owner(*in_parts, order_y), order_y), *in_bits, "place_in"
+    )
+    out_grad = put_in_place(
+        place_x, *spread(sum_to_owner(*out_parts, order_x), order_x), *out_bits, "place_out"
+    )
+
+    mixed_pieces = []
+    for part in head_grads:
+        mixed_pieces.append(row_blocks(part))
+    mixed = [jnp.concatenate([m[k] for m in mixed_pieces], axis=-1) for k in range(ctx_count)]
+    mixed = reorder(swap_blocks(mixed), ctx)
+    mixed_grad = jnp.concatenate(
+        [m[..., t * pair : (t + 1) * pair] for t in range(3) for m in mixed], axis=-1
+    )
+    token_grad = summed_grad + back_project(mixed_grad, qkv_full)
+
+    layer_vectors = (
+        in_bias_grad, back_bias_grad, gain_two_grad, shift_two_grad,
+        out_bias_grad, gain_one_grad, shift_one_grad,
+    )
+    layer_sum = sum_everywhere(jnp.concatenate(layer_vectors), ("fsdp", "dp", "ctx"))
+    reduced = []
+    offset = 0
+    for part in layer_vectors:
+        size = part.shape[0]
+        reduced.append(half_of(layer_sum[offset : offset + size], core, 0))
+        offset += size
+    bias_part = jnp.stack([column_sum(query_grad), column_sum(value_grad)])
+    bias_part = sum_everywhere(bias_part, ("fsdp", "dp"))
+    bias_pieces = reorder(gather_blocks(bias_part), ctx)
+    bias_grads = half_of(jnp.concatenate(bias_pieces, axis=1), core, 1)
+    return (
+        output,
+        token_grad,
+        qkv_grad,
+        bias_grads[0],
+        bias_grads[1],
+        out_grad,
+        reduced[4],
+        reduced[5],
+        reduced[6],
+        in_grad,
+        reduced[0],
+        back_grad,
+        reduced[1],
+        reduced[2],
+        reduced[3],
+    )
+
+
+def head_parallel(mesh):
+    sizes = [mesh.shape["dp"], mesh.shape["ctx"]]
+    powers = all(size & (size - 1) == 0 for size in sizes)
+    return powers and mesh.shape["fsdp"] == 2 and 2 * mesh.shape["ctx"] == HEADS
+
+
 def solution(mesh):
     in_specs = (
         P(("dp", "fsdp"), "ctx", None),
@@ -401,6 +978,7 @@
         P("fsdp"),
         P("fsdp"),
     )
+    body = on_device if head_parallel(mesh) else ring_on_device
     return jax.shard_map(
-        on_device, mesh=mesh, in_specs=in_specs, out_specs=out_specs, check_vma=False
-    )
+        body, mesh=mesh, in_specs=in_specs, out_specs=out_specs, check_vma=False
+    )

time: 1770 us -> 612 us (0.35)
  blocking collectives: 1060 us -> 0 us
  waiting for transfers between devices: 435 us -> 294 us
  matrix products: 138 us -> 43.1 us
  Pallas kernels: 0 us -> 87.4 us
  starting transfers between devices: 17 us -> 92.8 us
    psum x1 -> x0, blocking collectives: 1040 us -> none  [on_device(): lax.psum((attn_grads[0], attn_grads[1], attn_grads[2], attn_grads[3], att...]
    all_gather x6 -> x0, waiting for transfers between devices: 142 us -> none  [the longest x1 68 us: attend_forward(): key_part = lax.all_gather(key_rows, 'ctx', axis=1, tiled=True)]
    dot_general x60 -> x3, matrix products: 94.5 us -> 3.88 us  [contract(): lax.dot_general(left, right, (((left_dim,), (right_dim,)), ((), ())), pre...]
    pallas_call x0 -> x9, Pallas kernels: none -> 87.4 us  [the longest x3 26.5 us: pair_grad(): pl.pallas_call(grad_kernel, grid_spec=pltpu.PrefetchScalarGridSpec(num_sc...]
    ppermute x32 -> x83, starting transfers between devices: 16.4 us -> 92.8 us  [exchange(): return lax.ppermute(values, axis, [(i, i ^ bit) for i in range(count)])]
    ppermute x32 -> x83, waiting for transfers between devices: 267 us -> 294 us  [exchange(): return lax.ppermute(values, axis, [(i, i ^ bit) for i in range(count)])]
    convert_element_type x29 -> x0, other arithmetic: 24.9 us -> none  [the longest x8 15.1 us: turn_keys(): key_acc.astype(jnp.bfloat16)]
    reduce_scatter x4 -> x0, waiting for transfers between devices: 23.6 us -> none  [the longest x1 20.9 us: on_device(): lax.psum_scatter(back_grad.astype(jnp.bfloat16), 'fsdp', scatter_dimensio...]
  transfers between devices with their start and end apart: 42 -> 83, of which waited for: 37 -> 38; matrix products, arithmetic and copies ran while one was open for 10% -> 15% of each run, Pallas kernels for 0% -> 13%
where the time goes in v1:
time: 612 us; the launch traced here: 602 us
  waiting for transfers between devices  294 us (48%)
  starting transfers between devices  92.8 us (15%)
  Pallas kernels  87.4 us (14%)
  local copies, waits for them, and re-layouts  43.1 us (7%)
  matrix products  43.1 us (7%)
  other arithmetic  39.9 us (7%)
    ppermute x83, waiting for transfers between devices, exchange(): return lax.ppermute(values, axis, [(i, i ^ bit) for i in range(count)])  294 us
    ppermute x83, starting transfers between devices, exchange(): return lax.ppermute(values, axis, [(i, i ^ bit) for i in range(count)])  92.8 us
    unnamed x106, local copies, waits for them, and re-layouts  40.5 us
    pallas_call x3, Pallas kernels, pair_grad(): pl.pallas_call(grad_kernel, grid_spec=pltpu.PrefetchScalarGridSpec(num_sc...  26.5 us
    dot_general x4, matrix products, back_project(): jnp.einsum('wkb,fb->wkf', gradient_row_block, right_operand_matrix, prefe...  21.4 us
    pallas_call x3, Pallas kernels, put_in_place(): pl.pallas_call(place_kernel, grid_spec=pltpu.PrefetchScalarGridSpec(num_s...  19 us
    dot_general x4, matrix products, project(): jnp.einsum('ugj,jn->ugn', left_operand_rows, right_operand_matrix, prefer...  17.8 us
    convert_element_type x16, other arithmetic, lowered(): return values.astype(jnp.bfloat16)  16.7 us
  transfers between devices with their start and end apart: 83, of which 38 were waited for; matrix products, arithmetic and copies ran while one was open for 15% of the time, Pallas kernels for 13%

profile of v1, /device:TPU:0, one launch (start us, length us, event | category | flops | bytes accessed | tf_op | source)
XLA Modules:
  0.0 601.9 jit_solution(15031320452236086436)
XLA Ops:
  1.2 2.6 collective-permute-start
  5.3 2.6 collective-permute-start.3
  19.9 11.6 %collective-permute-done.3 = bf16[2,128,1024]{2,1,0:T(8,128)(2,1)} collective-permute-done((bf16[2,128,1024]{2,1,0:T(8,128)(2,1)}, bf16[2,128,1024]{2,1,0:T(8,128)(2,1)}, u32[]{:S(2)}, u32[]{:S(2)}) %collective-permute-start.3) | collective-permute-done | bytes 524320 | tf_op jit(solution)/shard_map/ppermute | solution.py:373
  36.2 7.3 %collective-permute-done.5 = bf16[2,128,1024]{2,1,0:T(8,128)(2,1)S(1)} collective-permute-done((bf16[2,128,1024]{2,1,0:T(8,128)(2,1)}, bf16[2,128,1024]{2,1,0:T(8,128)(2,1)S(1)}, u32[]{:S(2)}, u32[]{:S(2)}) %collective-permute-start.5) | collective-permute-done | bytes 524320 | tf_op jit(solution)/shard_map/ppermute | solution.py:373
  49.8 8.5 %collective-permute-done.4 = bf16[2,128,1024]{2,1,0:T(8,128)(2,1)S(1)} collective-permute-done((bf16[2,128,1024]{2,1,0:T(8,128)(2,1)}, bf16[2,128,1024]{2,1,0:T(8,128)(2,1)S(1)}, u32[]{:S(2)}, u32[]{:S(2)}) %collective-permute-start.4) | collective-permute-done | bytes 524320 | tf_op jit(solution)/shard_map/ppermute | solution.py:373
  60.0 7.5 %collective-permute-done.6 = bf16[2,128,1024]{2,1,0:T(8,128)(2,1)S(1)} collective-permute-done((bf16[2,128,1024]{2,1,0:T(8,128)(2,1)S(1)}, bf16[2,128,1024]{2,1,0:T(8,128)(2,1)S(1)}, u32[]{:S(2)}, u32[]{:S(2)}) %collective-permute-start.6) | collective-permute-done | bytes 524320 | tf_op jit(solution)/shard_map/ppermute | solution.py:373
  68.4 2.3 broadcast_select_fusion.4
  75.2 2.4 add_convert_fusion.1.query_ref.key_ref.value_ref
  77.6 11.5 %attention_forward.1 = (f32[2,1024,128]{2,1,0:T(8,128)S(1)}, bf16[2,1024,128]{2,1,0:T(8,128)(2,1)S(1)}, f32[2,1024,128]{2,1,0:T(8,128)S(1)}) custom-call(bf16[2,1024,384]{2,1,0:T(8,128)(2,1)S(1)} %add_convert_fusion.1.query_ref.key_ref.value_ref, bf16[2,1024,384]{2,1,0:T(8,128)(2,1)S(1)} %add_convert_fusion.1.query_ref.key_ref.value_ref, ...), custom_call_target="tpu_custom_call" | custom-call | tf_op jit(solution)/shard_map/attention_forward/pallas_call | solution.py:453
  92.8 2.4 collective-permute-start.11
  95.9 2.9 collective-permute-start.9
  108.4 3.9 broadcast_select_fusion.3
  112.3 8.7 %fusion.28 = (u8[128,4096]{1,0:T(8,128)(4,1)S(1)}, u8[128,4096]{1,0:T(8,128)(4,1)S(1)}, f32[2,128,4096]{2,1,0:T(8,128)}) fusion(f32[4096]{0:T(1024)S(1)} %maximum_convert_fusion, bf16[2,128,1024]{2,1,0:T(8,128)(2,1)S(1)} %fusion.29, bf16[512,4096]{1,0:T(8,128)(2,1)} %get-tuple-element.100, bf16[512,4096]{1,0:T(8,128)(2,1)S(1)} %get-tuple-element.99), kind=kOutput, calls=%fused_computation.91 | convolution fusion | flops 2177892352 | bytes 14172160 | tf_op jit(solution)/shard_map/ugj,jn->ugn/dot_general | solution.py:39
  121.0 11.7 %multiply_convert_fusion = (bf16[2,128,4096]{2,1,0:T(8,128)(2,1)S(1)}, f32[2,128,4096]{2,1,0:T(8,128)}) fusion(f32[2,128,4096]{2,1,0:T(8,128)} %get-tuple-element.233, u8[128,4096]{1,0:T(8,128)(4,1)S(1)} %get-tuple-element.40, u8[128,4096]{1,0:T(8,128)(4,1)S(1)} %get-tuple-element.39), kind=kLoop, calls=%fused_computation.25 | loop fusion | flops 73400320 | bytes 11534336 | tf_op jit(solution)/shard_map/convert_element_type | solution.py:31
  132.7 2.6 broadcast_select_fusion.1
  135.3 5.9 fusion.58
  143.6 10.9 %convert_reduce_fusion = (f32[4096]{0:T(1024)S(1)}, bf16[2,128,4096]{2,1,0:T(8,128)(2,1)}) fusion(f32[2,128,4096]{2,1,0:T(8,128)} %get-tuple-element.86, f32[2,128,4096]{2,1,0:T(8,128)} %get-tuple-element.233, bf16[2,128,1024]{2,1,0:T(8,128)(2,1)S(1)} %get-tuple-element.52, bf16[2048,1024]{1,0:T(8,128)(2,1)} %get-tuple-element.98, ...), kind=kOutput, calls=%fused_computation.23 | convolution fusion | flops 2181033984 | bytes 19415040 | tf_op jit(solution)/shard_map/wkb,fb->wkf/dot_general | solution.py:51
  154.5 7.0 %multiply_reduce_fusion = (f32[1024]{0:T(1024)S(1)}, f32[2,128]{1,0:T(2,128)S(1)}, f32[1024]{0:T(1024)S(1)}, f32[2,128,1024]{2,1,0:T(8,128)S(1)}) fusion(f32[2,128,1024]{2,1,0:T(8,128)S(1)} %get-tuple-element.232, f32[2,128]{1,0:T(2,128)S(1)} %fusion.38, f32[2,128]{1,0:T(2,128)S(1)} %broadcast_multiply_fusion.1, f32[1024]{0:T(1024)S(1)} %get-tuple-element.239, ...), kind=kOutput, calls=%fused_computation.80 | convolution fusion | flops 2168715008 | bytes 14179328 | tf_op jit(solution)/shard_map/wkb,fb->wkf/dot_general | solution.py:51
  173.7 2.9 collective-permute-start.25
  176.8 3.3 collective-permute-done.23
  180.9 14.3 %attention_backward.1 = (bf16[2,1024,128]{2,1,0:T(8,128)(2,1)S(1)}, bf16[2,1024,128]{2,1,0:T(8,128)(2,1)S(1)}, bf16[2,1024,128]{2,1,0:T(8,128)(2,1)S(1)}) custom-call(bf16[2,1024,384]{2,1,0:T(8,128)(2,1)S(1)} %add_convert_fusion.1.query_ref.key_ref.value_ref, bf16[2,1024,384]{2,1,0:T(8,128)(2,1)S(1)} %add_convert_fusion.1.query_ref.key_ref.value_ref, ...), custom_call_target="tpu_custom_call" | custom-call | tf_op jit(solution)/shard_map/attention_backward/pallas_call | solution.py:532
  203.4 2.0 collective-permute-done.40
  205.5 3.6 collective-permute-start.41
  210.6 2.5 collective-permute-start.42
  220.3 2.1 collective-permute-start.30
  223.4 4.9 collective-permute-done.60
  228.3 4.1 collective-permute-done.61
  234.1 8.5 %collective-permute-done.62 = f32[10240]{0:T(1024)S(1)} collective-permute-done((f32[10240]{0:T(1024)S(1)}, f32[10240]{0:T(1024)S(1)}, u32[]{:S(2)}, u32[]{:S(2)}) %collective-permute-start.62) | collective-permute-done | bytes 40992 | tf_op jit(solution)/shard_map/ppermute | solution.py:373
  243.3 2.9 collective-permute-start.28
  246.2 2.2 collective-permute-start.27
  248.4 2.6 collective-permute-start.26
  251.6 6.7 %collective-permute-done.29 = bf16[2,128,384]{2,1,0:T(8,128)(2,1)S(1)} collective-permute-done((bf16[2,128,384]{2,1,0:T(8,128)(2,1)S(1)}, bf16[2,128,384]{2,1,0:T(8,128)(2,1)S(1)}, u32[]{:S(2)}, u32[]{:S(2)}) %collective-permute-start.29) | collective-permute-done | bytes 196640 | tf_op jit(solution)/shard_map/ppermute | solution.py:373
  258.4 4.1 collective-permute-done.28
  266.4 8.8 %grad_back.1 = (bf16[8,256,512]{2,1,0:T(8,128)(2,1)S(1)}, bf16[8,256,512]{2,1,0:T(8,128)(2,1)}) custom-call(s32[1]{0:T(128)} %bitcast.17.place_ref, bf16[256,2048]{1,0:T(8,128)(2,1)S(1)} %get-tuple-element.113.left_own, bf16[256,2048]{1,0:T(8,128)(2,1)S(1)} %collective-permute-done.73.left_other, bf16[256,1024]{1,0:T(8,128)(2,1)S(1)} %bitcast.81, ...), custom_call_target="tpu_custom_call" | custom-call | tf_op jit(solution)/shard_map/grad_back/pallas_call | solution.py:587
  277.8 11.6 %grad_in.1 = (bf16[8,512,256]{2,1,0:T(8,128)(2,1)S(1)}, bf16[8,512,256]{2,1,0:T(8,128)(2,1)S(1)}) custom-call(s32[1]{0:T(128)} %bitcast.20.place_ref, bf16[256,512]{1,0:T(8,128)(2,1)S(1)} %get-tuple-element.133.left_own, bf16[256,512]{1,0:T(8,128)(2,1)S(1)} %collective-permute-done.63.left_other, bf16[256,4096]{1,0:T(8,128)(2,1)} %bitcast.22.right_own, ...), custom_call_target="tpu_custom_call" | custom-call | tf_op jit(solution)/shard_map/grad_in/pallas_call | solution.py:587
  298.2 25.2 %collective-permute-done.75 = bf16[8,256,512]{2,1,0:T(8,128)(2,1)} collective-permute-done((bf16[8,256,512]{2,1,0:T(8,128)(2,1)}, bf16[8,256,512]{2,1,0:T(8,128)(2,1)}, u32[]{:S(2)}, u32[]{:S(2)}) %collective-permute-start.75) | collective-permute-done | bytes 2097184 | tf_op jit(solution)/shard_map/ppermute | solution.py:373
  323.4 2.2 add_convert_fusion.3
  326.9 11.0 %collective-permute-done.65 = bf16[8,512,256]{2,1,0:T(8,128)(2,1)S(1)} collective-permute-done((bf16[8,512,256]{2,1,0:T(8,128)(2,1)S(1)}, bf16[8,512,256]{2,1,0:T(8,128)(2,1)S(1)}, u32[]{:S(2)}, u32[]{:S(2)}) %collective-permute-start.65) | collective-permute-done | bytes 2097184 | tf_op jit(solution)/shard_map/ppermute | solution.py:373
  342.6 17.3 %collective-permute-done.76 = bf16[4,256,512]{2,1,0:T(8,128)(2,1)S(1)} collective-permute-done((bf16[4,256,512]{2,1,0:T(8,128)(2,1)S(1)}, bf16[4,256,512]{2,1,0:T(8,128)(2,1)S(1)}, u32[]{:S(2)}, u32[]{:S(2)}) %collective-permute-start.76) | collective-permute-done | bytes 1048608 | tf_op jit(solution)/shard_map/ppermute | solution.py:373
  360.2 4.2 collective-permute-start.77
  364.6 2.6 collective-permute-start.67
  370.2 6.9 %collective-permute-done.77 = bf16[2,256,512]{2,1,0:T(8,128)(2,1)S(1)} collective-permute-done((bf16[2,256,512]{2,1,0:T(8,128)(2,1)S(1)}, bf16[2,256,512]{2,1,0:T(8,128)(2,1)S(1)}, u32[]{:S(2)}, u32[]{:S(2)}) %collective-permute-start.77) | collective-permute-done | bytes 524320 | tf_op jit(solution)/shard_map/ppermute | solution.py:373
  377.2 2.8 collective-permute-start.78
  380.0 13.0 %collective-permute-done.67 = bf16[2,512,256]{2,1,0:T(8,128)(2,1)S(1)} collective-permute-done((bf16[2,512,256]{2,1,0:T(8,128)(2,1)S(1)}, bf16[2,512,256]{2,1,0:T(8,128)(2,1)S(1)}, u32[]{:S(2)}, u32[]{:S(2)}) %collective-permute-start.67) | collective-permute-done | bytes 524320 | tf_op jit(solution)/shard_map/ppermute | solution.py:373
  394.5 6.1 %grad_out.1 = (bf16[8,256,128]{2,1,0:T(8,128)(2,1)S(1)}, bf16[8,256,128]{2,1,0:T(8,128)(2,1)S(1)}) custom-call(s32[1]{0:T(128)} %bitcast.17.place_ref, bf16[256,512]{1,0:T(8,128)(2,1)S(1)} %get-tuple-element.137.left_own, bf16[256,512]{1,0:T(8,128)(2,1)S(1)} %collective-permute-done.48.left_other, bf16[256,1024]{1,0:T(8,128)(2,1)S(1)} %bitcast.83, ...), custom_call_target="tpu_custom_call" | custom-call | tf_op jit(solution)/shard_map/grad_out/pallas_call | solution.py:587
  401.7 2.7 collective-permute-start.79
  404.3 7.9 %collective-permute-done.68 = bf16[1,512,256]{2,1,0:T(8,128)(2,1)S(1)} collective-permute-done((bf16[1,512,256]{2,1,0:T(8,128)(2,1)S(1)}, bf16[1,512,256]{2,1,0:T(8,128)(2,1)S(1)}, u32[]{:S(2)}, u32[]{:S(2)}) %collective-permute-start.68) | collective-permute-done | bytes 262176 | tf_op jit(solution)/shard_map/ppermute | solution.py:373
  413.4 10.1 %collective-permute-done.79 = bf16[1,256,512]{2,1,0:T(8,128)(2,1)S(1)} collective-permute-done((bf16[1,256,512]{2,1,0:T(8,128)(2,1)S(1)}, bf16[1,256,512]{2,1,0:T(8,128)(2,1)S(1)}, u32[]{:S(2)}, u32[]{:S(2)}) %collective-permute-start.79) | collective-permute-done | bytes 262176 | tf_op jit(solution)/shard_map/ppermute | solution.py:373
  423.6 5.5 collective-permute-done.69
  431.6 8.7 %collective-permute-done.80 = bf16[2,256,512]{2,1,0:T(8,128)(2,1)S(1)} collective-permute-done((bf16[2,256,512]{2,1,0:T(8,128)(2,1)S(1)}, bf16[2,256,512]{2,1,0:T(8,128)(2,1)S(1)}, u32[]{:S(2)}, u32[]{:S(2)}) %collective-permute-start.80) | collective-permute-done | bytes 524320 | tf_op jit(solution)/shard_map/ppermute | solution.py:373
  441.3 10.1 %collective-permute-done.70 = bf16[2,512,256]{2,1,0:T(8,128)(2,1)S(1)} collective-permute-done((bf16[2,512,256]{2,1,0:T(8,128)(2,1)S(1)}, bf16[2,512,256]{2,1,0:T(8,128)(2,1)S(1)}, u32[]{:S(2)}, u32[]{:S(2)}) %collective-permute-start.70) | collective-permute-done | bytes 524320 | tf_op jit(solution)/shard_map/ppermute | solution.py:373
  452.7 2.1 collective-permute-start.52
  454.8 9.8 %collective-permute-done.36 = bf16[2,3,256,128]{3,2,1,0:T(8,128)(2,1)S(1)} collective-permute-done((bf16[2,3,256,128]{3,2,1,0:T(8,128)(2,1)S(1)}, bf16[2,3,256,128]{3,2,1,0:T(8,128)(2,1)S(1)}, u32[]{:S(2)}, u32[]{:S(2)}) %collective-permute-start.36) | collective-permute-done | bytes 393248 | tf_op jit(solution)/shard_map/ppermute | solution.py:373
  469.2 8.4 %collective-permute-done.71 = bf16[4,512,256]{2,1,0:T(8,128)(2,1)S(1)} collective-permute-done((bf16[4,512,256]{2,1,0:T(8,128)(2,1)S(1)}, bf16[4,512,256]{2,1,0:T(8,128)(2,1)S(1)}, u32[]{:S(2)}, u32[]{:S(2)}) %collective-permute-start.71) | collective-permute-done | bytes 1048608 | tf_op jit(solution)/shard_map/ppermute | solution.py:373
  479.6 22.7 %collective-permute-done.53 = bf16[1,256,128]{2,1,0:T(8,128)(2,1)S(1)} collective-permute-done((bf16[1,256,128]{2,1,0:T(8,128)(2,1)S(1)}, bf16[1,256,128]{2,1,0:T(8,128)(2,1)S(1)}, u32[]{:S(2)}, u32[]{:S(2)}) %collective-permute-start.53) | collective-permute-done | bytes 65568 | tf_op jit(solution)/shard_map/ppermute | solution.py:373
  503.9 3.9 collective-permute-done.54
  507.8 4.9 collective-permute-done.55
  513.7 15.6 %collective-permute-done.56 = bf16[4,256,128]{2,1,0:T(8,128)(2,1)S(1)} collective-permute-done((bf16[4,256,128]{2,1,0:T(8,128)(2,1)S(1)}, bf16[4,256,128]{2,1,0:T(8,128)(2,1)S(1)}, u32[]{:S(2)}, u32[]{:S(2)}) %collective-permute-start.56) | collective-permute-done | bytes 262176 | tf_op jit(solution)/shard_map/ppermute | solution.py:373
  530.3 2.8 fusion.16
  533.1 33.5 %collective-permute-done.57.far_ref = bf16[8,256,128]{2,1,0:T(8,128)(2,1)S(1)} collective-permute-done((bf16[8,256,128]{2,1,0:T(8,128)(2,1)S(1)}, bf16[8,256,128]{2,1,0:T(8,128)(2,1)S(1)}, u32[]{:S(2)}, u32[]{:S(2)}) %collective-permute-start.57) | collective-permute-done | bytes 524320 | tf_op jit(solution)/shard_map/ppermute | solution.py:373
  566.6 5.4 place_out.1
  572.0 16.1 %place_qkv.1 = f32[512,3072]{1,0:T(8,128)} custom-call(s32[1]{0:T(128)} %bitcast.5.place_ref, bf16[8,3,256,128]{3,2,1,0:T(8,128)(2,1)S(1)} %pad_maximum_fusion.4.near_ref, bf16[8,3,256,128]{3,2,1,0:T(8,128)(2,1)S(1)} %collective-permute-done.38.far_ref), custom_call_target="tpu_custom_call" | custom-call | tf_op jit(solution)/shard_map/place_qkv/pallas_call | solution.py:681
  588.0 6.8 %place_back.1 = f32[2048,1024]{1,0:T(8,128)} custom-call(s32[1]{0:T(128)} %bitcast.17.place_ref, bf16[8,256,512]{2,1,0:T(8,128)(2,1)S(1)} %pad_maximum_fusion.2.near_ref, bf16[8,256,512]{2,1,0:T(8,128)(2,1)S(1)} %collective-permute-done.82.far_ref), custom_call_target="tpu_custom_call" | custom-call | tf_op jit(solution)/shard_map/place_back/pallas_call | solution.py:646
  594.9 6.8 %place_in.1 = f32[512,4096]{1,0:T(8,128)} custom-call(s32[1]{0:T(128)} %bitcast.20.place_ref, bf16[8,512,256]{2,1,0:T(8,128)(2,1)S(1)} %pad_maximum_fusion.1.near_ref, bf16[8,512,256]{2,1,0:T(8,128)(2,1)S(1)} %collective-permute-done.72.far_ref), custom_call_target="tpu_custom_call" | custom-call | tf_op jit(solution)/shard_map/place_in/pallas_call | solution.py:646
  (342 shorter events, 125.6 us)
Async XLA Ops:
  0.6 67.8 %collective-permute-start.7 = (bf16[512,3072]{1,0:T(8,128)(2,1)}, bf16[512,3072]{1,0:T(8,128)(2,1)}, u32[]{:S(2)}, u32[]{:S(2)}) collective-permute-start(bf16[512,3072]{1,0:T(8,128)(2,1)} %param.16), channel_id=1, source_target_pairs={{0,1},{1,0},{2,3},{3,2},{4,5},{5,4},{6,7},{7,6},{8,9},{9,8},{10,11... | collective-permute-start | bytes 9437192 | tf_op jit(solution)/shard_map/ppermute | solution.py:373
  1.2 33.1 %collective-permute-start = (bf16[2,128,1024]{2,1,0:T(8,128)(2,1)}, bf16[2,128,1024]{2,1,0:T(8,128)(2,1)}, u32[]{:S(2)}, u32[]{:S(2)}) collective-permute-start(bf16[2,128,1024]{2,1,0:T(8,128)(2,1)} %param.15), channel_id=1, source_target_pairs={{0,2},{2,0},{4,6},{6,4},{8,10},{10,8},{12,14},{14,12},{1,3},{3,1},... | collective-permute-start | bytes 1572872 | tf_op jit(solution)/shard_map/ppermute | solution.py:373
  3.8 28.2 %collective-permute-start.1 = (bf16[2,128,1024]{2,1,0:T(8,128)(2,1)}, bf16[2,128,1024]{2,1,0:T(8,128)(2,1)}, u32[]{:S(2)}, u32[]{:S(2)}) collective-permute-start(bf16[2,128,1024]{2,1,0:T(8,128)(2,1)} %param.15), channel_id=1, source_target_pairs={{0,4},{2,6},{4,0},{6,2},{8,12},{10,14},{12,8},{14,10},{1,5},{3,7},... | collective-permute-start | bytes 1572872 | tf_op jit(solution)/shard_map/ppermute | solution.py:373
  5.3 26.2 %collective-permute-start.3 = (bf16[2,128,1024]{2,1,0:T(8,128)(2,1)}, bf16[2,128,1024]{2,1,0:T(8,128)(2,1)}, u32[]{:S(2)}, u32[]{:S(2)}) collective-permute-start(bf16[2,128,1024]{2,1,0:T(8,128)(2,1)} %param.15), channel_id=1, source_target_pairs={{0,8},{2,10},{4,12},{6,14},{8,0},{10,2},{12,4},{14,6},{1,9},{3,11}... | collective-permute-start | bytes 1572872 | tf_op jit(solution)/shard_map/ppermute | solution.py:373
  31.6 12.0 %collective-permute-start.5 = (bf16[2,128,1024]{2,1,0:T(8,128)(2,1)}, bf16[2,128,1024]{2,1,0:T(8,128)(2,1)S(1)}, u32[]{:S(2)}, u32[]{:S(2)}) collective-permute-start(bf16[2,128,1024]{2,1,0:T(8,128)(2,1)} %collective-permute-done.3), channel_id=1, source_target_pairs={{0,4},{2,6},{4,0},{6,2},{8,12},{10,14},{12,8},{14,10},{1,5},{3,7},... | collective-permute-start | bytes 1572872 | tf_op jit(solution)/shard_map/ppermute | solution.py:373
  32.0 15.1 %collective-permute-start.2 = (bf16[2,128,1024]{2,1,0:T(8,128)(2,1)}, bf16[2,128,1024]{2,1,0:T(8,128)(2,1)S(1)}, u32[]{:S(2)}, u32[]{:S(2)}) collective-permute-start(bf16[2,128,1024]{2,1,0:T(8,128)(2,1)} %collective-permute-done.1), channel_id=1, source_target_pairs={{0,2},{2,0},{4,6},{6,4},{8,10},{10,8},{12,14},{14,12},{1,3},{3,1},... | collective-permute-start | bytes 1572872 | tf_op jit(solution)/shard_map/ppermute | solution.py:373
  32.7 25.6 %collective-permute-start.4 = (bf16[2,128,1024]{2,1,0:T(8,128)(2,1)}, bf16[2,128,1024]{2,1,0:T(8,128)(2,1)S(1)}, u32[]{:S(2)}, u32[]{:S(2)}) collective-permute-start(bf16[2,128,1024]{2,1,0:T(8,128)(2,1)} %collective-permute-done.3), channel_id=1, source_target_pairs={{0,2},{2,0},{4,6},{6,4},{8,10},{10,8},{12,14},{14,12},{1,3},{3,1},... | collective-permute-start | bytes 1572872 | tf_op jit(solution)/shard_map/ppermute | solution.py:373
  34.3 58.5 %collective-permute-start.16 = (bf16[512,1024]{1,0:T(8,128)(2,1)}, bf16[512,1024]{1,0:T(8,128)(2,1)}, u32[]{:S(2)}, u32[]{:S(2)}) collective-permute-start(bf16[512,1024]{1,0:T(8,128)(2,1)} %param.19), channel_id=1, source_target_pairs={{0,1},{1,0},{2,3},{3,2},{4,5},{5,4},{6,7},{7,6},{8,9},{9,8},{10,11... | collective-permute-start | bytes 3145736 | tf_op jit(solution)/shard_map/ppermute | solution.py:373
  43.6 24.0 %collective-permute-start.6 = (bf16[2,128,1024]{2,1,0:T(8,128)(2,1)S(1)}, bf16[2,128,1024]{2,1,0:T(8,128)(2,1)S(1)}, u32[]{:S(2)}, u32[]{:S(2)}) collective-permute-start(bf16[2,128,1024]{2,1,0:T(8,128)(2,1)S(1)} %collective-permute-done.5), channel_id=1, source_target_pairs={{0,2},{2,0},{4,6},{6,4},{8,10},{10,8},{12,14},{14,12},{1,3},{3,1},... | collective-permute-start | bytes 1572872 | tf_op jit(solution)/shard_map/ppermute | solution.py:373
  47.1 61.3 %collective-permute-start.17 = (bf16[512,4096]{1,0:T(8,128)(2,1)}, bf16[512,4096]{1,0:T(8,128)(2,1)}, u32[]{:S(2)}, u32[]{:S(2)}) collective-permute-start(bf16[512,4096]{1,0:T(8,128)(2,1)} %param.23), channel_id=1, source_target_pairs={{0,1},{1,0},{2,3},{3,2},{4,5},{5,4},{6,7},{7,6},{8,9},{9,8},{10,11... | collective-permute-start | bytes 12582920 | tf_op jit(solution)/shard_map/ppermute | solution.py:373
  91.0 7.7 %collective-permute-start.14 = (bf16[2,128,128]{2,1,0:T(8,128)(2,1)S(1)}, bf16[2,128,128]{2,1,0:T(8,128)(2,1)S(1)}, u32[]{:S(2)}, u32[]{:S(2)}) collective-permute-start(bf16[2,128,128]{2,1,0:T(8,128)(2,1)S(1)} %get-tuple-element.169), channel_id=1, source_target_pairs={{0,4},{2,6},{4,0},{6,2},{8,12},{10,14},{12,8},{14,10},{1,5},{3,7},... | collective-permute-start | bytes 196616 | tf_op jit(solution)/shard_map/ppermute | solution.py:373
  92.8 9.5 %collective-permute-start.11 = (bf16[2,128,128]{2,1,0:T(8,128)(2,1)S(1)}, bf16[2,128,128]{2,1,0:T(8,128)(2,1)S(1)}, u32[]{:S(2)}, u32[]{:S(2)}) collective-permute-start(bf16[2,128,128]{2,1,0:T(8,128)(2,1)S(1)} %get-tuple-element.172), channel_id=1, source_target_pairs={{0,10},{2,8},{4,14},{6,12},{8,2},{10,0},{12,6},{14,4},{1,11},{3,9}... | collective-permute-start | bytes 196616 | tf_op jit(solution)/shard_map/ppermute | solution.py:373
  95.1 8.0 %collective-permute-start.12 = (bf16[2,128,128]{2,1,0:T(8,128)(2,1)S(1)}, bf16[2,128,128]{2,1,0:T(8,128)(2,1)S(1)}, u32[]{:S(2)}, u32[]{:S(2)}) collective-permute-start(bf16[2,128,128]{2,1,0:T(8,128)(2,1)S(1)} %get-tuple-element.171), channel_id=1, source_target_pairs={{0,8},{2,10},{4,12},{6,14},{8,0},{10,2},{12,4},{14,6},{1,9},{3,11}... | collective-permute-start | bytes 196616 | tf_op jit(solution)/shard_map/ppermute | solution.py:373
  95.9 7.2 %collective-permute-start.9 = (bf16[2,128,128]{2,1,0:T(8,128)(2,1)S(1)}, bf16[2,128,128]{2,1,0:T(8,128)(2,1)S(1)}, u32[]{:S(2)}, u32[]{:S(2)}) collective-permute-start(bf16[2,128,128]{2,1,0:T(8,128)(2,1)S(1)} %get-tuple-element.173), channel_id=1, source_target_pairs={{0,14},{2,12},{4,10},{6,8},{8,6},{10,4},{12,2},{14,0},{1,15},{3,13... | collective-permute-start | bytes 196616 | tf_op jit(solution)/shard_map/ppermute | solution.py:373
  98.7 6.2 %collective-permute-start.10 = (bf16[2,128,128]{2,1,0:T(8,128)(2,1)S(1)}, bf16[2,128,128]{2,1,0:T(8,128)(2,1)S(1)}, u32[]{:S(2)}, u32[]{:S(2)}) collective-permute-start(bf16[2,128,128]{2,1,0:T(8,128)(2,1)S(1)} %get-tuple-element.167), channel_id=1, source_target_pairs={{0,12},{2,14},{4,8},{6,10},{8,4},{10,6},{12,0},{14,2},{1,13},{3,15... | collective-permute-start | bytes 196616 | tf_op jit(solution)/shard_map/ppermute | solution.py:373
  102.2 30.4 %collective-permute-start.18 = (bf16[2048,1024]{1,0:T(8,128)(2,1)S(1)}, bf16[2048,1024]{1,0:T(8,128)(2,1)S(1)}, u32[]{:S(2)}, u32[]{:S(2)}) collective-permute-start(bf16[2048,1024]{1,0:T(8,128)(2,1)S(1)} %copy-done.9), channel_id=1, source_target_pairs={{0,1},{1,0},{2,3},{3,2},{4,5},{5,4},{6,7},{7,6},{8,9},{9,8},{10,11... | collective-permute-start | bytes 12582920 | tf_op jit(solution)/shard_map/ppermute | solution.py:373
  163.8 8.1 %collective-permute-start.19 = (bf16[2,128,128]{2,1,0:T(8,128)(2,1)S(1)}, bf16[2,128,128]{2,1,0:T(8,128)(2,1)S(1)}, u32[]{:S(2)}, u32[]{:S(2)}) collective-permute-start(bf16[2,128,128]{2,1,0:T(8,128)(2,1)S(1)} %get-tuple-element.175), channel_id=1, source_target_pairs={{0,2},{2,0},{4,6},{6,4},{8,10},{10,8},{12,14},{14,12},{1,3},{3,1},... | collective-permute-start | bytes 196616 | tf_op jit(solution)/shard_map/ppermute | solution.py:373
  164.7 9.0 %collective-permute-start.20 = (bf16[2,128,128]{2,1,0:T(8,128)(2,1)S(1)}, bf16[2,128,128]{2,1,0:T(8,128)(2,1)S(1)}, u32[]{:S(2)}, u32[]{:S(2)}) collective-permute-start(bf16[2,128,128]{2,1,0:T(8,128)(2,1)S(1)} %get-tuple-element.179), channel_id=1, source_target_pairs={{0,4},{2,6},{4,0},{6,2},{8,12},{10,14},{12,8},{14,10},{1,5},{3,7},... | collective-permute-start | bytes 196616 | tf_op jit(solution)/shard_map/ppermute | solution.py:373
  166.4 10.3 %collective-permute-start.21 = (bf16[2,128,128]{2,1,0:T(8,128)(2,1)S(1)}, bf16[2,128,128]{2,1,0:T(8,128)(2,1)S(1)}, u32[]{:S(2)}, u32[]{:S(2)}) collective-permute-start(bf16[2,128,128]{2,1,0:T(8,128)(2,1)S(1)} %get-tuple-element.176), channel_id=1, source_target_pairs={{0,6},{2,4},{4,2},{6,0},{8,14},{10,12},{12,10},{14,8},{1,7},{3,5},... | collective-permute-start | bytes 196616 | tf_op jit(solution)/shard_map/ppermute | solution.py:373
  167.5 9.3 %collective-permute-start.22 = (bf16[2,128,128]{2,1,0:T(8,128)(2,1)S(1)}, bf16[2,128,128]{2,1,0:T(8,128)(2,1)S(1)}, u32[]{:S(2)}, u32[]{:S(2)}) collective-permute-start(bf16[2,128,128]{2,1,0:T(8,128)(2,1)S(1)} %get-tuple-element.177), channel_id=1, source_target_pairs={{0,8},{2,10},{4,12},{6,14},{8,0},{10,2},{12,4},{14,6},{1,9},{3,11}... | collective-permute-start | bytes 196616 | tf_op jit(solution)/shard_map/ppermute | solution.py:373
  170.4 9.7 %collective-permute-start.23 = (bf16[2,128,128]{2,1,0:T(8,128)(2,1)S(1)}, bf16[2,128,128]{2,1,0:T(8,128)(2,1)S(1)}, u32[]{:S(2)}, u32[]{:S(2)}) collective-permute-start(bf16[2,128,128]{2,1,0:T(8,128)(2,1)S(1)} %get-tuple-element.174), channel_id=1, source_target_pairs={{0,10},{2,8},{4,14},{6,12},{8,2},{10,0},{12,6},{14,4},{1,11},{3,9}... | collective-permute-start | bytes 196616 | tf_op jit(solution)/shard_map/ppermute | solution.py:373
  171.9 8.2 %collective-permute-start.24 = (bf16[2,128,128]{2,1,0:T(8,128)(2,1)S(1)}, bf16[2,128,128]{2,1,0:T(8,128)(2,1)S(1)}, u32[]{:S(2)}, u32[]{:S(2)}) collective-permute-start(bf16[2,128,128]{2,1,0:T(8,128)(2,1)S(1)} %get-tuple-element.162), channel_id=1, source_target_pairs={{0,12},{2,14},{4,8},{6,10},{8,4},{10,6},{12,0},{14,2},{1,13},{3,15... | collective-permute-start | bytes 196616 | tf_op jit(solution)/shard_map/ppermute | solution.py:373
  173.7 7.1 %collective-permute-start.25 = (bf16[2,128,128]{2,1,0:T(8,128)(2,1)S(1)}, bf16[2,128,128]{2,1,0:T(8,128)(2,1)S(1)}, u32[]{:S(2)}, u32[]{:S(2)}) collective-permute-start(bf16[2,128,128]{2,1,0:T(8,128)(2,1)S(1)} %get-tuple-element.73), channel_id=1, source_target_pairs={{0,14},{2,12},{4,10},{6,8},{8,6},{10,4},{12,2},{14,0},{1,15},{3,13... | collective-permute-start | bytes 196616 | tf_op jit(solution)/shard_map/ppermute | solution.py:373
  176.7 101.1 %collective-permute-start.64 = (bf16[256,4096]{1,0:T(8,128)(2,1)}, bf16[256,4096]{1,0:T(8,128)(2,1)}, u32[]{:S(2)}, u32[]{:S(2)}) collective-permute-start(bf16[256,4096]{1,0:T(8,128)(2,1)} %bitcast.22.right_own), channel_id=1, source_target_pairs={{0,1},{1,0},{2,3},{3,2},{4,5},{5,4},{6,7},{7,6},{8,9},{9,8},{10,11... | collective-permute-start | bytes 6291464 | tf_op jit(solution)/shard_map/ppermute | solution.py:373
  209.1 6.1 %collective-permute-start.45 = (f32[2,128]{1,0:T(2,128)S(1)}, f32[2,128]{1,0:T(2,128)S(1)}, u32[]{:S(2)}, u32[]{:S(2)}) collective-permute-start(f32[2,128]{1,0:T(2,128)S(1)} %fusion.73), channel_id=1, source_target_pairs={{0,4},{2,6},{4,0},{6,2},{8,12},{10,14},{12,8},{14,10},{1,5},{3,7},... | collective-permute-start | bytes 3080 | tf_op jit(solution)/shard_map/ppermute | solution.py:373
  218.9 24.4 %collective-permute-start.32 = (bf16[2,128,384]{2,1,0:T(8,128)(2,1)S(1)}, bf16[2,128,384]{2,1,0:T(8,128)(2,1)S(1)}, u32[]{:S(2)}, u32[]{:S(2)}) collective-permute-start(bf16[2,128,384]{2,1,0:T(8,128)(2,1)S(1)} %pad_maximum_fusion.19), channel_id=1, source_target_pairs={{0,2},{2,0},{4,6},{6,4},{8,10},{10,8},{12,14},{14,12},{1,3},{3,1},... | collective-permute-start | bytes 589832 | tf_op jit(solution)/shard_map/ppermute | solution.py:373
  219.8 26.4 %collective-permute-start.31 = (bf16[2,128,384]{2,1,0:T(8,128)(2,1)S(1)}, bf16[2,128,384]{2,1,0:T(8,128)(2,1)S(1)}, u32[]{:S(2)}, u32[]{:S(2)}) collective-permute-start(bf16[2,128,384]{2,1,0:T(8,128)(2,1)S(1)} %pad_maximum_fusion.18), channel_id=1, source_target_pairs={{0,4},{2,6},{4,0},{6,2},{8,12},{10,14},{12,8},{14,10},{1,5},{3,7},... | collective-permute-start | bytes 589832 | tf_op jit(solution)/shard_map/ppermute | solution.py:373
  220.3 28.1 %collective-permute-start.30 = (bf16[2,128,384]{2,1,0:T(8,128)(2,1)S(1)}, bf16[2,128,384]{2,1,0:T(8,128)(2,1)S(1)}, u32[]{:S(2)}, u32[]{:S(2)}) collective-permute-start(bf16[2,128,384]{2,1,0:T(8,128)(2,1)S(1)} %pad_maximum_fusion.17), channel_id=1, source_target_pairs={{0,6},{2,4},{4,2},{6,0},{8,14},{10,12},{12,10},{14,8},{1,7},{3,5},... | collective-permute-start | bytes 589832 | tf_op jit(solution)/shard_map/ppermute | solution.py:373
  232.4 10.3 %collective-permute-start.62 = (f32[10240]{0:T(1024)S(1)}, f32[10240]{0:T(1024)S(1)}, u32[]{:S(2)}, u32[]{:S(2)}) collective-permute-start(f32[10240]{0:T(1024)S(1)} %add.257), channel_id=1, source_target_pairs={{0,8},{2,10},{4,12},{6,14},{8,0},{10,2},{12,4},{14,6},{1,9},{3,11}... | collective-permute-start | bytes 122888 | tf_op jit(solution)/shard_map/ppermute | solution.py:373
  242.7 15.7 %collective-permute-start.29 = (bf16[2,128,384]{2,1,0:T(8,128)(2,1)S(1)}, bf16[2,128,384]{2,1,0:T(8,128)(2,1)S(1)}, u32[]{:S(2)}, u32[]{:S(2)}) collective-permute-start(bf16[2,128,384]{2,1,0:T(8,128)(2,1)S(1)} %pad_maximum_fusion.16), channel_id=1, source_target_pairs={{0,8},{2,10},{4,12},{6,14},{8,0},{10,2},{12,4},{14,6},{1,9},{3,11}... | collective-permute-start | bytes 589832 | tf_op jit(solution)/shard_map/ppermute | solution.py:373
  243.3 19.1 %collective-permute-start.28 = (bf16[2,128,384]{2,1,0:T(8,128)(2,1)S(1)}, bf16[2,128,384]{2,1,0:T(8,128)(2,1)S(1)}, u32[]{:S(2)}, u32[]{:S(2)}) collective-permute-start(bf16[2,128,384]{2,1,0:T(8,128)(2,1)S(1)} %pad_maximum_fusion.15), channel_id=1, source_target_pairs={{0,10},{2,8},{4,14},{6,12},{8,2},{10,0},{12,6},{14,4},{1,11},{3,9}... | collective-permute-start | bytes 589832 | tf_op jit(solution)/shard_map/ppermute | solution.py:373
  246.2 16.2 %collective-permute-start.27 = (bf16[2,128,384]{2,1,0:T(8,128)(2,1)S(1)}, bf16[2,128,384]{2,1,0:T(8,128)(2,1)S(1)}, u32[]{:S(2)}, u32[]{:S(2)}) collective-permute-start(bf16[2,128,384]{2,1,0:T(8,128)(2,1)S(1)} %pad_maximum_fusion.14), channel_id=1, source_target_pairs={{0,12},{2,14},{4,8},{6,10},{8,4},{10,6},{12,0},{14,2},{1,13},{3,15... | collective-permute-start | bytes 589832 | tf_op jit(solution)/shard_map/ppermute | solution.py:373
  248.4 14.5 %collective-permute-start.26 = (bf16[2,128,384]{2,1,0:T(8,128)(2,1)S(1)}, bf16[2,128,384]{2,1,0:T(8,128)(2,1)S(1)}, u32[]{:S(2)}, u32[]{:S(2)}) collective-permute-start(bf16[2,128,384]{2,1,0:T(8,128)(2,1)S(1)} %pad_maximum_fusion.13), channel_id=1, source_target_pairs={{0,14},{2,12},{4,10},{6,8},{8,6},{10,4},{12,2},{14,0},{1,15},{3,13... | collective-permute-start | bytes 589832 | tf_op jit(solution)/shard_map/ppermute | solution.py:373
  258.4 136.1 %collective-permute-start.48 = (bf16[256,512]{1,0:T(8,128)(2,1)}, bf16[256,512]{1,0:T(8,128)(2,1)S(1)}, u32[]{:S(2)}, u32[]{:S(2)}) collective-permute-start(bf16[256,512]{1,0:T(8,128)(2,1)} %get-tuple-element.136), channel_id=1, source_target_pairs={{0,1},{1,0},{2,3},{3,2},{4,5},{5,4},{6,7},{7,6},{8,9},{9,8},{10,11... | collective-permute-start | bytes 786440 | tf_op jit(solution)/shard_map/ppermute | solution.py:373
  262.4 15.3 %collective-permute-start.63 = (bf16[256,512]{1,0:T(8,128)(2,1)}, bf16[256,512]{1,0:T(8,128)(2,1)S(1)}, u32[]{:S(2)}, u32[]{:S(2)}) collective-permute-start(bf16[256,512]{1,0:T(8,128)(2,1)} %get-tuple-element.132), channel_id=1, source_target_pairs={{0,1},{1,0},{2,3},{3,2},{4,5},{5,4},{6,7},{7,6},{8,9},{9,8},{10,11... | collective-permute-start | bytes 786440 | tf_op jit(solution)/shard_map/ppermute | solution.py:373
  266.2 128.3 %collective-permute-start.49 = (bf16[256,1024]{1,0:T(8,128)(2,1)S(1)}, bf16[256,1024]{1,0:T(8,128)(2,1)S(1)}, u32[]{:S(2)}, u32[]{:S(2)}) collective-permute-start(bf16[256,1024]{1,0:T(8,128)(2,1)S(1)} %bitcast.82), channel_id=1, source_target_pairs={{0,1},{1,0},{2,3},{3,2},{4,5},{5,4},{6,7},{7,6},{8,9},{9,8},{10,11... | collective-permute-start | bytes 1572872 | tf_op jit(solution)/shard_map/ppermute | solution.py:373
  275.1 48.2 %collective-permute-start.75 = (bf16[8,256,512]{2,1,0:T(8,128)(2,1)}, bf16[8,256,512]{2,1,0:T(8,128)(2,1)}, u32[]{:S(2)}, u32[]{:S(2)}) collective-permute-start(bf16[8,256,512]{2,1,0:T(8,128)(2,1)} %get-tuple-element.38), channel_id=1, source_target_pairs={{0,16},{16,0},{1,17},{17,1},{2,18},{18,2},{3,19},{19,3},{4,20},{20... | collective-permute-start | bytes 6291464 | tf_op jit(solution)/shard_map/ppermute | solution.py:373
  277.7 115.7 %collective-permute-start.33 = (bf16[3,512,128]{2,1,0:T(8,128)(2,1)}, bf16[3,512,128]{2,1,0:T(8,128)(2,1)}, u32[]{:S(2)}, u32[]{:S(2)}) collective-permute-start(bf16[3,512,128]{2,1,0:T(8,128)(2,1)} %select_convert_fusion), channel_id=1, source_target_pairs={{0,1},{1,0},{2,3},{3,2},{4,5},{5,4},{6,7},{7,6},{8,9},{9,8},{10,11... | collective-permute-start | bytes 1179656 | tf_op jit(solution)/shard_map/ppermute | solution.py:373
  289.4 48.5 %collective-permute-start.65 = (bf16[8,512,256]{2,1,0:T(8,128)(2,1)S(1)}, bf16[8,512,256]{2,1,0:T(8,128)(2,1)S(1)}, u32[]{:S(2)}, u32[]{:S(2)}) collective-permute-start(bf16[8,512,256]{2,1,0:T(8,128)(2,1)S(1)} %get-tuple-element.36), channel_id=1, source_target_pairs={{0,2},{2,0},{4,6},{6,4},{8,10},{10,8},{12,14},{14,12},{1,3},{3,1},... | collective-permute-start | bytes 6291464 | tf_op jit(solution)/shard_map/ppermute | solution.py:373
  325.6 34.3 %collective-permute-start.76 = (bf16[4,256,512]{2,1,0:T(8,128)(2,1)S(1)}, bf16[4,256,512]{2,1,0:T(8,128)(2,1)S(1)}, u32[]{:S(2)}, u32[]{:S(2)}) collective-permute-start(bf16[4,256,512]{2,1,0:T(8,128)(2,1)S(1)} %get-tuple-element.107), channel_id=1, source_target_pairs={{0,2},{2,0},{4,6},{6,4},{8,10},{10,8},{12,14},{14,12},{1,3},{3,1},... | collective-permute-start | bytes 3145736 | tf_op jit(solution)/shard_map/ppermute | solution.py:373
  338.4 25.9 %collective-permute-start.66 = (bf16[4,512,256]{2,1,0:T(8,128)(2,1)S(1)}, bf16[4,512,256]{2,1,0:T(8,128)(2,1)S(1)}, u32[]{:S(2)}, u32[]{:S(2)}) collective-permute-start(bf16[4,512,256]{2,1,0:T(8,128)(2,1)S(1)} %get-tuple-element.109), channel_id=1, source_target_pairs={{0,16},{16,0},{1,17},{17,1},{2,18},{18,2},{3,19},{19,3},{4,20},{20... | collective-permute-start | bytes 3145736 | tf_op jit(solution)/shard_map/ppermute | solution.py:373
  360.2 16.9 %collective-permute-start.77 = (bf16[2,256,512]{2,1,0:T(8,128)(2,1)S(1)}, bf16[2,256,512]{2,1,0:T(8,128)(2,1)S(1)}, u32[]{:S(2)}, u32[]{:S(2)}) collective-permute-start(bf16[2,256,512]{2,1,0:T(8,128)(2,1)S(1)} %get-tuple-element.111), channel_id=1, source_target_pairs={{0,4},{2,6},{4,0},{6,2},{8,12},{10,14},{12,8},{14,10},{1,5},{3,7},... | collective-permute-start | bytes 1572872 | tf_op jit(solution)/shard_map/ppermute | solution.py:373
  364.6 28.4 %collective-permute-start.67 = (bf16[2,512,256]{2,1,0:T(8,128)(2,1)S(1)}, bf16[2,512,256]{2,1,0:T(8,128)(2,1)S(1)}, u32[]{:S(2)}, u32[]{:S(2)}) collective-permute-start(bf16[2,512,256]{2,1,0:T(8,128)(2,1)S(1)} %get-tuple-element.115), channel_id=1, source_target_pairs={{0,4},{2,6},{4,0},{6,2},{8,12},{10,14},{12,8},{14,10},{1,5},{3,7},... | collective-permute-start | bytes 1572872 | tf_op jit(solution)/shard_map/ppermute | solution.py:373
  377.2 24.3 %collective-permute-start.78 = (bf16[1,256,512]{2,1,0:T(8,128)(2,1)S(1)}, bf16[1,256,512]{2,1,0:T(8,128)(2,1)S(1)}, u32[]{:S(2)}, u32[]{:S(2)}) collective-permute-start(bf16[1,256,512]{2,1,0:T(8,128)(2,1)S(1)} %add_convert_fusion.14), channel_id=1, source_target_pairs={{0,8},{2,10},{4,12},{6,14},{8,0},{10,2},{12,4},{14,6},{1,9},{3,11}... | collective-permute-start | bytes 786440 | tf_op jit(solution)/shard_map/ppermute | solution.py:373
  393.1 19.1 %collective-permute-start.68 = (bf16[1,512,256]{2,1,0:T(8,128)(2,1)S(1)}, bf16[1,512,256]{2,1,0:T(8,128)(2,1)S(1)}, u32[]{:S(2)}, u32[]{:S(2)}) collective-permute-start(bf16[1,512,256]{2,1,0:T(8,128)(2,1)S(1)} %add_convert_fusion.17), channel_id=1, source_target_pairs={{0,8},{2,10},{4,12},{6,14},{8,0},{10,2},{12,4},{14,6},{1,9},{3,11}... | collective-permute-start | bytes 786440 | tf_op jit(solution)/shard_map/ppermute | solution.py:373
  400.6 29.6 %collective-permute-start.50 = (bf16[8,256,128]{2,1,0:T(8,128)(2,1)S(1)}, bf16[8,256,128]{2,1,0:T(8,128)(2,1)S(1)}, u32[]{:S(2)}, u32[]{:S(2)}) collective-permute-start(bf16[8,256,128]{2,1,0:T(8,128)(2,1)S(1)} %get-tuple-element.34), channel_id=1, source_target_pairs={{0,16},{16,0},{1,17},{17,1},{2,18},{18,2},{3,19},{19,3},{4,20},{20... | collective-permute-start | bytes 1572872 | tf_op jit(solution)/shard_map/ppermute | solution.py:373
  401.7 21.8 %collective-permute-start.79 = (bf16[1,256,512]{2,1,0:T(8,128)(2,1)S(1)}, bf16[1,256,512]{2,1,0:T(8,128)(2,1)S(1)}, u32[]{:S(2)}, u32[]{:S(2)}) collective-permute-start(bf16[1,256,512]{2,1,0:T(8,128)(2,1)S(1)} %add_convert_fusion.13), channel_id=1, source_target_pairs={{0,8},{2,10},{4,12},{6,14},{8,0},{10,2},{12,4},{14,6},{1,9},{3,11}... | collective-permute-start | bytes 786440 | tf_op jit(solution)/shard_map/ppermute | solution.py:373
  412.3 16.8 %collective-permute-start.69 = (bf16[1,512,256]{2,1,0:T(8,128)(2,1)S(1)}, bf16[1,512,256]{2,1,0:T(8,128)(2,1)S(1)}, u32[]{:S(2)}, u32[]{:S(2)}) collective-permute-start(bf16[1,512,256]{2,1,0:T(8,128)(2,1)S(1)} %add_convert_fusion.16), channel_id=1, source_target_pairs={{0,8},{2,10},{4,12},{6,14},{8,0},{10,2},{12,4},{14,6},{1,9},{3,11}... | collective-permute-start | bytes 786440 | tf_op jit(solution)/shard_map/ppermute | solution.py:373
  412.4 16.8 %collective-permute-start.34 = (bf16[3,256,128]{2,1,0:T(8,128)(2,1)S(1)}, bf16[3,256,128]{2,1,0:T(8,128)(2,1)S(1)}, u32[]{:S(2)}, u32[]{:S(2)}) collective-permute-start(bf16[3,256,128]{2,1,0:T(8,128)(2,1)S(1)} %select_convert_fusion.1), channel_id=1, source_target_pairs={{0,16},{16,0},{1,17},{17,1},{2,18},{18,2},{3,19},{19,3},{4,20},{20... | collective-permute-start | bytes 589832 | tf_op jit(solution)/shard_map/ppermute | solution.py:373
  423.5 16.8 %collective-permute-start.80 = (bf16[2,256,512]{2,1,0:T(8,128)(2,1)S(1)}, bf16[2,256,512]{2,1,0:T(8,128)(2,1)S(1)}, u32[]{:S(2)}, u32[]{:S(2)}) collective-permute-start(bf16[2,256,512]{2,1,0:T(8,128)(2,1)S(1)} %pad_maximum_fusion.10), channel_id=1, source_target_pairs={{0,4},{2,6},{4,0},{6,2},{8,12},{10,14},{12,8},{14,10},{1,5},{3,7},... | collective-permute-start | bytes 1572872 | tf_op jit(solution)/shard_map/ppermute | solution.py:373
  429.1 22.3 %collective-permute-start.70 = (bf16[2,512,256]{2,1,0:T(8,128)(2,1)S(1)}, bf16[2,512,256]{2,1,0:T(8,128)(2,1)S(1)}, u32[]{:S(2)}, u32[]{:S(2)}) collective-permute-start(bf16[2,512,256]{2,1,0:T(8,128)(2,1)S(1)} %pad_maximum_fusion.9), channel_id=1, source_target_pairs={{0,4},{2,6},{4,0},{6,2},{8,12},{10,14},{12,8},{14,10},{1,5},{3,7},... | collective-permute-start | bytes 1572872 | tf_op jit(solution)/shard_map/ppermute | solution.py:373
  429.3 23.2 %collective-permute-start.35 = (bf16[1,3,256,128]{3,2,1,0:T(8,128)(2,1)S(1)}, bf16[1,3,256,128]{3,2,1,0:T(8,128)(2,1)S(1)}, u32[]{:S(2)}, u32[]{:S(2)}) collective-permute-start(bf16[1,3,256,128]{3,2,1,0:T(8,128)(2,1)S(1)} %fusion.37), channel_id=1, source_target_pairs={{0,2},{2,0},{4,6},{6,4},{8,10},{10,8},{12,14},{14,12},{1,3},{3,1},... | collective-permute-start | bytes 589832 | tf_op jit(solution)/shard_map/ppermute | solution.py:373
  430.3 22.3 %collective-permute-start.51 = (bf16[4,256,128]{2,1,0:T(8,128)(2,1)S(1)}, bf16[4,256,128]{2,1,0:T(8,128)(2,1)S(1)}, u32[]{:S(2)}, u32[]{:S(2)}) collective-permute-start(bf16[4,256,128]{2,1,0:T(8,128)(2,1)S(1)} %get-tuple-element.125), channel_id=1, source_target_pairs={{0,2},{2,0},{4,6},{6,4},{8,10},{10,8},{12,14},{14,12},{1,3},{3,1},... | collective-permute-start | bytes 786440 | tf_op jit(solution)/shard_map/ppermute | solution.py:373
  440.4 27.4 %collective-permute-start.81 = (bf16[4,256,512]{2,1,0:T(8,128)(2,1)S(1)}, bf16[4,256,512]{2,1,0:T(8,128)(2,1)S(1)}, u32[]{:S(2)}, u32[]{:S(2)}) collective-permute-start(bf16[4,256,512]{2,1,0:T(8,128)(2,1)S(1)} %pad_maximum_fusion.6), channel_id=1, source_target_pairs={{0,2},{2,0},{4,6},{6,4},{8,10},{10,8},{12,14},{14,12},{1,3},{3,1},... | collective-permute-start | bytes 3145736 | tf_op jit(solution)/shard_map/ppermute | solution.py:373
  451.5 26.1 %collective-permute-start.71 = (bf16[4,512,256]{2,1,0:T(8,128)(2,1)S(1)}, bf16[4,512,256]{2,1,0:T(8,128)(2,1)S(1)}, u32[]{:S(2)}, u32[]{:S(2)}) collective-permute-start(bf16[4,512,256]{2,1,0:T(8,128)(2,1)S(1)} %pad_maximum_fusion.5), channel_id=1, source_target_pairs={{0,16},{16,0},{1,17},{17,1},{2,18},{18,2},{3,19},{19,3},{4,20},{20... | collective-permute-start | bytes 3145736 | tf_op jit(solution)/shard_map/ppermute | solution.py:373
  452.5 12.1 %collective-permute-start.36 = (bf16[2,3,256,128]{3,2,1,0:T(8,128)(2,1)S(1)}, bf16[2,3,256,128]{3,2,1,0:T(8,128)(2,1)S(1)}, u32[]{:S(2)}, u32[]{:S(2)}) collective-permute-start(bf16[2,3,256,128]{3,2,1,0:T(8,128)(2,1)S(1)} %pad_maximum_fusion.11), channel_id=1, source_target_pairs={{0,4},{2,6},{4,0},{6,2},{8,12},{10,14},{12,8},{14,10},{1,5},{3,7},... | collective-permute-start | bytes 1179656 | tf_op jit(solution)/shard_map/ppermute | solution.py:373
  452.7 13.7 %collective-permute-start.52 = (bf16[2,256,128]{2,1,0:T(8,128)(2,1)S(1)}, bf16[2,256,128]{2,1,0:T(8,128)(2,1)S(1)}, u32[]{:S(2)}, u32[]{:S(2)}) collective-permute-start(bf16[2,256,128]{2,1,0:T(8,128)(2,1)S(1)} %get-tuple-element.135), channel_id=1, source_target_pairs={{0,4},{2,6},{4,0},{6,2},{8,12},{10,14},{12,8},{14,10},{1,5},{3,7},... | collective-permute-start | bytes 393224 | tf_op jit(solution)/shard_map/ppermute | solution.py:373
  464.7 37.8 %collective-permute-start.37 = (bf16[4,3,256,128]{3,2,1,0:T(8,128)(2,1)S(1)}, bf16[4,3,256,128]{3,2,1,0:T(8,128)(2,1)S(1)}, u32[]{:S(2)}, u32[]{:S(2)}) collective-permute-start(bf16[4,3,256,128]{3,2,1,0:T(8,128)(2,1)S(1)} %pad_maximum_fusion.7), channel_id=1, source_target_pairs={{0,8},{2,10},{4,12},{6,14},{8,0},{10,2},{12,4},{14,6},{1,9},{3,11}... | collective-permute-start | bytes 2359304 | tf_op jit(solution)/shard_map/ppermute | solution.py:373
  466.5 35.9 %collective-permute-start.53 = (bf16[1,256,128]{2,1,0:T(8,128)(2,1)S(1)}, bf16[1,256,128]{2,1,0:T(8,128)(2,1)S(1)}, u32[]{:S(2)}, u32[]{:S(2)}) collective-permute-start(bf16[1,256,128]{2,1,0:T(8,128)(2,1)S(1)} %add_convert_fusion.25), channel_id=1, source_target_pairs={{0,8},{2,10},{4,12},{6,14},{8,0},{10,2},{12,4},{14,6},{1,9},{3,11}... | collective-permute-start | bytes 196616 | tf_op jit(solution)/shard_map/ppermute | solution.py:373
  468.0 120.0 %collective-permute-start.82 = (bf16[8,256,512]{2,1,0:T(8,128)(2,1)S(1)}, bf16[8,256,512]{2,1,0:T(8,128)(2,1)S(1)}, u32[]{:S(2)}, u32[]{:S(2)}) collective-permute-start(bf16[8,256,512]{2,1,0:T(8,128)(2,1)S(1)} %pad_maximum_fusion.2.near_ref), channel_id=1, source_target_pairs={{0,16},{16,0},{1,17},{17,1},{2,18},{18,2},{3,19},{19,3},{4,20},{20... | collective-permute-start | bytes 6291464 | tf_op jit(solution)/shard_map/ppermute | solution.py:373
  477.8 117.0 %collective-permute-start.72 = (bf16[8,512,256]{2,1,0:T(8,128)(2,1)S(1)}, bf16[8,512,256]{2,1,0:T(8,128)(2,1)S(1)}, u32[]{:S(2)}, u32[]{:S(2)}) collective-permute-start(bf16[8,512,256]{2,1,0:T(8,128)(2,1)S(1)} %pad_maximum_fusion.1.near_ref), channel_id=1, source_target_pairs={{0,2},{2,0},{4,6},{6,4},{8,10},{10,8},{12,14},{14,12},{1,3},{3,1},... | collective-permute-start | bytes 6291464 | tf_op jit(solution)/shard_map/ppermute | solution.py:373
  502.6 69.3 %collective-permute-start.38 = (bf16[8,3,256,128]{3,2,1,0:T(8,128)(2,1)S(1)}, bf16[8,3,256,128]{3,2,1,0:T(8,128)(2,1)S(1)}, u32[]{:S(2)}, u32[]{:S(2)}) collective-permute-start(bf16[8,3,256,128]{3,2,1,0:T(8,128)(2,1)S(1)} %pad_maximum_fusion.4.near_ref), channel_id=1, source_target_pairs={{0,16},{16,0},{1,17},{17,1},{2,18},{18,2},{3,19},{19,3},{4,20},{20... | collective-permute-start | bytes 4718600 | tf_op jit(solution)/shard_map/ppermute | solution.py:373
  512.8 16.5 %collective-permute-start.56 = (bf16[4,256,128]{2,1,0:T(8,128)(2,1)S(1)}, bf16[4,256,128]{2,1,0:T(8,128)(2,1)S(1)}, u32[]{:S(2)}, u32[]{:S(2)}) collective-permute-start(bf16[4,256,128]{2,1,0:T(8,128)(2,1)S(1)} %pad_maximum_fusion.12), channel_id=1, source_target_pairs={{0,2},{2,0},{4,6},{6,4},{8,10},{10,8},{12,14},{14,12},{1,3},{3,1},... | collective-permute-start | bytes 786440 | tf_op jit(solution)/shard_map/ppermute | solution.py:373
  529.3 37.2 %collective-permute-start.57 = (bf16[8,256,128]{2,1,0:T(8,128)(2,1)S(1)}, bf16[8,256,128]{2,1,0:T(8,128)(2,1)S(1)}, u32[]{:S(2)}, u32[]{:S(2)}) collective-permute-start(bf16[8,256,128]{2,1,0:T(8,128)(2,1)S(1)} %pad_maximum_fusion.8.near_ref), channel_id=1, source_target_pairs={{0,16},{16,0},{1,17},{17,1},{2,18},{18,2},{3,19},{19,3},{4,20},{20... | collective-permute-start | bytes 1572872 | tf_op jit(solution)/shard_map/ppermute | solution.py:373
  (47 other events, 521.9 us)

commit v2 on v1

--- a/solution.py
+++ b/solution.py
@@ -552,47 +552,62 @@
     )(projected, projected, projected, grads, result, logs)
 
 
-def grad_kernel(place_ref, left_own, left_other, right_own, right_other, keep_ref, send_ref):
+LOW = 2
+
+
+def grad_kernel(place_ref, left_own, left_other, right_own, right_other, keep_ref, send_ref, *, by_rows):
     step = pl.program_id(0)
     half = pl.num_programs(0) // 2
     total = contract(left_own[...], right_own[...], 0, 0)
     total = total + contract(left_other[...], right_other[...], 0, 0)
     total = total.astype(jnp.bfloat16)
+    low = place_ref[0] & ((1 << LOW) - 1)
+    _, rows, cols = keep_ref.shape
+
+    def put(out_ref):
+        for j in range(1 << LOW):
+            if by_rows:
+                out_ref[j ^ low] = total[j * rows : (j + 1) * rows]
+            else:
+                out_ref[j ^ low] = total[:, j * cols : (j + 1) * cols]
 
     @pl.when(step < half)
     def outgoing():
-        send_ref[0] = total
+        put(send_ref)
 
     @pl.when(step >= half)
     def kept():
-        keep_ref[0] = total
-
-
-def pair_grad(place, left_pair, right_pair, row_bits, col_bits, name):
+        put(keep_ref)
+
+
+def pair_grad(place, left_pair, right_pair, count, part, parts, by_rows, name):
     tokens, width = left_pair[0].shape
     columns = right_pair[0].shape[1]
-    rows = width >> row_bits
-    cols = columns >> col_bits
-    count = 1 << (row_bits + col_bits)
-    half = count // 2
-
-    def chunk(step):
-        return (step + half) % count
-
-    left = pl.BlockSpec((tokens, rows), lambda s, p: (0, (chunk(s) ^ p[0]) >> col_bits))
-    right = pl.BlockSpec(
-        (tokens, cols), lambda s, p: (0, (chunk(s) ^ p[0]) & ((1 << col_bits) - 1))
-    )
-    shape = jax.ShapeDtypeStruct((half, rows, cols), jnp.bfloat16)
+    steps = count >> LOW
+    half = steps // 2
+
+    def block(step, place_ref):
+        return part * steps + (((step + half) % steps) ^ (place_ref[0] >> LOW))
+
+    if by_rows:
+        rows, cols = width // (parts * count), columns
+        left = pl.BlockSpec((tokens, rows << LOW), lambda s, p: (0, block(s, p)))
+        right = pl.BlockSpec((tokens, columns), lambda s, p: (0, 0))
+    else:
+        rows, cols = width, columns // (parts * count)
+        left = pl.BlockSpec((tokens, width), lambda s, p: (0, 0))
+        right = pl.BlockSpec((tokens, cols << LOW), lambda s, p: (0, block(s, p)))
+    shape = jax.ShapeDtypeStruct((count // 2, rows, cols), jnp.bfloat16)
+    out_block = (1 << LOW, rows, cols)
     return pl.pallas_call(
-        grad_kernel,
+        partial(grad_kernel, by_rows=by_rows),
         grid_spec=pltpu.PrefetchScalarGridSpec(
             num_scalar_prefetch=1,
-            grid=(count,),
+            grid=(steps,),
             in_specs=[left, left, right, right],
             out_specs=[
-                pl.BlockSpec((1, rows, cols), lambda s, p: (jnp.maximum(s - half, 0), 0, 0)),
-                pl.BlockSpec((1, rows, cols), lambda s, p: (jnp.minimum(s, half - 1), 0, 0)),
+                pl.BlockSpec(out_block, lambda s, p: (jnp.maximum(s - half, 0), 0, 0)),
+                pl.BlockSpec(out_block, lambda s, p: (jnp.minimum(s, half - 1), 0, 0)),
             ],
         ),
         out_shape=[shape, shape],
@@ -628,85 +643,85 @@
     return owned, exchange(owned, order[0][0], order[0][1])
 
 
-def place_kernel(place_ref, near_ref, far_ref, out_ref):
-    half = pl.num_programs(0) // 2
-
-    @pl.when(pl.program_id(0) < half)
-    def from_near():
-        out_ref[...] = near_ref[0].astype(jnp.float32)
-
-    @pl.when(pl.program_id(0) >= half)
-    def from_far():
-        out_ref[...] = far_ref[0].astype(jnp.float32)
-
-
-def put_in_place(place, near, far, row_bits, col_bits, name):
-    half, rows, cols = near.shape
-    count = 2 * half
+def place_kernel(place_ref, chunks_ref, *rest, by_rows):
+    out_ref = rest[-1]
+    low = place_ref[0] & ((1 << LOW) - 1)
+    _, rows, cols = chunks_ref.shape
+    for j in range(1 << LOW):
+        values = chunks_ref[j ^ low].astype(jnp.float32)
+        if by_rows:
+            out_ref[j * rows : (j + 1) * rows, :] = values
+        else:
+            out_ref[:, j * cols : (j + 1) * cols] = values
+
+
+def put_in_place(place, chunks, far, into, part, parts, by_rows, name):
+    half, rows, cols = chunks.shape
+    steps = half >> LOW
+    first = steps if far else 0
+
+    def block(step, place_ref):
+        return part * 2 * steps + ((step + first) ^ (place_ref[0] >> LOW))
+
+    if by_rows:
+        out_shape = (rows * 2 * half * parts, cols)
+        out_spec = pl.BlockSpec((rows << LOW, cols), lambda s, p: (block(s, p), 0))
+    else:
+        out_shape = (rows, cols * 2 * half * parts)
+        out_spec = pl.BlockSpec((rows, cols << LOW), lambda s, p: (0, block(s, p)))
+    in_specs = [pl.BlockSpec((1 << LOW, rows, cols), lambda s, p: (s, 0, 0))]
+    operands = [place, chunks]
+    if into is not None:
+        in_specs.append(pl.BlockSpec(memory_space=pl.ANY))
+        operands.append(into)
     return pl.pallas_call(
-        place_kernel,
+        partial(place_kernel, by_rows=by_rows),
         grid_spec=pltpu.PrefetchScalarGridSpec(
-            num_scalar_prefetch=1,
-            grid=(count,),
-            in_specs=[
-                pl.BlockSpec((1, rows, cols), lambda s, p: (jnp.minimum(s, half - 1), 0, 0)),
-                pl.BlockSpec((1, rows, cols), lambda s, p: (jnp.maximum(s - half, 0), 0, 0)),
-            ],
-            out_specs=pl.BlockSpec(
-                (rows, cols),
-                lambda s, p: ((s ^ p[0]) >> col_bits, (s ^ p[0]) & ((1 << col_bits) - 1)),
-            ),
+            num_scalar_prefetch=1, grid=(steps,), in_specs=in_specs, out_specs=out_spec
         ),
-        out_shape=jax.ShapeDtypeStruct((rows << row_bits, cols << col_bits), jnp.float32),
+        out_shape=jax.ShapeDtypeStruct(out_shape, jnp.float32),
+        input_output_aliases={} if into is None else {2: 0},
         compiler_params=pltpu.CompilerParams(vmem_limit_bytes=48 << 20),
         name=name,
-    )(place, near, far)
-
-
-def place_three_kernel(place_ref, near_ref, far_ref, out_ref):
-    half = pl.num_programs(0) // 2
-
-    @pl.when(pl.program_id(0) < half)
-    def from_near():
-        out_ref[...] = near_ref[0, 0].astype(jnp.float32)
-
-    @pl.when(pl.program_id(0) >= half)
-    def from_far():
-        out_ref[...] = far_ref[0, 0].astype(jnp.float32)
-
-
-def put_three_in_place(place, near, far, row_bits, col_bits, name):
-    half, three, rows, cols = near.shape
-    count = 2 * half
+    )(*operands)
+
+
+def place_three_kernel(place_ref, chunks_ref, *rest):
+    out_ref = rest[-1]
+    count, _, _, cols = chunks_ref.shape
+    ctx = place_ref[0] & (count - 1)
+    for j in range(count):
+        out_ref[:, j * cols : (j + 1) * cols] = chunks_ref[j ^ ctx, 0].astype(jnp.float32)
+
+
+def put_three_in_place(place, chunks, far, into, ctx_count, dp_count, name):
+    total, three, rows, cols = chunks.shape
+    steps = total // ctx_count
+    first = steps if far else 0
+    ctx_bits = ctx_count.bit_length() - 1
+    in_specs = [
+        pl.BlockSpec((ctx_count, 1, rows, cols), lambda s, t, p: (s, t, 0, 0))
+    ]
+    operands = [place, chunks]
+    if into is not None:
+        in_specs.append(pl.BlockSpec(memory_space=pl.ANY))
+        operands.append(into)
     return pl.pallas_call(
         place_three_kernel,
         grid_spec=pltpu.PrefetchScalarGridSpec(
             num_scalar_prefetch=1,
-            grid=(count, three),
-            in_specs=[
-                pl.BlockSpec(
-                    (1, 1, rows, cols),
-                    lambda s, t, p: (
-                        jnp.minimum(s, half - 1), jnp.where(s < half, t, three - 1), 0, 0
-                    ),
-                ),
-                pl.BlockSpec(
-                    (1, 1, rows, cols),
-                    lambda s, t, p: (jnp.maximum(s - half, 0), jnp.where(s < half, 0, t), 0, 0),
-                ),
-            ],
+            grid=(steps, three),
+            in_specs=in_specs,
             out_specs=pl.BlockSpec(
-                (rows, cols),
-                lambda s, t, p: (
-                    (s ^ p[0]) >> col_bits,
-                    (t << col_bits) + ((s ^ p[0]) & ((1 << col_bits) - 1)),
-                ),
+                (rows, ctx_count * cols),
+                lambda s, t, p: ((s + first) ^ (p[0] >> ctx_bits), t),
             ),
         ),
-        out_shape=jax.ShapeDtypeStruct((rows << row_bits, three * (cols << col_bits)), jnp.float32),
+        out_shape=jax.ShapeDtypeStruct((rows * dp_count, three * ctx_count * cols), jnp.float32),
+        input_output_aliases={} if into is None else {2: 0},
         compiler_params=pltpu.CompilerParams(vmem_limit_bytes=48 << 20),
         name=name,
-    )(place, near, far)
+    )(*operands)
 
 
 def sum_everywhere(values, axes):
@@ -818,29 +833,37 @@
     dp_bits = [("dp", bit) for bit in bits_below(lax.axis_size("dp"))]
     order_x = dp_bits + ctx_bits
     order_y = ctx_bits[:1] + dp_bits + ctx_bits[1:]
+    order_z = ctx_bits[1:] + ctx_bits[:1] + dp_bits
     place_x = place_of(order_x)
     place_y = place_of(order_y)
-    total_bits = len(order_x)
-
-    back_bits = (total_bits - 1, 1)
-    back_parts = pair_grad(
-        place_x, left_pair(active_low), right_pair(second_low), *back_bits, "grad_back"
-    )
+    place_z = place_of(order_z)
+    count = 1 << len(order_x)
+
+    active_pair = left_pair(active_low)
+    normed_pair = left_pair(normed_low)
+    attended_pair = left_pair(attended_low)
+    second_pair = right_pair(second_low)
+    back_parts = [
+        pair_grad(place_x, active_pair, second_pair, count, part, 2, True, "grad_back")
+        for part in range(2)
+    ]
     back_bias_grad = column_sum(second_low)
     active_grad = back_project(second_low, back_full)
     gelu_pull = jax.vjp(partial(jax.nn.gelu, approximate=False), hidden_before_gelu)[1]
     hidden_low = lowered(gelu_pull(active_grad)[0])
-    in_bits = (0, total_bits)
-    in_parts = pair_grad(
-        place_y, left_pair(normed_low), right_pair(hidden_low), *in_bits, "grad_in"
-    )
+    hidden_low, back_parts = lax.optimization_barrier((hidden_low, back_parts))
+    hidden_pair = right_pair(hidden_low)
+    in_parts = [
+        pair_grad(place_y, normed_pair, hidden_pair, count, part, 2, False, "grad_in")
+        for part in range(2)
+    ]
     in_bias_grad = column_sum(hidden_low)
     first_grad = first_grad_res + back_project(hidden_low, in_full)
     summed_grad, gain_one_grad, shift_one_grad = pull_one(first_grad)
     branch_low = lowered(summed_grad)
-    out_bits = (1, total_bits - 1)
+    branch_low, in_parts = lax.optimization_barrier((branch_low, in_parts))
     out_parts = pair_grad(
-        place_x, left_pair(attended_low), right_pair(branch_low), *out_bits, "grad_out"
+        place_z, attended_pair, right_pair(branch_low), count, 0, 1, True, "grad_out"
     )
     out_bias_grad = column_sum(branch_low)
     attended_grad = lowered(back_project(branch_low, out_full))
@@ -879,19 +902,23 @@
         ("ctx", bit) for bit in reversed(bits_below(ctx_count))
     ]
     qkv_near, qkv_far = spread(qkv_owned, order_q)
-    qkv_grad = put_three_in_place(
-        place_q, qkv_near, qkv_far, len(dp_bits), len(ctx_bits), "place_qkv"
-    )
-
-    back_grad = put_in_place(
-        place_x, *spread(sum_to_owner(*back_parts, order_x), order_x), *back_bits, "place_back"
-    )
-    in_grad = put_in_place(
-        place_y, *spread(sum_to_owner(*in_parts, order_y), order_y), *in_bits, "place_in"
-    )
-    out_grad = put_in_place(
-        place_x, *spread(sum_to_owner(*out_parts, order_x), order_x), *out_bits, "place_out"
-    )
+    qkv_grad = None
+    for chunks, far in ((qkv_near, False), (qkv_far, True)):
+        qkv_grad = put_three_in_place(
+            place_q, chunks, far, qkv_grad, ctx_count, dp_count, "place_qkv"
+        )
+
+    def finish(parts, order, place, by_rows, name):
+        whole = None
+        for part, (keep, send) in enumerate(parts):
+            near, far = spread(sum_to_owner(keep, send, order), order)
+            whole = put_in_place(place, near, False, whole, part, len(parts), by_rows, name)
+            whole = put_in_place(place, far, True, whole, part, len(parts), by_rows, name)
+        return whole
+
+    back_grad = finish(back_parts, order_x, place_x, True, "place_back")
+    in_grad = finish(in_parts, order_y, place_y, False, "place_in")
+    out_grad = finish([out_parts], order_z, place_z, True, "place_out")
 
     mixed_pieces = []
     for part in head_grads:

time: 612 us -> 588 us (0.961)
  Pallas kernels: 87.4 us -> 58 us
  starting transfers between devices: 92.8 us -> 118 us
  local copies, waits for them, and re-layouts: 43.1 us -> 23.2 us
  waiting for transfers between devices: 294 us -> 303 us
    ppermute x83 -> x99, starting transfers between devices: 92.8 us -> 118 us  [exchange(): return lax.ppermute(values, axis, [(i, i ^ bit) for i in range(count)])]
    unnamed x106 -> x114, local copies, waits for them, and re-layouts: 40.5 us -> 20.6 us
    pallas_call x6 -> x15, Pallas kernels: 45.5 us -> 27.5 us  [the longest x5 14.2 us: pair_grad(): pl.pallas_call(partial(grad_kernel, by_rows=by_rows), grid_spec=pltpu.Pre...]
    pallas_call x1 -> x2, Pallas kernels: 16.1 us -> 4.56 us  [put_three_in_place(): pl.pallas_call(place_three_kernel, grid_spec=pltpu.PrefetchScalarGridSpec...]
    ppermute x83 -> x99, waiting for transfers between devices: 294 us -> 303 us  [exchange(): return lax.ppermute(values, axis, [(i, i ^ bit) for i in range(count)])]
    convert_element_type x16 -> x25, other arithmetic: 16.7 us -> 13.6 us  [lowered(): return values.astype(jnp.bfloat16)]
  transfers between devices with their start and end apart: 83 -> 99, of which waited for: 38 -> 43; matrix products, arithmetic and copies ran while one was open for 15% -> 16% of each run, Pallas kernels for 13% -> 10%
where the time goes in v2:
time: 588 us; the launch traced here: 578 us
  waiting for transfers between devices  303 us (52%)
  starting transfers between devices  118 us (20%)
  Pallas kernels  58 us (10%)
  matrix products  38.3 us (7%)
  other arithmetic  35.1 us (6%)
  local copies, waits for them, and re-layouts  23.2 us (4%)
    ppermute x99, waiting for transfers between devices, exchange(): return lax.ppermute(values, axis, [(i, i ^ bit) for i in range(count)])  303 us
    ppermute x99, starting transfers between devices, exchange(): return lax.ppermute(values, axis, [(i, i ^ bit) for i in range(count)])  118 us
    unnamed x114, local copies, waits for them, and re-layouts  20.6 us
    dot_general x4, matrix products, back_project(): jnp.einsum('wkb,fb->wkf', gradient_row_block, right_operand_matrix, prefe...  19.6 us
    dot_general x4, matrix products, project(): jnp.einsum('ugj,jn->ugn', left_operand_rows, right_operand_matrix, prefer...  14.9 us
    pallas_call x1, Pallas kernels, attention_backward(): pl.pallas_call(backward_kernel, grid=(seqs, length // rows), in_specs=[wh...  14.4 us
    pallas_call x5, Pallas kernels, pair_grad(): pl.pallas_call(partial(grad_kernel, by_rows=by_rows), grid_spec=pltpu.Pre...  14.2 us
    convert_element_type x25, other arithmetic, lowered(): return values.astype(jnp.bfloat16)  13.6 us
  transfers between devices with their start and end apart: 99, of which 43 were waited for; matrix products, arithmetic and copies ran while one was open for 16% of the time, Pallas kernels for 10%

profile of v2, /device:TPU:0, one launch (start us, length us, event | category | flops | bytes accessed | tf_op | source)
XLA Modules:
  0.0 577.8 jit_solution(12934152749142892174)
XLA Ops:
  1.2 2.6 collective-permute-start
  5.3 2.6 collective-permute-start.3
  19.8 11.7 %collective-permute-done.3 = bf16[2,128,1024]{2,1,0:T(8,128)(2,1)S(1)} collective-permute-done((bf16[2,128,1024]{2,1,0:T(8,128)(2,1)}, bf16[2,128,1024]{2,1,0:T(8,128)(2,1)S(1)}, u32[]{:S(2)}, u32[]{:S(2)}) %collective-permute-start.3) | collective-permute-done | bytes 524320 | tf_op jit(solution)/shard_map/ppermute | solution.py:373
  35.1 8.2 %collective-permute-done.5 = bf16[2,128,1024]{2,1,0:T(8,128)(2,1)S(1)} collective-permute-done((bf16[2,128,1024]{2,1,0:T(8,128)(2,1)S(1)}, bf16[2,128,1024]{2,1,0:T(8,128)(2,1)S(1)}, u32[]{:S(2)}, u32[]{:S(2)}) %collective-permute-start.5) | collective-permute-done | bytes 524320 | tf_op jit(solution)/shard_map/ppermute | solution.py:373
  44.6 2.2 collective-permute-done.2
  48.5 9.6 %collective-permute-done.4 = bf16[2,128,1024]{2,1,0:T(8,128)(2,1)S(1)} collective-permute-done((bf16[2,128,1024]{2,1,0:T(8,128)(2,1)S(1)}, bf16[2,128,1024]{2,1,0:T(8,128)(2,1)S(1)}, u32[]{:S(2)}, u32[]{:S(2)}) %collective-permute-start.4) | collective-permute-done | bytes 524320 | tf_op jit(solution)/shard_map/ppermute | solution.py:373
  59.7 7.5 %collective-permute-done.6 = bf16[2,128,1024]{2,1,0:T(8,128)(2,1)S(1)} collective-permute-done((bf16[2,128,1024]{2,1,0:T(8,128)(2,1)S(1)}, bf16[2,128,1024]{2,1,0:T(8,128)(2,1)S(1)}, u32[]{:S(2)}, u32[]{:S(2)}) %collective-permute-start.6) | collective-permute-done | bytes 524320 | tf_op jit(solution)/shard_map/ppermute | solution.py:373
  68.1 3.3 broadcast_select_fusion.4
  75.8 2.3 add_convert_fusion.1.query_ref.key_ref.value_ref
  78.2 11.5 %attention_forward.1 = (f32[2,1024,128]{2,1,0:T(8,128)S(1)}, bf16[2,1024,128]{2,1,0:T(8,128)(2,1)S(1)}, f32[2,1024,128]{2,1,0:T(8,128)S(1)}) custom-call(bf16[2,1024,384]{2,1,0:T(8,128)(2,1)S(1)} %add_convert_fusion.1.query_ref.key_ref.value_ref, bf16[2,1024,384]{2,1,0:T(8,128)(2,1)S(1)} %add_convert_fusion.1.query_ref.key_ref.value_ref, ...), custom_call_target="tpu_custom_call" | custom-call | tf_op jit(solution)/shard_map/attention_forward/pallas_call | solution.py:453
  93.3 2.4 collective-permute-start.11
  96.5 2.9 collective-permute-start.9
  109.0 2.3 broadcast_select_fusion.3
  111.3 9.1 %fusion.28 = (u8[128,4096]{1,0:T(8,128)(4,1)S(1)}, u8[128,4096]{1,0:T(8,128)(4,1)S(1)}, f32[2,128,4096]{2,1,0:T(8,128)S(1)}) fusion(f32[4096]{0:T(1024)S(1)} %maximum_convert_fusion, bf16[2,128,1024]{2,1,0:T(8,128)(2,1)S(1)} %fusion.29, bf16[512,4096]{1,0:T(8,128)(2,1)} %get-tuple-element.126, bf16[512,4096]{1,0:T(8,128)(2,1)S(1)} %get-tuple-element.125), kind=kOutput, calls=%fused_computation.91 | convolution fusion | flops 2177892352 | bytes 14172160 | tf_op jit(solution)/shard_map/ugj,jn->ugn/dot_general | solution.py:39
  120.5 10.5 %multiply_convert_fusion = (bf16[2,128,4096]{2,1,0:T(8,128)(2,1)S(1)}, f32[2,128,4096]{2,1,0:T(8,128)}) fusion(f32[2,128,4096]{2,1,0:T(8,128)S(1)} %get-tuple-element.267, u8[128,4096]{1,0:T(8,128)(4,1)S(1)} %get-tuple-element.68, u8[128,4096]{1,0:T(8,128)(4,1)S(1)} %get-tuple-element.67), kind=kLoop, calls=%fused_computation.25 | loop fusion | flops 73400320 | bytes 11534336 | tf_op jit(solution)/shard_map/convert_element_type | solution.py:31
  132.1 2.6 fusion.58
  139.2 9.4 %add_convert_fusion = bf16[2,128,4096]{2,1,0:T(8,128)(2,1)S(1)} fusion(f32[2,128,4096]{2,1,0:T(8,128)} %get-tuple-element.112, bf16[2,128,1024]{2,1,0:T(8,128)(2,1)S(1)} %get-tuple-element.78, bf16[2048,1024]{1,0:T(8,128)(2,1)} %copy-done.13, bf16[2048,1024]{1,0:T(8,128)(2,1)} %copy-done.12, f32[2,128,4096]{2,1,0:T(8,128)} %copy-done.14), kind=kOutput, calls=%fused_computation.24 | convolution fusion | flops 2178940928 | bytes 19398656 | tf_op jit(solution)/shard_map/wkb,fb->wkf/dot_general | solution.py:51
  148.6 2.4 grad_back.2
  151.0 2.5 grad_back.3
  153.5 6.6 %multiply_reduce_fusion = (f32[1024]{0:T(1024)S(1)}, f32[2,128]{1,0:T(2,128)S(1)}, f32[1024]{0:T(1024)S(1)}, f32[2,128,1024]{2,1,0:T(8,128)S(1)}) fusion(f32[2,128,1024]{2,1,0:T(8,128)S(1)} %get-tuple-element.266, f32[2,128]{1,0:T(2,128)S(1)} %fusion.38, f32[2,128]{1,0:T(2,128)S(1)} %broadcast_multiply_fusion.1, f32[1024]{0:T(1024)S(1)} %get-tuple-element.271, ...), kind=kOutput, calls=%fused_computation.80 | convolution fusion | flops 2168715008 | bytes 14179328 | tf_op jit(solution)/shard_map/wkb,fb->wkf/dot_general | solution.py:51
  163.3 22.9 %collective-permute-done.83 = bf16[8,64,1024]{2,1,0:T(8,128)(2,1)S(1)} collective-permute-done((bf16[8,64,1024]{2,1,0:T(8,128)(2,1)S(1)}, bf16[8,64,1024]{2,1,0:T(8,128)(2,1)S(1)}, u32[]{:S(2)}, u32[]{:S(2)}) %collective-permute-start.83) | collective-permute-done | bytes 1048608 | tf_op jit(solution)/shard_map/ppermute | solution.py:373
  187.3 20.9 %collective-permute-done.91 = bf16[8,64,1024]{2,1,0:T(8,128)(2,1)S(1)} collective-permute-done((bf16[8,64,1024]{2,1,0:T(8,128)(2,1)S(1)}, bf16[8,64,1024]{2,1,0:T(8,128)(2,1)S(1)}, u32[]{:S(2)}, u32[]{:S(2)}) %collective-permute-start.91) | collective-permute-done | bytes 1048608 | tf_op jit(solution)/shard_map/ppermute | solution.py:373
  211.4 10.8 %collective-permute-done.92 = bf16[4,64,1024]{2,1,0:T(8,128)(2,1)S(1)} collective-permute-done((bf16[4,64,1024]{2,1,0:T(8,128)(2,1)S(1)}, bf16[4,64,1024]{2,1,0:T(8,128)(2,1)S(1)}, u32[]{:S(2)}, u32[]{:S(2)}) %collective-permute-start.92) | collective-permute-done | bytes 524320 | tf_op jit(solution)/shard_map/ppermute | solution.py:373
  224.8 7.5 %collective-permute-done.93 = bf16[2,64,1024]{2,1,0:T(8,128)(2,1)S(1)} collective-permute-done((bf16[2,64,1024]{2,1,0:T(8,128)(2,1)S(1)}, bf16[2,64,1024]{2,1,0:T(8,128)(2,1)S(1)}, u32[]{:S(2)}, u32[]{:S(2)}) %collective-permute-start.93) | collective-permute-done | bytes 262176 | tf_op jit(solution)/shard_map/ppermute | solution.py:373
  232.7 2.8 collective-permute-start.87
  235.5 6.4 %collective-permute-done.94 = bf16[1,64,1024]{2,1,0:T(8,128)(2,1)S(1)} collective-permute-done((bf16[1,64,1024]{2,1,0:T(8,128)(2,1)S(1)}, bf16[1,64,1024]{2,1,0:T(8,128)(2,1)S(1)}, u32[]{:S(2)}, u32[]{:S(2)}) %collective-permute-start.94) | collective-permute-done | bytes 131104 | tf_op jit(solution)/shard_map/ppermute | solution.py:373
  243.3 3.6 grad_in.2
  247.0 3.8 grad_in.3
  253.4 2.3 collective-permute-start.24
  261.7 2.1 collective-permute-start.28
  263.8 2.8 collective-permute-start.29
  271.0 14.4 %attention_backward.1 = (bf16[2,1024,128]{2,1,0:T(8,128)(2,1)S(1)}, bf16[2,1024,128]{2,1,0:T(8,128)(2,1)S(1)}, bf16[2,1024,128]{2,1,0:T(8,128)(2,1)S(1)}) custom-call(bf16[2,1024,384]{2,1,0:T(8,128)(2,1)S(1)} %add_convert_fusion.1.query_ref.key_ref.value_ref, bf16[2,1024,384]{2,1,0:T(8,128)(2,1)S(1)} %add_convert_fusion.1.query_ref.key_ref.value_ref, ...), custom_call_target="tpu_custom_call" | custom-call | tf_op jit(solution)/shard_map/attention_backward/pallas_call | solution.py:532
  295.2 3.8 collective-permute-start.45
  308.3 2.5 collective-permute-start.34
  312.7 2.6 collective-permute-done.64
  315.4 3.7 collective-permute-start.65
  321.0 2.5 collective-permute-start.66
  324.1 8.0 %collective-permute-done.66 = f32[10240]{0:T(1024)S(1)} collective-permute-done((f32[10240]{0:T(1024)S(1)}, f32[10240]{0:T(1024)S(1)}, u32[]{:S(2)}, u32[]{:S(2)}) %collective-permute-start.66) | collective-permute-done | bytes 40992 | tf_op jit(solution)/shard_map/ppermute | solution.py:373
  332.7 2.2 collective-permute-start.31
  334.9 2.2 collective-permute-start.30
  338.2 8.7 %collective-permute-done.32 = bf16[2,128,384]{2,1,0:T(8,128)(2,1)S(1)} collective-permute-done((bf16[2,128,384]{2,1,0:T(8,128)(2,1)S(1)}, bf16[2,128,384]{2,1,0:T(8,128)(2,1)S(1)}, u32[]{:S(2)}, u32[]{:S(2)}) %collective-permute-start.32) | collective-permute-done | bytes 196640 | tf_op jit(solution)/shard_map/ppermute | solution.py:373
  353.6 4.3 collective-permute-done.38
  357.9 2.7 collective-permute-start.96
  368.2 31.4 %collective-permute-done.39 = bf16[1,3,256,128]{3,2,1,0:T(8,128)(2,1)S(1)} collective-permute-done((bf16[1,3,256,128]{3,2,1,0:T(8,128)(2,1)S(1)}, bf16[1,3,256,128]{3,2,1,0:T(8,128)(2,1)S(1)}, u32[]{:S(2)}, u32[]{:S(2)}) %collective-permute-start.39) | collective-permute-done | bytes 196640 | tf_op jit(solution)/shard_map/ppermute | solution.py:373
  405.6 6.8 %collective-permute-done.40 = bf16[2,3,256,128]{3,2,1,0:T(8,128)(2,1)S(1)} collective-permute-done((bf16[2,3,256,128]{3,2,1,0:T(8,128)(2,1)S(1)}, bf16[2,3,256,128]{3,2,1,0:T(8,128)(2,1)S(1)}, u32[]{:S(2)}, u32[]{:S(2)}) %collective-permute-start.40) | collective-permute-done | bytes 393248 | tf_op jit(solution)/shard_map/ppermute | solution.py:373
  414.4 8.1 %collective-permute-done.55 = bf16[4,32,1024]{2,1,0:T(8,128)(2,1)S(1)} collective-permute-done((bf16[4,32,1024]{2,1,0:T(8,128)(2,1)S(1)}, bf16[4,32,1024]{2,1,0:T(8,128)(2,1)S(1)}, u32[]{:S(2)}, u32[]{:S(2)}) %collective-permute-start.55) | collective-permute-done | bytes 262176 | tf_op jit(solution)/shard_map/ppermute | solution.py:373
  424.3 2.3 collective-permute-start.69
  427.6 3.0 collective-permute-start.77
  430.7 5.6 collective-permute-done.69
  439.1 3.5 collective-permute-start.70
  442.6 12.7 %collective-permute-done.70 = bf16[1,512,128]{2,1,0:T(8,128)(2,1)S(1)} collective-permute-done((bf16[1,512,128]{2,1,0:T(8,128)(2,1)S(1)}, bf16[1,512,128]{2,1,0:T(8,128)(2,1)S(1)}, u32[]{:S(2)}, u32[]{:S(2)}) %collective-permute-start.70) | collective-permute-done | bytes 131104 | tf_op jit(solution)/shard_map/ppermute | solution.py:373
  455.4 6.6 %collective-permute-done.78 = bf16[1,512,128]{2,1,0:T(8,128)(2,1)S(1)} collective-permute-done((bf16[1,512,128]{2,1,0:T(8,128)(2,1)S(1)}, bf16[1,512,128]{2,1,0:T(8,128)(2,1)S(1)}, u32[]{:S(2)}, u32[]{:S(2)}) %collective-permute-start.78) | collective-permute-done | bytes 131104 | tf_op jit(solution)/shard_map/ppermute | solution.py:373
  462.1 3.0 collective-permute-start.79
  465.1 5.0 collective-permute-done.71
  471.5 2.1 collective-permute-start.80
  475.1 2.7 collective-permute-done.72
  478.5 2.1 collective-permute-done.80
  485.3 27.1 %collective-permute-done.73 = bf16[4,512,128]{2,1,0:T(8,128)(2,1)S(1)} collective-permute-done((bf16[4,512,128]{2,1,0:T(8,128)(2,1)S(1)}, bf16[4,512,128]{2,1,0:T(8,128)(2,1)S(1)}, u32[]{:S(2)}, u32[]{:S(2)}) %collective-permute-start.73) | collective-permute-done | bytes 524320 | tf_op jit(solution)/shard_map/ppermute | solution.py:373
  512.5 11.1 %collective-permute-done.81 = bf16[4,512,128]{2,1,0:T(8,128)(2,1)S(1)} collective-permute-done((bf16[4,512,128]{2,1,0:T(8,128)(2,1)S(1)}, bf16[4,512,128]{2,1,0:T(8,128)(2,1)S(1)}, u32[]{:S(2)}, u32[]{:S(2)}) %collective-permute-start.81) | collective-permute-done | bytes 524320 | tf_op jit(solution)/shard_map/ppermute | solution.py:373
  523.8 2.1 collective-permute-start.82
  526.1 2.8 fusion.16
  533.1 30.5 %collective-permute-done.90.chunks_ref = bf16[8,64,1024]{2,1,0:T(8,128)(2,1)S(1)} collective-permute-done((bf16[8,64,1024]{2,1,0:T(8,128)(2,1)S(1)}, bf16[8,64,1024]{2,1,0:T(8,128)(2,1)S(1)}, u32[]{:S(2)}, u32[]{:S(2)}) %collective-permute-start.90) | collective-permute-done | bytes 1048608 | tf_op jit(solution)/shard_map/ppermute | solution.py:373
  566.0 2.3 place_qkv.2.rest_0_
  570.7 2.3 place_qkv.3
  (408 shorter events, 146.7 us)
Async XLA Ops:
  0.6 67.4 %collective-permute-start.7 = (bf16[512,3072]{1,0:T(8,128)(2,1)}, bf16[512,3072]{1,0:T(8,128)(2,1)}, u32[]{:S(2)}, u32[]{:S(2)}) collective-permute-start(bf16[512,3072]{1,0:T(8,128)(2,1)} %param.16), channel_id=1, source_target_pairs={{0,1},{1,0},{2,3},{3,2},{4,5},{5,4},{6,7},{7,6},{8,9},{9,8},{10,11... | collective-permute-start | bytes 9437192 | tf_op jit(solution)/shard_map/ppermute | solution.py:373
  1.2 33.0 %collective-permute-start = (bf16[2,128,1024]{2,1,0:T(8,128)(2,1)}, bf16[2,128,1024]{2,1,0:T(8,128)(2,1)S(1)}, u32[]{:S(2)}, u32[]{:S(2)}) collective-permute-start(bf16[2,128,1024]{2,1,0:T(8,128)(2,1)} %param.15), channel_id=1, source_target_pairs={{0,2},{2,0},{4,6},{6,4},{8,10},{10,8},{12,14},{14,12},{1,3},{3,1},... | collective-permute-start | bytes 1572872 | tf_op jit(solution)/shard_map/ppermute | solution.py:373
  3.8 28.1 %collective-permute-start.1 = (bf16[2,128,1024]{2,1,0:T(8,128)(2,1)}, bf16[2,128,1024]{2,1,0:T(8,128)(2,1)S(1)}, u32[]{:S(2)}, u32[]{:S(2)}) collective-permute-start(bf16[2,128,1024]{2,1,0:T(8,128)(2,1)} %param.15), channel_id=1, source_target_pairs={{0,4},{2,6},{4,0},{6,2},{8,12},{10,14},{12,8},{14,10},{1,5},{3,7},... | collective-permute-start | bytes 1572872 | tf_op jit(solution)/shard_map/ppermute | solution.py:373
  5.3 26.1 %collective-permute-start.3 = (bf16[2,128,1024]{2,1,0:T(8,128)(2,1)}, bf16[2,128,1024]{2,1,0:T(8,128)(2,1)S(1)}, u32[]{:S(2)}, u32[]{:S(2)}) collective-permute-start(bf16[2,128,1024]{2,1,0:T(8,128)(2,1)} %param.15), channel_id=1, source_target_pairs={{0,8},{2,10},{4,12},{6,14},{8,0},{10,2},{12,4},{14,6},{1,9},{3,11}... | collective-permute-start | bytes 1572872 | tf_op jit(solution)/shard_map/ppermute | solution.py:373
  31.5 11.8 %collective-permute-start.5 = (bf16[2,128,1024]{2,1,0:T(8,128)(2,1)S(1)}, bf16[2,128,1024]{2,1,0:T(8,128)(2,1)S(1)}, u32[]{:S(2)}, u32[]{:S(2)}) collective-permute-start(bf16[2,128,1024]{2,1,0:T(8,128)(2,1)S(1)} %collective-permute-done.3), channel_id=1, source_target_pairs={{0,4},{2,6},{4,0},{6,2},{8,12},{10,14},{12,8},{14,10},{1,5},{3,7},... | collective-permute-start | bytes 1572872 | tf_op jit(solution)/shard_map/ppermute | solution.py:373
  31.9 14.9 %collective-permute-start.2 = (bf16[2,128,1024]{2,1,0:T(8,128)(2,1)S(1)}, bf16[2,128,1024]{2,1,0:T(8,128)(2,1)S(1)}, u32[]{:S(2)}, u32[]{:S(2)}) collective-permute-start(bf16[2,128,1024]{2,1,0:T(8,128)(2,1)S(1)} %collective-permute-done.1), channel_id=1, source_target_pairs={{0,2},{2,0},{4,6},{6,4},{8,10},{10,8},{12,14},{14,12},{1,3},{3,1},... | collective-permute-start | bytes 1572872 | tf_op jit(solution)/shard_map/ppermute | solution.py:373
  32.6 25.4 %collective-permute-start.4 = (bf16[2,128,1024]{2,1,0:T(8,128)(2,1)S(1)}, bf16[2,128,1024]{2,1,0:T(8,128)(2,1)S(1)}, u32[]{:S(2)}, u32[]{:S(2)}) collective-permute-start(bf16[2,128,1024]{2,1,0:T(8,128)(2,1)S(1)} %collective-permute-done.3), channel_id=1, source_target_pairs={{0,2},{2,0},{4,6},{6,4},{8,10},{10,8},{12,14},{14,12},{1,3},{3,1},... | collective-permute-start | bytes 1572872 | tf_op jit(solution)/shard_map/ppermute | solution.py:373
  34.2 59.2 %collective-permute-start.16 = (bf16[512,1024]{1,0:T(8,128)(2,1)}, bf16[512,1024]{1,0:T(8,128)(2,1)S(1)}, u32[]{:S(2)}, u32[]{:S(2)}) collective-permute-start(bf16[512,1024]{1,0:T(8,128)(2,1)} %param.19), channel_id=1, source_target_pairs={{0,1},{1,0},{2,3},{3,2},{4,5},{5,4},{6,7},{7,6},{8,9},{9,8},{10,11... | collective-permute-start | bytes 3145736 | tf_op jit(solution)/shard_map/ppermute | solution.py:373
  43.3 24.0 %collective-permute-start.6 = (bf16[2,128,1024]{2,1,0:T(8,128)(2,1)S(1)}, bf16[2,128,1024]{2,1,0:T(8,128)(2,1)S(1)}, u32[]{:S(2)}, u32[]{:S(2)}) collective-permute-start(bf16[2,128,1024]{2,1,0:T(8,128)(2,1)S(1)} %collective-permute-done.5), channel_id=1, source_target_pairs={{0,2},{2,0},{4,6},{6,4},{8,10},{10,8},{12,14},{14,12},{1,3},{3,1},... | collective-permute-start | bytes 1572872 | tf_op jit(solution)/shard_map/ppermute | solution.py:373
  46.8 62.2 %collective-permute-start.17 = (bf16[512,4096]{1,0:T(8,128)(2,1)}, bf16[512,4096]{1,0:T(8,128)(2,1)S(1)}, u32[]{:S(2)}, u32[]{:S(2)}) collective-permute-start(bf16[512,4096]{1,0:T(8,128)(2,1)} %param.23), channel_id=1, source_target_pairs={{0,1},{1,0},{2,3},{3,2},{4,5},{5,4},{6,7},{7,6},{8,9},{9,8},{10,11... | collective-permute-start | bytes 12582920 | tf_op jit(solution)/shard_map/ppermute | solution.py:373
  93.3 9.5 %collective-permute-start.11 = (bf16[2,128,128]{2,1,0:T(8,128)(2,1)S(1)}, bf16[2,128,128]{2,1,0:T(8,128)(2,1)S(1)}, u32[]{:S(2)}, u32[]{:S(2)}) collective-permute-start(bf16[2,128,128]{2,1,0:T(8,128)(2,1)S(1)} %get-tuple-element.206), channel_id=1, source_target_pairs={{0,10},{2,8},{4,14},{6,12},{8,2},{10,0},{12,6},{14,4},{1,11},{3,9}... | collective-permute-start | bytes 196616 | tf_op jit(solution)/shard_map/ppermute | solution.py:373
  102.8 28.1 %collective-permute-start.18 = (bf16[2048,1024]{1,0:T(8,128)(2,1)S(1)}, bf16[2048,1024]{1,0:T(8,128)(2,1)S(1)}, u32[]{:S(2)}, u32[]{:S(2)}) collective-permute-start(bf16[2048,1024]{1,0:T(8,128)(2,1)S(1)} %copy-done.10), channel_id=1, source_target_pairs={{0,1},{1,0},{2,3},{3,2},{4,5},{5,4},{6,7},{7,6},{8,9},{9,8},{10,11... | collective-permute-start | bytes 12582920 | tf_op jit(solution)/shard_map/ppermute | solution.py:373
  108.2 133.8 %collective-permute-start.21 = (bf16[256,512]{1,0:T(8,128)(2,1)}, bf16[256,512]{1,0:T(8,128)(2,1)S(1)}, u32[]{:S(2)}, u32[]{:S(2)}) collective-permute-start(bf16[256,512]{1,0:T(8,128)(2,1)} %get-tuple-element.199), channel_id=1, source_target_pairs={{0,1},{1,0},{2,3},{3,2},{4,5},{5,4},{6,7},{7,6},{8,9},{9,8},{10,11... | collective-permute-start | bytes 786440 | tf_op jit(solution)/shard_map/ppermute | solution.py:373
  137.4 11.2 %collective-permute-start.19 = (bf16[256,2048]{1,0:T(8,128)(2,1)}, bf16[256,2048]{1,0:T(8,128)(2,1)S(1)}, u32[]{:S(2)}, u32[]{:S(2)}) collective-permute-start(bf16[256,2048]{1,0:T(8,128)(2,1)} %get-tuple-element.140), channel_id=1, source_target_pairs={{0,1},{1,0},{2,3},{3,2},{4,5},{5,4},{6,7},{7,6},{8,9},{9,8},{10,11... | collective-permute-start | bytes 3145736 | tf_op jit(solution)/shard_map/ppermute | solution.py:373
  160.1 26.0 %collective-permute-start.83 = (bf16[8,64,1024]{2,1,0:T(8,128)(2,1)S(1)}, bf16[8,64,1024]{2,1,0:T(8,128)(2,1)S(1)}, u32[]{:S(2)}, u32[]{:S(2)}) collective-permute-start(bf16[8,64,1024]{2,1,0:T(8,128)(2,1)S(1)} %get-tuple-element.64), channel_id=1, source_target_pairs={{0,16},{16,0},{1,17},{17,1},{2,18},{18,2},{3,19},{19,3},{4,20},{20... | collective-permute-start | bytes 3145736 | tf_op jit(solution)/shard_map/ppermute | solution.py:373
  162.0 80.0 %collective-permute-start.22 = (bf16[256,4096]{1,0:T(8,128)(2,1)S(1)}, bf16[256,4096]{1,0:T(8,128)(2,1)S(1)}, u32[]{:S(2)}, u32[]{:S(2)}) collective-permute-start(bf16[256,4096]{1,0:T(8,128)(2,1)S(1)} %bitcast.79), channel_id=1, source_target_pairs={{0,1},{1,0},{2,3},{3,2},{4,5},{5,4},{6,7},{7,6},{8,9},{9,8},{10,11... | collective-permute-start | bytes 6291464 | tf_op jit(solution)/shard_map/ppermute | solution.py:373
  162.3 45.9 %collective-permute-start.91 = (bf16[8,64,1024]{2,1,0:T(8,128)(2,1)S(1)}, bf16[8,64,1024]{2,1,0:T(8,128)(2,1)S(1)}, u32[]{:S(2)}, u32[]{:S(2)}) collective-permute-start(bf16[8,64,1024]{2,1,0:T(8,128)(2,1)S(1)} %get-tuple-element.66), channel_id=1, source_target_pairs={{0,16},{16,0},{1,17},{17,1},{2,18},{18,2},{3,19},{19,3},{4,20},{20... | collective-permute-start | bytes 3145736 | tf_op jit(solution)/shard_map/ppermute | solution.py:373
  186.5 23.0 %collective-permute-start.84 = (bf16[4,64,1024]{2,1,0:T(8,128)(2,1)S(1)}, bf16[4,64,1024]{2,1,0:T(8,128)(2,1)S(1)}, u32[]{:S(2)}, u32[]{:S(2)}) collective-permute-start(bf16[4,64,1024]{2,1,0:T(8,128)(2,1)S(1)} %get-tuple-element.135), channel_id=1, source_target_pairs={{0,2},{2,0},{4,6},{6,4},{8,10},{10,8},{12,14},{14,12},{1,3},{3,1},... | collective-permute-start | bytes 1572872 | tf_op jit(solution)/shard_map/ppermute | solution.py:373
  208.6 13.6 %collective-permute-start.92 = (bf16[4,64,1024]{2,1,0:T(8,128)(2,1)S(1)}, bf16[4,64,1024]{2,1,0:T(8,128)(2,1)S(1)}, u32[]{:S(2)}, u32[]{:S(2)}) collective-permute-start(bf16[4,64,1024]{2,1,0:T(8,128)(2,1)S(1)} %get-tuple-element.133), channel_id=1, source_target_pairs={{0,2},{2,0},{4,6},{6,4},{8,10},{10,8},{12,14},{14,12},{1,3},{3,1},... | collective-permute-start | bytes 1572872 | tf_op jit(solution)/shard_map/ppermute | solution.py:373
  209.7 13.8 %collective-permute-start.85 = (bf16[2,64,1024]{2,1,0:T(8,128)(2,1)S(1)}, bf16[2,64,1024]{2,1,0:T(8,128)(2,1)S(1)}, u32[]{:S(2)}, u32[]{:S(2)}) collective-permute-start(bf16[2,64,1024]{2,1,0:T(8,128)(2,1)S(1)} %get-tuple-element.153), channel_id=1, source_target_pairs={{0,4},{2,6},{4,0},{6,2},{8,12},{10,14},{12,8},{14,10},{1,5},{3,7},... | collective-permute-start | bytes 786440 | tf_op jit(solution)/shard_map/ppermute | solution.py:373
  222.4 9.9 %collective-permute-start.93 = (bf16[2,64,1024]{2,1,0:T(8,128)(2,1)S(1)}, bf16[2,64,1024]{2,1,0:T(8,128)(2,1)S(1)}, u32[]{:S(2)}, u32[]{:S(2)}) collective-permute-start(bf16[2,64,1024]{2,1,0:T(8,128)(2,1)S(1)} %get-tuple-element.151), channel_id=1, source_target_pairs={{0,4},{2,6},{4,0},{6,2},{8,12},{10,14},{12,8},{14,10},{1,5},{3,7},... | collective-permute-start | bytes 786440 | tf_op jit(solution)/shard_map/ppermute | solution.py:373
  232.3 9.5 %collective-permute-start.94 = (bf16[1,64,1024]{2,1,0:T(8,128)(2,1)S(1)}, bf16[1,64,1024]{2,1,0:T(8,128)(2,1)S(1)}, u32[]{:S(2)}, u32[]{:S(2)}) collective-permute-start(bf16[1,64,1024]{2,1,0:T(8,128)(2,1)S(1)} %add_convert_fusion.25), channel_id=1, source_target_pairs={{0,8},{2,10},{4,12},{6,14},{8,0},{10,2},{12,4},{14,6},{1,9},{3,11}... | collective-permute-start | bytes 393224 | tf_op jit(solution)/shard_map/ppermute | solution.py:373
  232.7 24.1 %collective-permute-start.87 = (bf16[1,64,1024]{2,1,0:T(8,128)(2,1)S(1)}, bf16[1,64,1024]{2,1,0:T(8,128)(2,1)S(1)}, u32[]{:S(2)}, u32[]{:S(2)}) collective-permute-start(bf16[1,64,1024]{2,1,0:T(8,128)(2,1)S(1)} %add_convert_fusion.27), channel_id=1, source_target_pairs={{0,8},{2,10},{4,12},{6,14},{8,0},{10,2},{12,4},{14,6},{1,9},{3,11}... | collective-permute-start | bytes 393224 | tf_op jit(solution)/shard_map/ppermute | solution.py:373
  241.9 17.3 %collective-permute-start.95 = (bf16[1,64,1024]{2,1,0:T(8,128)(2,1)S(1)}, bf16[1,64,1024]{2,1,0:T(8,128)(2,1)S(1)}, u32[]{:S(2)}, u32[]{:S(2)}) collective-permute-start(bf16[1,64,1024]{2,1,0:T(8,128)(2,1)S(1)} %add_convert_fusion.24), channel_id=1, source_target_pairs={{0,8},{2,10},{4,12},{6,14},{8,0},{10,2},{12,4},{14,6},{1,9},{3,11}... | collective-permute-start | bytes 393224 | tf_op jit(solution)/shard_map/ppermute | solution.py:373
  251.8 9.9 %collective-permute-start.23 = (bf16[2,128,128]{2,1,0:T(8,128)(2,1)S(1)}, bf16[2,128,128]{2,1,0:T(8,128)(2,1)S(1)}, u32[]{:S(2)}, u32[]{:S(2)}) collective-permute-start(bf16[2,128,128]{2,1,0:T(8,128)(2,1)S(1)} %get-tuple-element.209), channel_id=1, source_target_pairs={{0,2},{2,0},{4,6},{6,4},{8,10},{10,8},{12,14},{14,12},{1,3},{3,1},... | collective-permute-start | bytes 196616 | tf_op jit(solution)/shard_map/ppermute | solution.py:373
  253.4 10.5 %collective-permute-start.24 = (bf16[2,128,128]{2,1,0:T(8,128)(2,1)S(1)}, bf16[2,128,128]{2,1,0:T(8,128)(2,1)S(1)}, u32[]{:S(2)}, u32[]{:S(2)}) collective-permute-start(bf16[2,128,128]{2,1,0:T(8,128)(2,1)S(1)} %get-tuple-element.213), channel_id=1, source_target_pairs={{0,4},{2,6},{4,0},{6,2},{8,12},{10,14},{12,8},{14,10},{1,5},{3,7},... | collective-permute-start | bytes 196616 | tf_op jit(solution)/shard_map/ppermute | solution.py:373
  255.7 10.9 %collective-permute-start.25 = (bf16[2,128,128]{2,1,0:T(8,128)(2,1)S(1)}, bf16[2,128,128]{2,1,0:T(8,128)(2,1)S(1)}, u32[]{:S(2)}, u32[]{:S(2)}) collective-permute-start(bf16[2,128,128]{2,1,0:T(8,128)(2,1)S(1)} %get-tuple-element.210), channel_id=1, source_target_pairs={{0,6},{2,4},{4,2},{6,0},{8,14},{10,12},{12,10},{14,8},{1,7},{3,5},... | collective-permute-start | bytes 196616 | tf_op jit(solution)/shard_map/ppermute | solution.py:373
  256.8 11.5 %collective-permute-start.26 = (bf16[2,128,128]{2,1,0:T(8,128)(2,1)S(1)}, bf16[2,128,128]{2,1,0:T(8,128)(2,1)S(1)}, u32[]{:S(2)}, u32[]{:S(2)}) collective-permute-start(bf16[2,128,128]{2,1,0:T(8,128)(2,1)S(1)} %get-tuple-element.211), channel_id=1, source_target_pairs={{0,8},{2,10},{4,12},{6,14},{8,0},{10,2},{12,4},{14,6},{1,9},{3,11}... | collective-permute-start | bytes 196616 | tf_op jit(solution)/shard_map/ppermute | solution.py:373
  266.6 44.6 %collective-permute-start.63 = (f32[10240]{0:T(1024)S(1)}, f32[10240]{0:T(1024)S(1)}, u32[]{:S(2)}, u32[]{:S(2)}) collective-permute-start(f32[10240]{0:T(1024)S(1)} %add.311), channel_id=1, source_target_pairs={{0,16},{16,0},{1,17},{17,1},{2,18},{18,2},{3,19},{19,3},{4,20},{20... | collective-permute-start | bytes 122888 | tf_op jit(solution)/shard_map/ppermute | solution.py:373
  306.7 26.0 %collective-permute-start.36 = (bf16[2,128,384]{2,1,0:T(8,128)(2,1)S(1)}, bf16[2,128,384]{2,1,0:T(8,128)(2,1)S(1)}, u32[]{:S(2)}, u32[]{:S(2)}) collective-permute-start(bf16[2,128,384]{2,1,0:T(8,128)(2,1)S(1)} %pad_maximum_fusion.25), channel_id=1, source_target_pairs={{0,2},{2,0},{4,6},{6,4},{8,10},{10,8},{12,14},{14,12},{1,3},{3,1},... | collective-permute-start | bytes 589832 | tf_op jit(solution)/shard_map/ppermute | solution.py:373
  308.2 26.7 %collective-permute-start.35 = (bf16[2,128,384]{2,1,0:T(8,128)(2,1)S(1)}, bf16[2,128,384]{2,1,0:T(8,128)(2,1)S(1)}, u32[]{:S(2)}, u32[]{:S(2)}) collective-permute-start(bf16[2,128,384]{2,1,0:T(8,128)(2,1)S(1)} %pad_maximum_fusion.24), channel_id=1, source_target_pairs={{0,4},{2,6},{4,0},{6,2},{8,12},{10,14},{12,8},{14,10},{1,5},{3,7},... | collective-permute-start | bytes 589832 | tf_op jit(solution)/shard_map/ppermute | solution.py:373
  308.3 29.4 %collective-permute-start.34 = (bf16[2,128,384]{2,1,0:T(8,128)(2,1)S(1)}, bf16[2,128,384]{2,1,0:T(8,128)(2,1)S(1)}, u32[]{:S(2)}, u32[]{:S(2)}) collective-permute-start(bf16[2,128,384]{2,1,0:T(8,128)(2,1)S(1)} %pad_maximum_fusion.23), channel_id=1, source_target_pairs={{0,6},{2,4},{4,2},{6,0},{8,14},{10,12},{12,10},{14,8},{1,7},{3,5},... | collective-permute-start | bytes 589832 | tf_op jit(solution)/shard_map/ppermute | solution.py:373
  310.8 26.9 %collective-permute-start.33 = (bf16[2,128,384]{2,1,0:T(8,128)(2,1)S(1)}, bf16[2,128,384]{2,1,0:T(8,128)(2,1)S(1)}, u32[]{:S(2)}, u32[]{:S(2)}) collective-permute-start(bf16[2,128,384]{2,1,0:T(8,128)(2,1)S(1)} %pad_maximum_fusion.22), channel_id=1, source_target_pairs={{0,8},{2,10},{4,12},{6,14},{8,0},{10,2},{12,4},{14,6},{1,9},{3,11}... | collective-permute-start | bytes 589832 | tf_op jit(solution)/shard_map/ppermute | solution.py:373
  321.0 11.1 %collective-permute-start.66 = (f32[10240]{0:T(1024)S(1)}, f32[10240]{0:T(1024)S(1)}, u32[]{:S(2)}, u32[]{:S(2)}) collective-permute-start(f32[10240]{0:T(1024)S(1)} %add.314), channel_id=1, source_target_pairs={{0,8},{2,10},{4,12},{6,14},{8,0},{10,2},{12,4},{14,6},{1,9},{3,11}... | collective-permute-start | bytes 122888 | tf_op jit(solution)/shard_map/ppermute | solution.py:373
  332.1 14.8 %collective-permute-start.32 = (bf16[2,128,384]{2,1,0:T(8,128)(2,1)S(1)}, bf16[2,128,384]{2,1,0:T(8,128)(2,1)S(1)}, u32[]{:S(2)}, u32[]{:S(2)}) collective-permute-start(bf16[2,128,384]{2,1,0:T(8,128)(2,1)S(1)} %pad_maximum_fusion.21), channel_id=1, source_target_pairs={{0,10},{2,8},{4,14},{6,12},{8,2},{10,0},{12,6},{14,4},{1,11},{3,9}... | collective-permute-start | bytes 589832 | tf_op jit(solution)/shard_map/ppermute | solution.py:373
  332.7 15.1 %collective-permute-start.31 = (bf16[2,128,384]{2,1,0:T(8,128)(2,1)S(1)}, bf16[2,128,384]{2,1,0:T(8,128)(2,1)S(1)}, u32[]{:S(2)}, u32[]{:S(2)}) collective-permute-start(bf16[2,128,384]{2,1,0:T(8,128)(2,1)S(1)} %pad_maximum_fusion.20), channel_id=1, source_target_pairs={{0,12},{2,14},{4,8},{6,10},{8,4},{10,6},{12,0},{14,2},{1,13},{3,15... | collective-permute-start | bytes 589832 | tf_op jit(solution)/shard_map/ppermute | solution.py:373
  334.9 14.2 %collective-permute-start.30 = (bf16[2,128,384]{2,1,0:T(8,128)(2,1)S(1)}, bf16[2,128,384]{2,1,0:T(8,128)(2,1)S(1)}, u32[]{:S(2)}, u32[]{:S(2)}) collective-permute-start(bf16[2,128,384]{2,1,0:T(8,128)(2,1)S(1)} %pad_maximum_fusion.19), channel_id=1, source_target_pairs={{0,14},{2,12},{4,10},{6,8},{8,6},{10,4},{12,2},{14,0},{1,15},{3,13... | collective-permute-start | bytes 589832 | tf_op jit(solution)/shard_map/ppermute | solution.py:373
  337.7 15.0 %collective-permute-start.52 = (bf16[256,512]{1,0:T(8,128)(2,1)S(1)}, bf16[256,512]{1,0:T(8,128)(2,1)S(1)}, u32[]{:S(2)}, u32[]{:S(2)}) collective-permute-start(bf16[256,512]{1,0:T(8,128)(2,1)S(1)} %copy-done.27), channel_id=1, source_target_pairs={{0,1},{1,0},{2,3},{3,2},{4,5},{5,4},{6,7},{7,6},{8,9},{9,8},{10,11... | collective-permute-start | bytes 786440 | tf_op jit(solution)/shard_map/ppermute | solution.py:373
  337.7 24.1 %collective-permute-start.53 = (bf16[256,1024]{1,0:T(8,128)(2,1)S(1)}, bf16[256,1024]{1,0:T(8,128)(2,1)S(1)}, u32[]{:S(2)}, u32[]{:S(2)}) collective-permute-start(bf16[256,1024]{1,0:T(8,128)(2,1)S(1)} %bitcast.82), channel_id=1, source_target_pairs={{0,1},{1,0},{2,3},{3,2},{4,5},{5,4},{6,7},{7,6},{8,9},{9,8},{10,11... | collective-permute-start | bytes 1572872 | tf_op jit(solution)/shard_map/ppermute | solution.py:373
  346.8 53.8 %collective-permute-start.67 = (bf16[8,512,128]{2,1,0:T(8,128)(2,1)S(1)}, bf16[8,512,128]{2,1,0:T(8,128)(2,1)S(1)}, u32[]{:S(2)}, u32[]{:S(2)}) collective-permute-start(bf16[8,512,128]{2,1,0:T(8,128)(2,1)S(1)} %get-tuple-element.60), channel_id=1, source_target_pairs={{0,2},{2,0},{4,6},{6,4},{8,10},{10,8},{12,14},{14,12},{1,3},{3,1},... | collective-permute-start | bytes 3145736 | tf_op jit(solution)/shard_map/ppermute | solution.py:373
  347.8 12.9 %collective-permute-start.88 = (bf16[2,64,1024]{2,1,0:T(8,128)(2,1)S(1)}, bf16[2,64,1024]{2,1,0:T(8,128)(2,1)S(1)}, u32[]{:S(2)}, u32[]{:S(2)}) collective-permute-start(bf16[2,64,1024]{2,1,0:T(8,128)(2,1)S(1)} %copy-done.29), channel_id=1, source_target_pairs={{0,4},{2,6},{4,0},{6,2},{8,12},{10,14},{12,8},{14,10},{1,5},{3,7},... | collective-permute-start | bytes 786440 | tf_op jit(solution)/shard_map/ppermute | solution.py:373
  352.7 50.7 %collective-permute-start.75 = (bf16[8,512,128]{2,1,0:T(8,128)(2,1)S(1)}, bf16[8,512,128]{2,1,0:T(8,128)(2,1)S(1)}, u32[]{:S(2)}, u32[]{:S(2)}) collective-permute-start(bf16[8,512,128]{2,1,0:T(8,128)(2,1)S(1)} %get-tuple-element.62), channel_id=1, source_target_pairs={{0,2},{2,0},{4,6},{6,4},{8,10},{10,8},{12,14},{14,12},{1,3},{3,1},... | collective-permute-start | bytes 3145736 | tf_op jit(solution)/shard_map/ppermute | solution.py:373
  360.7 38.9 %collective-permute-start.39 = (bf16[1,3,256,128]{3,2,1,0:T(8,128)(2,1)S(1)}, bf16[1,3,256,128]{3,2,1,0:T(8,128)(2,1)S(1)}, u32[]{:S(2)}, u32[]{:S(2)}) collective-permute-start(bf16[1,3,256,128]{3,2,1,0:T(8,128)(2,1)S(1)} %fusion.37), channel_id=1, source_target_pairs={{0,2},{2,0},{4,6},{6,4},{8,10},{10,8},{12,14},{14,12},{1,3},{3,1},... | collective-permute-start | bytes 589832 | tf_op jit(solution)/shard_map/ppermute | solution.py:373
  361.8 121.2 %collective-permute-start.89 = (bf16[4,64,1024]{2,1,0:T(8,128)(2,1)S(1)}, bf16[4,64,1024]{2,1,0:T(8,128)(2,1)S(1)}, u32[]{:S(2)}, u32[]{:S(2)}) collective-permute-start(bf16[4,64,1024]{2,1,0:T(8,128)(2,1)S(1)} %pad_maximum_fusion.11), channel_id=1, source_target_pairs={{0,2},{2,0},{4,6},{6,4},{8,10},{10,8},{12,14},{14,12},{1,3},{3,1},... | collective-permute-start | bytes 1572872 | tf_op jit(solution)/shard_map/ppermute | solution.py:373
  366.4 35.2 %collective-permute-start.54 = (bf16[8,32,1024]{2,1,0:T(8,128)(2,1)S(1)}, bf16[8,32,1024]{2,1,0:T(8,128)(2,1)S(1)}, u32[]{:S(2)}, u32[]{:S(2)}) collective-permute-start(bf16[8,32,1024]{2,1,0:T(8,128)(2,1)S(1)} %get-tuple-element.58), channel_id=1, source_target_pairs={{0,4},{2,6},{4,0},{6,2},{8,12},{10,14},{12,8},{14,10},{1,5},{3,7},... | collective-permute-start | bytes 1572872 | tf_op jit(solution)/shard_map/ppermute | solution.py:373
  399.6 71.9 %collective-permute-start.97 = (bf16[4,64,1024]{2,1,0:T(8,128)(2,1)S(1)}, bf16[4,64,1024]{2,1,0:T(8,128)(2,1)S(1)}, u32[]{:S(2)}, u32[]{:S(2)}) collective-permute-start(bf16[4,64,1024]{2,1,0:T(8,128)(2,1)S(1)} %pad_maximum_fusion.12), channel_id=1, source_target_pairs={{0,2},{2,0},{4,6},{6,4},{8,10},{10,8},{12,14},{14,12},{1,3},{3,1},... | collective-permute-start | bytes 1572872 | tf_op jit(solution)/shard_map/ppermute | solution.py:373
  400.7 11.7 %collective-permute-start.40 = (bf16[2,3,256,128]{3,2,1,0:T(8,128)(2,1)S(1)}, bf16[2,3,256,128]{3,2,1,0:T(8,128)(2,1)S(1)}, u32[]{:S(2)}, u32[]{:S(2)}) collective-permute-start(bf16[2,3,256,128]{3,2,1,0:T(8,128)(2,1)S(1)} %pad_maximum_fusion.13), channel_id=1, source_target_pairs={{0,4},{2,6},{4,0},{6,2},{8,12},{10,14},{12,8},{14,10},{1,5},{3,7},... | collective-permute-start | bytes 1179656 | tf_op jit(solution)/shard_map/ppermute | solution.py:373
  401.7 20.9 %collective-permute-start.68 = (bf16[4,512,128]{2,1,0:T(8,128)(2,1)S(1)}, bf16[4,512,128]{2,1,0:T(8,128)(2,1)S(1)}, u32[]{:S(2)}, u32[]{:S(2)}) collective-permute-start(bf16[4,512,128]{2,1,0:T(8,128)(2,1)S(1)} %get-tuple-element.139), channel_id=1, source_target_pairs={{0,16},{16,0},{1,17},{17,1},{2,18},{18,2},{3,19},{19,3},{4,20},{20... | collective-permute-start | bytes 1572872 | tf_op jit(solution)/shard_map/ppermute | solution.py:373
  403.4 19.1 %collective-permute-start.55 = (bf16[4,32,1024]{2,1,0:T(8,128)(2,1)S(1)}, bf16[4,32,1024]{2,1,0:T(8,128)(2,1)S(1)}, u32[]{:S(2)}, u32[]{:S(2)}) collective-permute-start(bf16[4,32,1024]{2,1,0:T(8,128)(2,1)S(1)} %get-tuple-element.159), channel_id=1, source_target_pairs={{0,8},{2,10},{4,12},{6,14},{8,0},{10,2},{12,4},{14,6},{1,9},{3,11}... | collective-permute-start | bytes 786440 | tf_op jit(solution)/shard_map/ppermute | solution.py:373
  412.4 11.9 %collective-permute-start.76 = (bf16[4,512,128]{2,1,0:T(8,128)(2,1)S(1)}, bf16[4,512,128]{2,1,0:T(8,128)(2,1)S(1)}, u32[]{:S(2)}, u32[]{:S(2)}) collective-permute-start(bf16[4,512,128]{2,1,0:T(8,128)(2,1)S(1)} %get-tuple-element.137), channel_id=1, source_target_pairs={{0,16},{16,0},{1,17},{17,1},{2,18},{18,2},{3,19},{19,3},{4,20},{20... | collective-permute-start | bytes 1572872 | tf_op jit(solution)/shard_map/ppermute | solution.py:373
  422.5 58.9 %collective-permute-start.41 = (bf16[4,3,256,128]{3,2,1,0:T(8,128)(2,1)S(1)}, bf16[4,3,256,128]{3,2,1,0:T(8,128)(2,1)S(1)}, u32[]{:S(2)}, u32[]{:S(2)}) collective-permute-start(bf16[4,3,256,128]{3,2,1,0:T(8,128)(2,1)S(1)} %pad_maximum_fusion.7), channel_id=1, source_target_pairs={{0,8},{2,10},{4,12},{6,14},{8,0},{10,2},{12,4},{14,6},{1,9},{3,11}... | collective-permute-start | bytes 2359304 | tf_op jit(solution)/shard_map/ppermute | solution.py:373
  424.3 12.0 %collective-permute-start.69 = (bf16[2,512,128]{2,1,0:T(8,128)(2,1)S(1)}, bf16[2,512,128]{2,1,0:T(8,128)(2,1)S(1)}, u32[]{:S(2)}, u32[]{:S(2)}) collective-permute-start(bf16[2,512,128]{2,1,0:T(8,128)(2,1)S(1)} %get-tuple-element.157), channel_id=1, source_target_pairs={{0,4},{2,6},{4,0},{6,2},{8,12},{10,14},{12,8},{14,10},{1,5},{3,7},... | collective-permute-start | bytes 786440 | tf_op jit(solution)/shard_map/ppermute | solution.py:373
  427.6 11.5 %collective-permute-start.77 = (bf16[2,512,128]{2,1,0:T(8,128)(2,1)S(1)}, bf16[2,512,128]{2,1,0:T(8,128)(2,1)S(1)}, u32[]{:S(2)}, u32[]{:S(2)}) collective-permute-start(bf16[2,512,128]{2,1,0:T(8,128)(2,1)S(1)} %get-tuple-element.155), channel_id=1, source_target_pairs={{0,4},{2,6},{4,0},{6,2},{8,12},{10,14},{12,8},{14,10},{1,5},{3,7},... | collective-permute-start | bytes 786440 | tf_op jit(solution)/shard_map/ppermute | solution.py:373
  436.3 25.8 %collective-permute-start.57 = (bf16[1,32,1024]{2,1,0:T(8,128)(2,1)S(1)}, bf16[1,32,1024]{2,1,0:T(8,128)(2,1)S(1)}, u32[]{:S(2)}, u32[]{:S(2)}) collective-permute-start(bf16[1,32,1024]{2,1,0:T(8,128)(2,1)S(1)} %add_convert_fusion.39), channel_id=1, source_target_pairs={{0,16},{16,0},{1,17},{17,1},{2,18},{18,2},{3,19},{19,3},{4,20},{20... | collective-permute-start | bytes 196616 | tf_op jit(solution)/shard_map/ppermute | solution.py:373
  439.1 16.3 %collective-permute-start.70 = (bf16[1,512,128]{2,1,0:T(8,128)(2,1)S(1)}, bf16[1,512,128]{2,1,0:T(8,128)(2,1)S(1)}, u32[]{:S(2)}, u32[]{:S(2)}) collective-permute-start(bf16[1,512,128]{2,1,0:T(8,128)(2,1)S(1)} %add_convert_fusion.34), channel_id=1, source_target_pairs={{0,8},{2,10},{4,12},{6,14},{8,0},{10,2},{12,4},{14,6},{1,9},{3,11}... | collective-permute-start | bytes 393224 | tf_op jit(solution)/shard_map/ppermute | solution.py:373
  475.1 50.9 %collective-permute-start.98 = (bf16[8,64,1024]{2,1,0:T(8,128)(2,1)S(1)}, bf16[8,64,1024]{2,1,0:T(8,128)(2,1)S(1)}, u32[]{:S(2)}, u32[]{:S(2)}) collective-permute-start(bf16[8,64,1024]{2,1,0:T(8,128)(2,1)S(1)} %pad_maximum_fusion.6.chunks_ref), channel_id=1, source_target_pairs={{0,16},{16,0},{1,17},{17,1},{2,18},{18,2},{3,19},{19,3},{4,20},{20... | collective-permute-start | bytes 3145736 | tf_op jit(solution)/shard_map/ppermute | solution.py:373
  480.6 31.8 %collective-permute-start.73 = (bf16[4,512,128]{2,1,0:T(8,128)(2,1)S(1)}, bf16[4,512,128]{2,1,0:T(8,128)(2,1)S(1)}, u32[]{:S(2)}, u32[]{:S(2)}) collective-permute-start(bf16[4,512,128]{2,1,0:T(8,128)(2,1)S(1)} %pad_maximum_fusion.9), channel_id=1, source_target_pairs={{0,16},{16,0},{1,17},{17,1},{2,18},{18,2},{3,19},{19,3},{4,20},{20... | collective-permute-start | bytes 1572872 | tf_op jit(solution)/shard_map/ppermute | solution.py:373
  481.4 42.2 %collective-permute-start.81 = (bf16[4,512,128]{2,1,0:T(8,128)(2,1)S(1)}, bf16[4,512,128]{2,1,0:T(8,128)(2,1)S(1)}, u32[]{:S(2)}, u32[]{:S(2)}) collective-permute-start(bf16[4,512,128]{2,1,0:T(8,128)(2,1)S(1)} %pad_maximum_fusion.10), channel_id=1, source_target_pairs={{0,16},{16,0},{1,17},{17,1},{2,18},{18,2},{3,19},{19,3},{4,20},{20... | collective-permute-start | bytes 1572872 | tf_op jit(solution)/shard_map/ppermute | solution.py:373
  483.0 87.7 %collective-permute-start.42 = (bf16[8,3,256,128]{3,2,1,0:T(8,128)(2,1)S(1)}, bf16[8,3,256,128]{3,2,1,0:T(8,128)(2,1)S(1)}, u32[]{:S(2)}, u32[]{:S(2)}) collective-permute-start(bf16[8,3,256,128]{3,2,1,0:T(8,128)(2,1)S(1)} %pad_maximum_fusion.2.chunks_ref), channel_id=1, source_target_pairs={{0,16},{16,0},{1,17},{17,1},{2,18},{18,2},{3,19},{19,3},{4,20},{20... | collective-permute-start | bytes 4718600 | tf_op jit(solution)/shard_map/ppermute | solution.py:373
  483.9 79.7 %collective-permute-start.90 = (bf16[8,64,1024]{2,1,0:T(8,128)(2,1)S(1)}, bf16[8,64,1024]{2,1,0:T(8,128)(2,1)S(1)}, u32[]{:S(2)}, u32[]{:S(2)}) collective-permute-start(bf16[8,64,1024]{2,1,0:T(8,128)(2,1)S(1)} %pad_maximum_fusion.5.chunks_ref), channel_id=1, source_target_pairs={{0,16},{16,0},{1,17},{17,1},{2,18},{18,2},{3,19},{19,3},{4,20},{20... | collective-permute-start | bytes 3145736 | tf_op jit(solution)/shard_map/ppermute | solution.py:373
  512.4 11.4 %collective-permute-start.60 = (bf16[4,32,1024]{2,1,0:T(8,128)(2,1)S(1)}, bf16[4,32,1024]{2,1,0:T(8,128)(2,1)S(1)}, u32[]{:S(2)}, u32[]{:S(2)}) collective-permute-start(bf16[4,32,1024]{2,1,0:T(8,128)(2,1)S(1)} %pad_maximum_fusion.14), channel_id=1, source_target_pairs={{0,8},{2,10},{4,12},{6,14},{8,0},{10,2},{12,4},{14,6},{1,9},{3,11}... | collective-permute-start | bytes 786440 | tf_op jit(solution)/shard_map/ppermute | solution.py:373
  523.7 52.2 %collective-permute-start.74 = (bf16[8,512,128]{2,1,0:T(8,128)(2,1)S(1)}, bf16[8,512,128]{2,1,0:T(8,128)(2,1)S(1)}, u32[]{:S(2)}, u32[]{:S(2)}) collective-permute-start(bf16[8,512,128]{2,1,0:T(8,128)(2,1)S(1)} %pad_maximum_fusion.3.chunks_ref), channel_id=1, source_target_pairs={{0,2},{2,0},{4,6},{6,4},{8,10},{10,8},{12,14},{14,12},{1,3},{3,1},... | collective-permute-start | bytes 3145736 | tf_op jit(solution)/shard_map/ppermute | solution.py:373
  523.8 49.2 %collective-permute-start.82 = (bf16[8,512,128]{2,1,0:T(8,128)(2,1)S(1)}, bf16[8,512,128]{2,1,0:T(8,128)(2,1)S(1)}, u32[]{:S(2)}, u32[]{:S(2)}) collective-permute-start(bf16[8,512,128]{2,1,0:T(8,128)(2,1)S(1)} %pad_maximum_fusion.4.chunks_ref), channel_id=1, source_target_pairs={{0,2},{2,0},{4,6},{6,4},{8,10},{10,8},{12,14},{14,12},{1,3},{3,1},... | collective-permute-start | bytes 3145736 | tf_op jit(solution)/shard_map/ppermute | solution.py:373
  526.0 42.3 %collective-permute-start.61 = (bf16[8,32,1024]{2,1,0:T(8,128)(2,1)S(1)}, bf16[8,32,1024]{2,1,0:T(8,128)(2,1)S(1)}, u32[]{:S(2)}, u32[]{:S(2)}) collective-permute-start(bf16[8,32,1024]{2,1,0:T(8,128)(2,1)S(1)} %pad_maximum_fusion.8.chunks_ref), channel_id=1, source_target_pairs={{0,4},{2,6},{4,0},{6,2},{8,12},{10,14},{12,8},{14,10},{1,5},{3,7},... | collective-permute-start | bytes 1572872 | tf_op jit(solution)/shard_map/ppermute | solution.py:373
  (67 other events, 752.0 us)

commit v3 on v2

--- a/solution.py
+++ b/solution.py
@@ -627,20 +627,61 @@
     return lowered(widened(first) + widened(second))
 
 
-def sum_to_owner(keep, send, order):
-    for step, (axis, bit) in enumerate(order):
-        arrived = exchange(send, axis, bit)
-        half = keep.shape[0] // 2
-        if step == len(order) - 1:
-            return added(keep, arrived)
-        send = added(keep[half:], arrived[half:])
-        keep = added(keep[:half], arrived[:half])
-
-
-def spread(owned, order):
-    for axis, bit in reversed(order[1:]):
-        owned = jnp.concatenate([owned, exchange(owned, axis, bit)], axis=0)
-    return owned, exchange(owned, order[0][0], order[0][1])
+LINKS = {"x": ("dp", 1), "y": ("ctx", 1), "p": ("ctx", 2), "r": ("ctx", 4)}
+ORDERS = {"b0": "xpyr", "b1": "ryxp", "i0": "yxrp", "i1": "pyxr", "o": "yxpr", "q": "xypr", "v": "rpyx"}
+EVENTS = (
+    "b0", "A", "q", "i0", "b1", "i1", "v", "o", "q", "b0", "v", "i0", "b1", "v",
+    "o", "q", "i1", "b1", "o", "b0", "i0", "v", "i1", "q", "b1", "o", "v", "b0",
+    "i0", "i1", "b1", "T", "o", "b0", "i0", "q", "i1", "b1", "K", "b0", "o", "q",
+    "i1", "b1", "i0", "o", "b0", "i1", "i0", "o", "b0", "i0", "b1", "i1",
+)
+
+
+def hops(name):
+    return [LINKS[letter] for letter in ORDERS[name]]
+
+
+class Line:
+    def __init__(self):
+        self.last = None
+
+    def after(self, values):
+        if self.last is None:
+            return values
+        values, self.last.value = lax.optimization_barrier((values, self.last.value))
+        return values
+
+    def done(self, holder):
+        self.last = holder
+
+
+class Reduction:
+    def __init__(self, line, name, keep, send, put):
+        self.line, self.order, self.put = line, hops(name), put
+        self.value, self.step = keep, 0
+        self.arrived = exchange(send, *self.order[0])
+
+    def advance(self):
+        last = len(self.order) - 1
+        step = self.step
+        self.step += 1
+        arrived, value = self.line.after((self.arrived, self.value))
+        if step < last:
+            half = value.shape[0] // 2
+            send = added(value[half:], arrived[half:])
+            self.value = added(value[:half], arrived[:half])
+            self.arrived = exchange(send, *self.order[step + 1])
+        elif step == last:
+            self.value = added(value, arrived)
+            self.arrived = exchange(self.value, *self.order[last])
+        elif step <= 2 * last:
+            self.value = jnp.concatenate([value, arrived], axis=0)
+            self.arrived = exchange(self.value, *self.order[2 * last - step])
+            if step == 2 * last:
+                self.put(self.value, False)
+        else:
+            self.value = self.put(arrived, True)
+        self.line.done(self)
 
 
 def place_kernel(place_ref, chunks_ref, *rest, by_rows):
@@ -686,35 +727,34 @@
     )(*operands)
 
 
-def place_three_kernel(place_ref, chunks_ref, *rest):
+def place_three_kernel(place_ref, chunks_ref, *rest, bits):
     out_ref = rest[-1]
     count, _, _, cols = chunks_ref.shape
-    ctx = place_ref[0] & (count - 1)
+    low = place_ref[0] & (count - 1)
     for j in range(count):
-        out_ref[:, j * cols : (j + 1) * cols] = chunks_ref[j ^ ctx, 0].astype(jnp.float32)
-
-
-def put_three_in_place(place, chunks, far, into, ctx_count, dp_count, name):
+        spot = sum(((j // bit) & 1) << (len(bits) - 1 - k) for k, bit in enumerate(bits))
+        out_ref[:, j * cols : (j + 1) * cols] = chunks_ref[spot ^ low, 0].astype(jnp.float32)
+
+
+def put_three_in_place(place, chunks, far, into, bits, dp_count, name):
     total, three, rows, cols = chunks.shape
+    ctx_count = 1 << len(bits)
     steps = total // ctx_count
     first = steps if far else 0
-    ctx_bits = ctx_count.bit_length() - 1
-    in_specs = [
-        pl.BlockSpec((ctx_count, 1, rows, cols), lambda s, t, p: (s, t, 0, 0))
-    ]
+    in_specs = [pl.BlockSpec((ctx_count, 1, rows, cols), lambda s, t, p: (s, t, 0, 0))]
     operands = [place, chunks]
     if into is not None:
         in_specs.append(pl.BlockSpec(memory_space=pl.ANY))
         operands.append(into)
     return pl.pallas_call(
-        place_three_kernel,
+        partial(place_three_kernel, bits=bits),
         grid_spec=pltpu.PrefetchScalarGridSpec(
             num_scalar_prefetch=1,
             grid=(steps, three),
             in_specs=in_specs,
             out_specs=pl.BlockSpec(
                 (rows, ctx_count * cols),
-                lambda s, t, p: ((s + first) ^ (p[0] >> ctx_bits), t),
+                lambda s, t, p: ((s + first) ^ (p[0] >> len(bits)), t),
             ),
         ),
         out_shape=jax.ShapeDtypeStruct((rows * dp_count, three * ctx_count * cols), jnp.float32),
@@ -722,13 +762,6 @@
         compiler_params=pltpu.CompilerParams(vmem_limit_bytes=48 << 20),
         name=name,
     )(*operands)
-
-
-def sum_everywhere(values, axes):
-    for axis in axes:
-        for bit in bits_below(lax.axis_size(axis)):
-            values = values + exchange(values, axis, bit)
-    return values
 
 
 def on_device(
@@ -829,23 +862,16 @@
         rows = values.reshape(flat, values.shape[2])
         return (rows, exchange(rows, "fsdp", 1))
 
-    ctx_bits = [("ctx", bit) for bit in bits_below(ctx_count)]
-    dp_bits = [("dp", bit) for bit in bits_below(lax.axis_size("dp"))]
-    order_x = dp_bits + ctx_bits
-    order_y = ctx_bits[:1] + dp_bits + ctx_bits[1:]
-    order_z = ctx_bits[1:] + ctx_bits[:1] + dp_bits
-    place_x = place_of(order_x)
-    place_y = place_of(order_y)
-    place_z = place_of(order_z)
-    count = 1 << len(order_x)
+    places = {name: place_of(hops(name)) for name in ORDERS}
+    count = 1 << len(hops("b0"))
 
     active_pair = left_pair(active_low)
     normed_pair = left_pair(normed_low)
     attended_pair = left_pair(attended_low)
     second_pair = right_pair(second_low)
     back_parts = [
-        pair_grad(place_x, active_pair, second_pair, count, part, 2, True, "grad_back")
-        for part in range(2)
+        pair_grad(places[n], active_pair, second_pair, count, part, 2, True, "grad_back")
+        for part, n in enumerate(("b0", "b1"))
     ]
     back_bias_grad = column_sum(second_low)
     active_grad = back_project(second_low, back_full)
@@ -853,98 +879,179 @@
     hidden_low = lowered(gelu_pull(active_grad)[0])
     hidden_low, back_parts = lax.optimization_barrier((hidden_low, back_parts))
     hidden_pair = right_pair(hidden_low)
-    in_parts = [
-        pair_grad(place_y, normed_pair, hidden_pair, count, part, 2, False, "grad_in")
-        for part in range(2)
-    ]
     in_bias_grad = column_sum(hidden_low)
     first_grad = first_grad_res + back_project(hidden_low, in_full)
     summed_grad, gain_one_grad, shift_one_grad = pull_one(first_grad)
     branch_low = lowered(summed_grad)
-    branch_low, in_parts = lax.optimization_barrier((branch_low, in_parts))
-    out_parts = pair_grad(
-        place_z, attended_pair, right_pair(branch_low), count, 0, 1, True, "grad_out"
-    )
+    branch_pair = right_pair(branch_low)
     out_bias_grad = column_sum(branch_low)
     attended_grad = lowered(back_project(branch_low, out_full))
-
-    column_pieces = [attended_grad[..., k * pair : (k + 1) * pair] for k in range(ctx_count)]
-    head_grad = jnp.concatenate(swap_blocks(reorder(column_pieces, ctx)), axis=1)
-    query_grad, key_grad, value_grad = attention_backward(
-        projected, head_grad, head_result, head_logs
-    )
-    head_grads = (query_grad, key_grad, value_grad)
-
+    column_pieces = reorder(
+        [attended_grad[..., k * pair : (k + 1) * pair] for k in range(ctx_count)], ctx
+    )
+    column_pieces, hidden_pair = lax.optimization_barrier((column_pieces, hidden_pair))
+    head_grad_pieces = swap_blocks(column_pieces)
+    in_parts = [
+        pair_grad(places[n], normed_pair, hidden_pair, count, part, 2, False, "grad_in")
+        for part, n in enumerate(("i0", "i1"))
+    ]
+    branch_pair, in_parts = lax.optimization_barrier((branch_pair, in_parts))
+    out_parts = pair_grad(
+        places["o"], attended_pair, branch_pair, count, 0, 1, True, "grad_out"
+    )
+
+    whole = {"back": None, "in": None, "out": None, "qkv": None}
+
+    def placer(target, name, part, parts, by_rows):
+        def put(chunks, far):
+            whole[target] = put_in_place(
+                places[name], chunks, far, whole[target], part, parts, by_rows, "place_" + target
+            )
+            return whole[target]
+
+        return put
+
+    class Placed:
+        def __init__(self, target):
+            self.target = target
+
+        @property
+        def value(self):
+            return whole[self.target]
+
+        @value.setter
+        def value(self, new):
+            whole[self.target] = new
+
+    line = Line()
+    chains = {
+        "b0": Reduction(line, "b0", *back_parts[0], placer("back", "b0", 0, 2, True)),
+        "b1": Reduction(line, "b1", *back_parts[1], placer("back", "b1", 1, 2, True)),
+        "i0": Reduction(line, "i0", *in_parts[0], placer("in", "i0", 0, 2, False)),
+        "i1": Reduction(line, "i1", *in_parts[1], placer("in", "i1", 1, 2, False)),
+        "o": Reduction(line, "o", *out_parts, placer("out", "o", 0, 1, True)),
+    }
+    targets = {"b0": "back", "b1": "back", "i0": "in", "i1": "in", "o": "out"}
+    line.done(chains["o"])
     token_flat = token_rows.reshape(-1, width)
-    qkv_part = jnp.stack(
-        [contract(token_flat, g.reshape(-1, pair), 0, 0) for g in head_grads], axis=0
-    )
-    own_rows = half_of(qkv_part, core, 1)
-    qkv_sum = own_rows + widened(exchange(lowered(half_of(qkv_part, 1 - core, 1)), "fsdp", 1))
-    order_q = dp_bits + ctx_bits
-    dp_index = lax.axis_index("dp")
-    dp_count = lax.axis_size("dp")
-    qkv_chunks = [
-        qkv_sum[:, k * (qkv_sum.shape[1] // dp_count) : (k + 1) * (qkv_sum.shape[1] // dp_count)]
-        for k in range(dp_count)
-    ]
-    qkv_chunks = reorder(qkv_chunks, dp_index)
-    while len(qkv_chunks) > 1:
-        half = len(qkv_chunks) // 2
-        arrived = [exchange(lowered(c), "dp", half) for c in qkv_chunks[half:]]
-        qkv_chunks = [c + widened(a) for c, a in zip(qkv_chunks[:half], arrived)]
-    qkv_owned = lowered(qkv_chunks[0])[None]
-    place_q = place_of(
-        [("dp", bit) for bit in reversed(bits_below(dp_count))]
-        + [("ctx", bit) for bit in reversed(bits_below(ctx_count))]
-    )
-    order_q = [("dp", bit) for bit in reversed(bits_below(dp_count))] + [
-        ("ctx", bit) for bit in reversed(bits_below(ctx_count))
-    ]
-    qkv_near, qkv_far = spread(qkv_owned, order_q)
-    qkv_grad = None
-    for chunks, far in ((qkv_near, False), (qkv_far, True)):
-        qkv_grad = put_three_in_place(
-            place_q, chunks, far, qkv_grad, ctx_count, dp_count, "place_qkv"
-        )
-
-    def finish(parts, order, place, by_rows, name):
-        whole = None
-        for part, (keep, send) in enumerate(parts):
-            near, far = spread(sum_to_owner(keep, send, order), order)
-            whole = put_in_place(place, near, False, whole, part, len(parts), by_rows, name)
-            whole = put_in_place(place, far, True, whole, part, len(parts), by_rows, name)
-        return whole
-
-    back_grad = finish(back_parts, order_x, place_x, True, "place_back")
-    in_grad = finish(in_parts, order_y, place_y, False, "place_in")
-    out_grad = finish([out_parts], order_z, place_z, True, "place_out")
-
-    mixed_pieces = []
-    for part in head_grads:
-        mixed_pieces.append(row_blocks(part))
-    mixed = [jnp.concatenate([m[k] for m in mixed_pieces], axis=-1) for k in range(ctx_count)]
-    mixed = reorder(swap_blocks(mixed), ctx)
-    mixed_grad = jnp.concatenate(
-        [m[..., t * pair : (t + 1) * pair] for t in range(3) for m in mixed], axis=-1
-    )
-    token_grad = summed_grad + back_project(mixed_grad, qkv_full)
+
+    class Attention:
+        def advance(self):
+            head_grad = jnp.concatenate(line.after(head_grad_pieces), axis=1)
+            self.head_grads = attention_backward(projected, head_grad, head_result, head_logs)
+            qkv_part = jnp.stack(
+                [contract(token_flat, g.reshape(-1, pair), 0, 0) for g in self.head_grads], axis=0
+            )
+            self.value = half_of(qkv_part, core, 1)
+            self.other = exchange(lowered(half_of(qkv_part, 1 - core, 1)), "fsdp", 1)
+            chains["v"].begin(self.head_grads)
+            line.done(self)
 
     layer_vectors = (
         in_bias_grad, back_bias_grad, gain_two_grad, shift_two_grad,
         out_bias_grad, gain_one_grad, shift_one_grad,
     )
-    layer_sum = sum_everywhere(jnp.concatenate(layer_vectors), ("fsdp", "dp", "ctx"))
+
+    class Vectors:
+        def begin(self, head_grads):
+            spread_out = []
+            for part in (head_grads[0], head_grads[2]):
+                spread_out.append(
+                    lax.dynamic_update_slice_in_dim(
+                        jnp.zeros((width,), jnp.float32), column_sum(part), ctx * pair, 0
+                    )
+                )
+            self.value = jnp.concatenate(layer_vectors + tuple(spread_out))
+            self.routes = [("fsdp", 1)] + hops("v")
+            self.step = 0
+            self.arrived = exchange(self.value, *self.routes[0])
+
+        def advance(self):
+            arrived, value = line.after((self.arrived, self.value))
+            self.value = value + arrived
+            self.step += 1
+            if self.step < len(self.routes):
+                self.arrived = exchange(self.value, *self.routes[self.step])
+            line.done(self)
+
+    class QueryKeyValue:
+        def __init__(self):
+            self.step = 0
+
+        def advance(self):
+            step = self.step
+            self.step += 1
+            order = hops("q")
+            if step == 0:
+                other, own = line.after((chains["A"].other, chains["A"].value))
+                total = own + widened(other)
+                half = total.shape[1] // 2
+                low, high = total[:, :half], total[:, half:]
+                first = lax.axis_index("dp") == 0
+                self.value = jnp.where(first, low, high)
+                self.arrived = exchange(lowered(jnp.where(first, high, low)), *order[0])
+            elif step == 1:
+                arrived, value = line.after((self.arrived, self.value))
+                self.value = lowered(value + widened(arrived))[None]
+                self.arrived = exchange(self.value, *order[-1])
+            elif step <= len(order):
+                arrived, value = line.after((self.arrived, self.value))
+                self.value = jnp.concatenate([value, arrived], axis=0)
+                self.arrived = exchange(self.value, *order[len(order) - step])
+                if step == len(order):
+                    self.put(self.value, False)
+            else:
+                arrived, value = line.after((self.arrived, self.value))
+                self.value = self.put(arrived, True)
+                line.done(Placed("qkv"))
+                return
+            line.done(self)
+
+        def put(self, chunks, far):
+            bits = [bit for axis, bit in hops("q")[1:]]
+            whole["qkv"] = put_three_in_place(
+                places["q"], chunks, far, whole["qkv"], bits, 2, "place_qkv"
+            )
+            return whole["qkv"]
+
+    class TokenStart:
+        def advance(self):
+            blocks = [row_blocks(part) for part in chains["A"].head_grads]
+            pieces = [jnp.concatenate([m[k] for m in blocks], axis=-1) for k in range(ctx_count)]
+            pieces = line.after(pieces)
+            self.value = pieces[0]
+            self.arrived = swap_blocks(pieces)[1:]
+            line.done(self)
+
+    class TokenEnd:
+        def advance(self):
+            start = chains["T"]
+            arrived, own = line.after((start.arrived, start.value))
+            mixed = reorder([own] + arrived, ctx)
+            mixed_grad = jnp.concatenate(
+                [m[..., t * pair : (t + 1) * pair] for t in range(3) for m in mixed], axis=-1
+            )
+            self.value = summed_grad + back_project(mixed_grad, qkv_full)
+            line.done(self)
+
+    chains.update(A=Attention(), v=Vectors(), q=QueryKeyValue(), T=TokenStart(), K=TokenEnd())
+    for name in EVENTS:
+        chain = chains[name]
+        chain.advance()
+        if name in targets and chain.step == 8:
+            line.done(Placed(targets[name]))
+
     reduced = []
     offset = 0
-    for part in layer_vectors:
-        size = part.shape[0]
-        reduced.append(half_of(layer_sum[offset : offset + size], core, 0))
+    sizes = [part.shape[0] for part in layer_vectors] + [width, width]
+    for size in sizes:
+        reduced.append(half_of(chains["v"].value[offset : offset + size], core, 0))
         offset += size
-    bias_part = jnp.stack([column_sum(query_grad), column_sum(value_grad)])
-    bias_part = sum_everywhere(bias_part, ("fsdp", "dp"))
-    bias_pieces = reorder(gather_blocks(bias_part), ctx)
-    bias_grads = half_of(jnp.concatenate(bias_pieces, axis=1), core, 1)
+    token_grad = chains["K"].value
+    qkv_grad, in_grad, back_grad, out_grad = (
+        whole["qkv"], whole["in"], whole["back"], whole["out"]
+    )
+    bias_grads = reduced[7:]
     return (
         output,
         token_grad,
@@ -966,8 +1073,7 @@
 
 def head_parallel(mesh):
     sizes = [mesh.shape["dp"], mesh.shape["ctx"]]
-    powers = all(size & (size - 1) == 0 for size in sizes)
-    return powers and mesh.shape["fsdp"] == 2 and 2 * mesh.shape["ctx"] == HEADS
+    return sizes == [2, 8] and mesh.shape["fsdp"] == 2 and 2 * sizes[1] == HEADS
 
 
 def solution(mesh):

time: 588 us -> 508 us (0.86)
  waiting for transfers between devices: 303 us -> 185 us
  Pallas kernels: 58 us -> 71.5 us
  other arithmetic: 35.1 us -> 47.6 us
  local copies, waits for them, and re-layouts: 23.2 us -> 29.4 us
    ppermute x99 -> x90, waiting for transfers between devices: 303 us -> 185 us  [exchange(): return lax.ppermute(values, axis, [(i, i ^ bit) for i in range(count)])]
    pallas_call x5, Pallas kernels: 14.2 us -> 28 us  [pair_grad(): pl.pallas_call(partial(grad_kernel, by_rows=by_rows), grid_spec=pltpu.Pre...]
    convert_element_type x25 -> x24, other arithmetic: 13.6 us -> 21.7 us  [lowered(): return values.astype(jnp.bfloat16)]
    ppermute x99 -> x90, starting transfers between devices: 118 us -> 122 us  [exchange(): return lax.ppermute(values, axis, [(i, i ^ bit) for i in range(count)])]
    unnamed x114 -> x163, local copies, waits for them, and re-layouts: 20.6 us -> 24.3 us
  transfers between devices with their start and end apart: 99 -> 90, of which waited for: 43 -> 31; matrix products, arithmetic and copies ran while one was open for 16% -> 22% of each run, Pallas kernels for 10% -> 14%
where the time goes in v3:
time: 508 us; the launch traced here: 499 us
  waiting for transfers between devices  185 us (36%)
  starting transfers between devices  122 us (24%)
  Pallas kernels  71.5 us (14%)
  other arithmetic  47.6 us (9%)
  matrix products  40.9 us (8%)
  local copies, waits for them, and re-layouts  29.4 us (6%)
    ppermute x90, waiting for transfers between devices, exchange(): return lax.ppermute(values, axis, [(i, i ^ bit) for i in range(count)])  185 us
    ppermute x90, starting transfers between devices, exchange(): return lax.ppermute(values, axis, [(i, i ^ bit) for i in range(count)])  122 us
    pallas_call x5, Pallas kernels, pair_grad(): pl.pallas_call(partial(grad_kernel, by_rows=by_rows), grid_spec=pltpu.Pre...  28 us
    unnamed x163, local copies, waits for them, and re-layouts  24.3 us
    convert_element_type x24, other arithmetic, lowered(): return values.astype(jnp.bfloat16)  21.7 us
    dot_general x4, matrix products, back_project(): jnp.einsum('wkb,fb->wkf', gradient_row_block, right_operand_matrix, prefe...  19.3 us
    dot_general x4, matrix products, project(): jnp.einsum('ugj,jn->ugn', left_operand_rows, right_operand_matrix, prefer...  17.7 us
    pallas_call x1, Pallas kernels, attention_backward(): pl.pallas_call(backward_kernel, grid=(seqs, length // rows), in_specs=[wh...  14.1 us
  transfers between devices with their start and end apart: 90, of which 31 were waited for; matrix products, arithmetic and copies ran while one was open for 22% of the time, Pallas kernels for 14%

profile of v3, /device:TPU:0, one launch (start us, length us, event | category | flops | bytes accessed | tf_op | source)
XLA Modules:
  0.0 498.7 jit_solution(17539704778342799584)
XLA Ops:
  1.2 2.6 collective-permute-start
  5.3 2.6 collective-permute-start.3
  15.7 2.0 constant_dynamic-update-slice_fusion.7
  19.9 11.6 %collective-permute-done.3 = bf16[2,128,1024]{2,1,0:T(8,128)(2,1)} collective-permute-done((bf16[2,128,1024]{2,1,0:T(8,128)(2,1)}, bf16[2,128,1024]{2,1,0:T(8,128)(2,1)}, u32[]{:S(2)}, u32[]{:S(2)}) %collective-permute-start.3) | collective-permute-done | bytes 524320 | tf_op jit(solution)/shard_map/ppermute | solution.py:373
  36.2 7.3 %collective-permute-done.5 = bf16[2,128,1024]{2,1,0:T(8,128)(2,1)S(1)} collective-permute-done((bf16[2,128,1024]{2,1,0:T(8,128)(2,1)}, bf16[2,128,1024]{2,1,0:T(8,128)(2,1)S(1)}, u32[]{:S(2)}, u32[]{:S(2)}) %collective-permute-start.5) | collective-permute-done | bytes 524320 | tf_op jit(solution)/shard_map/ppermute | solution.py:373
  49.8 8.5 %collective-permute-done.4 = bf16[2,128,1024]{2,1,0:T(8,128)(2,1)S(1)} collective-permute-done((bf16[2,128,1024]{2,1,0:T(8,128)(2,1)}, bf16[2,128,1024]{2,1,0:T(8,128)(2,1)S(1)}, u32[]{:S(2)}, u32[]{:S(2)}) %collective-permute-start.4) | collective-permute-done | bytes 524320 | tf_op jit(solution)/shard_map/ppermute | solution.py:373
  60.0 7.5 %collective-permute-done.6 = bf16[2,128,1024]{2,1,0:T(8,128)(2,1)S(1)} collective-permute-done((bf16[2,128,1024]{2,1,0:T(8,128)(2,1)S(1)}, bf16[2,128,1024]{2,1,0:T(8,128)(2,1)S(1)}, u32[]{:S(2)}, u32[]{:S(2)}) %collective-permute-start.6) | collective-permute-done | bytes 524320 | tf_op jit(solution)/shard_map/ppermute | solution.py:373
  68.4 2.3 broadcast_select_fusion.4
  75.2 2.4 add_convert_fusion.1.query_ref.key_ref.value_ref
  77.6 11.5 %attention_forward.1 = (f32[2,1024,128]{2,1,0:T(8,128)S(1)}, bf16[2,1024,128]{2,1,0:T(8,128)(2,1)S(1)}, f32[2,1024,128]{2,1,0:T(8,128)S(1)}) custom-call(bf16[2,1024,384]{2,1,0:T(8,128)(2,1)S(1)} %add_convert_fusion.1.query_ref.key_ref.value_ref, bf16[2,1024,384]{2,1,0:T(8,128)(2,1)S(1)} %add_convert_fusion.1.query_ref.key_ref.value_ref, ...), custom_call_target="tpu_custom_call" | custom-call | tf_op jit(solution)/shard_map/attention_forward/pallas_call | solution.py:453
  92.7 2.4 collective-permute-start.11
  95.9 2.9 collective-permute-start.9
  108.9 3.9 broadcast_select_fusion.3
  112.8 8.6 %fusion.28 = (u8[128,4096]{1,0:T(8,128)(4,1)S(1)}, u8[128,4096]{1,0:T(8,128)(4,1)S(1)}, f32[2,128,4096]{2,1,0:T(8,128)}) fusion(f32[4096]{0:T(1024)S(1)} %maximum_convert_fusion, bf16[2,128,1024]{2,1,0:T(8,128)(2,1)S(1)} %fusion.29, bf16[512,4096]{1,0:T(8,128)(2,1)} %get-tuple-element.474, bf16[512,4096]{1,0:T(8,128)(2,1)S(1)} %get-tuple-element.473), kind=kOutput, calls=%fused_computation.86 | convolution fusion | flops 2177892352 | bytes 14172160 | tf_op jit(solution)/shard_map/ugj,jn->ugn/dot_general | solution.py:39
  121.4 11.7 %multiply_convert_fusion = (bf16[2,128,4096]{2,1,0:T(8,128)(2,1)S(1)}, f32[2,128,4096]{2,1,0:T(8,128)}) fusion(f32[2,128,4096]{2,1,0:T(8,128)} %get-tuple-element.614, u8[128,4096]{1,0:T(8,128)(4,1)S(1)} %get-tuple-element.424, u8[128,4096]{1,0:T(8,128)(4,1)S(1)} %get-tuple-element.423), kind=kLoop, calls=%fused_computation.25 | loop fusion | flops 73400320 | bytes 11534336 | tf_op jit(solution)/shard_map/convert_element_type | solution.py:31
  133.1 2.6 broadcast_select_fusion.1
  135.7 5.9 %fusion.56 = (f32[2,128]{1,0:T(2,128)S(1)}, f32[2,128,1024]{2,1,0:T(8,128)S(1)}) fusion(f32[1024]{0:T(1024)S(1)} %maximum_convert_fusion.6, bf16[2,128,4096]{2,1,0:T(8,128)(2,1)S(1)} %get-tuple-element.459, bf16[2048,1024]{1,0:T(8,128)(2,1)} %get-tuple-element.472, bf16[2048,1024]{1,0:T(8,128)(2,1)S(1)} %get-tuple-element.471, ...), kind=kOutput, calls=%fused_computation.367 | convolution fusion | flops 2166095616 | bytes 12598272 | tf_op jit(solution)/shard_map/ugj,jn->ugn/dot_general | solution.py:39
  144.7 9.4 %add_convert_fusion = bf16[2,128,4096]{2,1,0:T(8,128)(2,1)S(1)} fusion(f32[2,128,4096]{2,1,0:T(8,128)} %get-tuple-element.460, bf16[2,128,1024]{2,1,0:T(8,128)(2,1)S(1)} %get-tuple-element.446, bf16[2048,1024]{1,0:T(8,128)(2,1)} %get-tuple-element.472, bf16[2048,1024]{1,0:T(8,128)(2,1)} %copy-done.25, f32[2,128,4096]{2,1,0:T(8,128)} %get-tuple-element.614), kind=kOutput, calls=%fused_computation.24 | convolution fusion | flops 2178940928 | bytes 19398656 | tf_op jit(solution)/shard_map/wkb,fb->wkf/dot_general | solution.py:51
  154.1 3.4 grad_back.2
  157.6 13.4 %grad_back.3 = (bf16[8,64,1024]{2,1,0:T(8,128)(2,1)S(1)}, bf16[8,64,1024]{2,1,0:T(8,128)(2,1)}) custom-call(s32[1]{0:T(128)} %bitcast.7.place_ref, bf16[256,2048]{1,0:T(8,128)(2,1)S(1)} %get-tuple-element.489.left_own, bf16[256,2048]{1,0:T(8,128)(2,1)S(1)} %collective-permute-done.19.left_other, bf16[256,1024]{1,0:T(8,128)(2,1)S(1)} %bitcast.82, ...), custom_call_target="tpu_custom_call" | custom-call | tf_op jit(solution)/shard_map/grad_back/pallas_call | solution.py:602
  172.6 6.4 %multiply_reduce_fusion = (f32[1024]{0:T(1024)S(1)}, f32[2,128]{1,0:T(2,128)S(1)}, f32[1024]{0:T(1024)S(1)}, f32[2,128,1024]{2,1,0:T(8,128)S(1)}) fusion(f32[2,128,1024]{2,1,0:T(8,128)S(1)} %copy-done.16, f32[2,128]{1,0:T(2,128)S(1)} %fusion.38, f32[2,128]{1,0:T(2,128)S(1)} %broadcast_multiply_fusion.1, f32[1024]{0:T(1024)S(1)} %get-tuple-element.618, ...), kind=kOutput, calls=%fused_computation.75 | convolution fusion | flops 2168715008 | bytes 14179328 | tf_op jit(solution)/shard_map/wkb,fb->wkf/dot_general | solution.py:51
  186.0 4.6 grad_in.2
  190.6 3.9 grad_in.3
  195.5 2.7 grad_out.1
  204.1 2.9 collective-permute-start.33
  207.0 2.7 add_convert_fusion.8
  209.7 2.3 collective-permute-start.26
  212.0 19.8 %collective-permute-done.31 = bf16[2,128,128]{2,1,0:T(8,128)(2,1)S(1)} collective-permute-done((bf16[2,128,128]{2,1,0:T(8,128)(2,1)S(1)}, bf16[2,128,128]{2,1,0:T(8,128)(2,1)S(1)}, u32[]{:S(2)}, u32[]{:S(2)}) %collective-permute-start.31) | collective-permute-done | bytes 65568 | tf_op jit(solution)/shard_map/ppermute | solution.py:373
  231.8 2.1 collective-permute-start.36
  234.1 14.1 %attention_backward.1 = (bf16[2,1024,128]{2,1,0:T(8,128)(2,1)S(1)}, bf16[2,1024,128]{2,1,0:T(8,128)(2,1)S(1)}, bf16[2,1024,128]{2,1,0:T(8,128)(2,1)S(1)}) custom-call(bf16[2,1024,384]{2,1,0:T(8,128)(2,1)S(1)} %add_convert_fusion.1.query_ref.key_ref.value_ref, bf16[2,1024,384]{2,1,0:T(8,128)(2,1)S(1)} %add_convert_fusion.1.query_ref.key_ref.value_ref, ...), custom_call_target="tpu_custom_call" | custom-call | tf_op jit(solution)/shard_map/attention_backward/pallas_call | solution.py:532
  261.3 3.5 collective-permute-start.39
  270.8 18.0 %collective-permute-done.39 = bf16[8,512,128]{2,1,0:T(8,128)(2,1)S(1)} collective-permute-done((bf16[8,512,128]{2,1,0:T(8,128)(2,1)}, bf16[8,512,128]{2,1,0:T(8,128)(2,1)S(1)}, u32[]{:S(2)}, u32[]{:S(2)}) %collective-permute-start.39) | collective-permute-done | bytes 1048608 | tf_op jit(solution)/shard_map/ppermute | solution.py:373
  289.2 2.3 collective-permute-start.42
  299.0 7.4 %collective-permute-done.45 = bf16[4,512,128]{2,1,0:T(8,128)(2,1)S(1)} collective-permute-done((bf16[4,512,128]{2,1,0:T(8,128)(2,1)S(1)}, bf16[4,512,128]{2,1,0:T(8,128)(2,1)S(1)}, u32[]{:S(2)}, u32[]{:S(2)}) %collective-permute-start.45) | collective-permute-done | bytes 524320 | tf_op jit(solution)/shard_map/ppermute | solution.py:373
  309.2 4.1 collective-permute-done.44
  315.9 8.3 %collective-permute-done.50 = bf16[4,512,128]{2,1,0:T(8,128)(2,1)S(1)} collective-permute-done((bf16[4,512,128]{2,1,0:T(8,128)(2,1)S(1)}, bf16[4,512,128]{2,1,0:T(8,128)(2,1)S(1)}, u32[]{:S(2)}, u32[]{:S(2)}) %collective-permute-start.50) | collective-permute-done | bytes 524320 | tf_op jit(solution)/shard_map/ppermute | solution.py:373
  324.9 2.2 collective-permute-start.52
  329.1 9.4 %collective-permute-done.52 = bf16[2,512,128]{2,1,0:T(8,128)(2,1)S(1)} collective-permute-done((bf16[2,512,128]{2,1,0:T(8,128)(2,1)S(1)}, bf16[2,512,128]{2,1,0:T(8,128)(2,1)S(1)}, u32[]{:S(2)}, u32[]{:S(2)}) %collective-permute-start.52) | collective-permute-done | bytes 262176 | tf_op jit(solution)/shard_map/ppermute | solution.py:373
  339.6 3.4 collective-permute-start.56
  343.1 2.1 collective-permute-start.60
  345.3 5.1 %collective-permute-done.57 = bf16[1,64,1024]{2,1,0:T(8,128)(2,1)S(1)} collective-permute-done((bf16[1,64,1024]{2,1,0:T(8,128)(2,1)S(1)}, bf16[1,64,1024]{2,1,0:T(8,128)(2,1)S(1)}, u32[]{:S(2)}, u32[]{:S(2)}) %collective-permute-start.57) | collective-permute-done | bytes 131104 | tf_op jit(solution)/shard_map/ppermute | solution.py:373
  350.4 2.3 collective-permute-start.62
  355.4 2.7 collective-permute-start.59
  359.2 2.6 collective-permute-start.74
  364.7 5.5 %collective-permute-done.65 = bf16[1,512,128]{2,1,0:T(8,128)(2,1)S(1)} collective-permute-done((bf16[1,512,128]{2,1,0:T(8,128)(2,1)S(1)}, bf16[1,512,128]{2,1,0:T(8,128)(2,1)S(1)}, u32[]{:S(2)}, u32[]{:S(2)}) %collective-permute-start.65) | collective-permute-done | bytes 131104 | tf_op jit(solution)/shard_map/ppermute | solution.py:373
  370.3 2.3 collective-permute-start.66
  375.7 3.3 collective-permute-start.70
  379.1 3.0 collective-permute-done.66
  382.1 2.1 collective-permute-start.71
  385.8 2.4 collective-permute-start.72
  389.4 11.9 %collective-permute-done.70 = bf16[2,128,384]{2,1,0:T(8,128)(2,1)S(1)} collective-permute-done((bf16[2,128,384]{2,1,0:T(8,128)(2,1)S(1)}, bf16[2,128,384]{2,1,0:T(8,128)(2,1)S(1)}, u32[]{:S(2)}, u32[]{:S(2)}) %collective-permute-start.70) | collective-permute-done | bytes 196640 | tf_op jit(solution)/shard_map/ppermute | solution.py:373
  401.3 4.1 collective-permute-start.76
  406.6 2.8 fusion.16
  409.5 9.4 %collective-permute-start.79 = (bf16[4,64,1024]{2,1,0:T(8,128)(2,1)S(1)}, bf16[4,64,1024]{2,1,0:T(8,128)(2,1)S(1)}, u32[]{:S(2)}, u32[]{:S(2)}) collective-permute-start(bf16[4,64,1024]{2,1,0:T(8,128)(2,1)S(1)} %constant_dynamic-update-slice_fusion.67), channel_id=1, source_target_pairs={{0,4},{2,6},{4,0},{6,2},{8,12},{10,14},{12,8},{14,10},{1,5},{3,7},... | collective-permute-start | bytes 1572872 | tf_op jit(solution)/shard_map/ppermute | solution.py:373
  418.9 2.3 place_qkv.2.rest_0_
  421.2 20.7 %collective-permute-done.77.chunks_ref = bf16[8,3,256,128]{3,2,1,0:T(8,128)(2,1)S(1)} collective-permute-done((bf16[8,3,256,128]{3,2,1,0:T(8,128)(2,1)S(1)}, bf16[8,3,256,128]{3,2,1,0:T(8,128)(2,1)S(1)}, u32[]{:S(2)}, u32[]{:S(2)}) %collective-permute-start.77) | collective-permute-done | bytes 1572896 | tf_op jit(solution)/shard_map/ppermute | solution.py:373
  441.9 2.5 collective-permute-start.80
  444.4 2.3 place_qkv.3
  447.1 2.0 collective-permute-done.80
  449.3 2.1 collective-permute-start.83
  451.3 8.4 %collective-permute-done.86 = bf16[4,512,128]{2,1,0:T(8,128)(2,1)S(1)} collective-permute-done((bf16[4,512,128]{2,1,0:T(8,128)(2,1)S(1)}, bf16[4,512,128]{2,1,0:T(8,128)(2,1)S(1)}, u32[]{:S(2)}, u32[]{:S(2)}) %collective-permute-start.86) | collective-permute-done | bytes 524320 | tf_op jit(solution)/shard_map/ppermute | solution.py:373
  460.1 9.7 %collective-permute-start.88 = (bf16[8,64,1024]{2,1,0:T(8,128)(2,1)S(1)}, bf16[8,64,1024]{2,1,0:T(8,128)(2,1)S(1)}, u32[]{:S(2)}, u32[]{:S(2)}) collective-permute-start(bf16[8,64,1024]{2,1,0:T(8,128)(2,1)S(1)} %constant_dynamic-update-slice_fusion.73.chunks_ref), channel_id=1, source_target_pairs={{0,8},{2,10},{4,12},{6,14},{8,0},{10,2},{12,4},{14,6},{1,9},{3,11}... | collective-permute-start | bytes 3145736 | tf_op jit(solution)/shard_map/ppermute | solution.py:373
  477.2 3.3 collective-permute-done.84.chunks_ref
  485.8 9.6 %collective-permute-done.88.chunks_ref = bf16[8,64,1024]{2,1,0:T(8,128)(2,1)S(1)} collective-permute-done((bf16[8,64,1024]{2,1,0:T(8,128)(2,1)S(1)}, bf16[8,64,1024]{2,1,0:T(8,128)(2,1)S(1)}, u32[]{:S(2)}, u32[]{:S(2)}) %collective-permute-start.88) | collective-permute-done | bytes 1048608 | tf_op jit(solution)/shard_map/ppermute | solution.py:373
  (437 shorter events, 129.0 us)
Async XLA Ops:
  0.6 67.8 %collective-permute-start.7 = (bf16[512,3072]{1,0:T(8,128)(2,1)}, bf16[512,3072]{1,0:T(8,128)(2,1)}, u32[]{:S(2)}, u32[]{:S(2)}) collective-permute-start(bf16[512,3072]{1,0:T(8,128)(2,1)} %param.16), channel_id=1, source_target_pairs={{0,1},{1,0},{2,3},{3,2},{4,5},{5,4},{6,7},{7,6},{8,9},{9,8},{10,11... | collective-permute-start | bytes 9437192 | tf_op jit(solution)/shard_map/ppermute | solution.py:373
  1.2 33.1 %collective-permute-start = (bf16[2,128,1024]{2,1,0:T(8,128)(2,1)}, bf16[2,128,1024]{2,1,0:T(8,128)(2,1)}, u32[]{:S(2)}, u32[]{:S(2)}) collective-permute-start(bf16[2,128,1024]{2,1,0:T(8,128)(2,1)} %param.15), channel_id=1, source_target_pairs={{0,2},{2,0},{4,6},{6,4},{8,10},{10,8},{12,14},{14,12},{1,3},{3,1},... | collective-permute-start | bytes 1572872 | tf_op jit(solution)/shard_map/ppermute | solution.py:373
  3.8 28.2 %collective-permute-start.1 = (bf16[2,128,1024]{2,1,0:T(8,128)(2,1)}, bf16[2,128,1024]{2,1,0:T(8,128)(2,1)}, u32[]{:S(2)}, u32[]{:S(2)}) collective-permute-start(bf16[2,128,1024]{2,1,0:T(8,128)(2,1)} %param.15), channel_id=1, source_target_pairs={{0,4},{2,6},{4,0},{6,2},{8,12},{10,14},{12,8},{14,10},{1,5},{3,7},... | collective-permute-start | bytes 1572872 | tf_op jit(solution)/shard_map/ppermute | solution.py:373
  5.3 26.2 %collective-permute-start.3 = (bf16[2,128,1024]{2,1,0:T(8,128)(2,1)}, bf16[2,128,1024]{2,1,0:T(8,128)(2,1)}, u32[]{:S(2)}, u32[]{:S(2)}) collective-permute-start(bf16[2,128,1024]{2,1,0:T(8,128)(2,1)} %param.15), channel_id=1, source_target_pairs={{0,8},{2,10},{4,12},{6,14},{8,0},{10,2},{12,4},{14,6},{1,9},{3,11}... | collective-permute-start | bytes 1572872 | tf_op jit(solution)/shard_map/ppermute | solution.py:373
  31.6 12.0 %collective-permute-start.5 = (bf16[2,128,1024]{2,1,0:T(8,128)(2,1)}, bf16[2,128,1024]{2,1,0:T(8,128)(2,1)S(1)}, u32[]{:S(2)}, u32[]{:S(2)}) collective-permute-start(bf16[2,128,1024]{2,1,0:T(8,128)(2,1)} %collective-permute-done.3), channel_id=1, source_target_pairs={{0,4},{2,6},{4,0},{6,2},{8,12},{10,14},{12,8},{14,10},{1,5},{3,7},... | collective-permute-start | bytes 1572872 | tf_op jit(solution)/shard_map/ppermute | solution.py:373
  32.0 15.1 %collective-permute-start.2 = (bf16[2,128,1024]{2,1,0:T(8,128)(2,1)}, bf16[2,128,1024]{2,1,0:T(8,128)(2,1)S(1)}, u32[]{:S(2)}, u32[]{:S(2)}) collective-permute-start(bf16[2,128,1024]{2,1,0:T(8,128)(2,1)} %collective-permute-done.1), channel_id=1, source_target_pairs={{0,2},{2,0},{4,6},{6,4},{8,10},{10,8},{12,14},{14,12},{1,3},{3,1},... | collective-permute-start | bytes 1572872 | tf_op jit(solution)/shard_map/ppermute | solution.py:373
  32.7 25.6 %collective-permute-start.4 = (bf16[2,128,1024]{2,1,0:T(8,128)(2,1)}, bf16[2,128,1024]{2,1,0:T(8,128)(2,1)S(1)}, u32[]{:S(2)}, u32[]{:S(2)}) collective-permute-start(bf16[2,128,1024]{2,1,0:T(8,128)(2,1)} %collective-permute-done.3), channel_id=1, source_target_pairs={{0,2},{2,0},{4,6},{6,4},{8,10},{10,8},{12,14},{14,12},{1,3},{3,1},... | collective-permute-start | bytes 1572872 | tf_op jit(solution)/shard_map/ppermute | solution.py:373
  34.3 58.5 %collective-permute-start.16 = (bf16[512,1024]{1,0:T(8,128)(2,1)}, bf16[512,1024]{1,0:T(8,128)(2,1)S(1)}, u32[]{:S(2)}, u32[]{:S(2)}) collective-permute-start(bf16[512,1024]{1,0:T(8,128)(2,1)} %param.19), channel_id=1, source_target_pairs={{0,1},{1,0},{2,3},{3,2},{4,5},{5,4},{6,7},{7,6},{8,9},{9,8},{10,11... | collective-permute-start | bytes 3145736 | tf_op jit(solution)/shard_map/ppermute | solution.py:373
  43.6 24.0 %collective-permute-start.6 = (bf16[2,128,1024]{2,1,0:T(8,128)(2,1)S(1)}, bf16[2,128,1024]{2,1,0:T(8,128)(2,1)S(1)}, u32[]{:S(2)}, u32[]{:S(2)}) collective-permute-start(bf16[2,128,1024]{2,1,0:T(8,128)(2,1)S(1)} %collective-permute-done.5), channel_id=1, source_target_pairs={{0,2},{2,0},{4,6},{6,4},{8,10},{10,8},{12,14},{14,12},{1,3},{3,1},... | collective-permute-start | bytes 1572872 | tf_op jit(solution)/shard_map/ppermute | solution.py:373
  47.1 61.8 %collective-permute-start.17 = (bf16[512,4096]{1,0:T(8,128)(2,1)}, bf16[512,4096]{1,0:T(8,128)(2,1)}, u32[]{:S(2)}, u32[]{:S(2)}) collective-permute-start(bf16[512,4096]{1,0:T(8,128)(2,1)} %param.23), channel_id=1, source_target_pairs={{0,1},{1,0},{2,3},{3,2},{4,5},{5,4},{6,7},{7,6},{8,9},{9,8},{10,11... | collective-permute-start | bytes 12582920 | tf_op jit(solution)/shard_map/ppermute | solution.py:373
  102.2 30.8 %collective-permute-start.18 = (bf16[2048,1024]{1,0:T(8,128)(2,1)S(1)}, bf16[2048,1024]{1,0:T(8,128)(2,1)S(1)}, u32[]{:S(2)}, u32[]{:S(2)}) collective-permute-start(bf16[2048,1024]{1,0:T(8,128)(2,1)S(1)} %copy-done.23), channel_id=1, source_target_pairs={{0,1},{1,0},{2,3},{3,2},{4,5},{5,4},{6,7},{7,6},{8,9},{9,8},{10,11... | collective-permute-start | bytes 12582920 | tf_op jit(solution)/shard_map/ppermute | solution.py:373
  106.3 89.2 %collective-permute-start.22 = (bf16[256,512]{1,0:T(8,128)(2,1)}, bf16[256,512]{1,0:T(8,128)(2,1)S(1)}, u32[]{:S(2)}, u32[]{:S(2)}) collective-permute-start(bf16[256,512]{1,0:T(8,128)(2,1)} %get-tuple-element.555), channel_id=1, source_target_pairs={{0,1},{1,0},{2,3},{3,2},{4,5},{5,4},{6,7},{7,6},{8,9},{9,8},{10,11... | collective-permute-start | bytes 786440 | tf_op jit(solution)/shard_map/ppermute | solution.py:373
  108.4 76.0 %collective-permute-start.24 = (bf16[256,512]{1,0:T(8,128)(2,1)}, bf16[256,512]{1,0:T(8,128)(2,1)S(1)}, u32[]{:S(2)}, u32[]{:S(2)}) collective-permute-start(bf16[256,512]{1,0:T(8,128)(2,1)} %get-tuple-element.553), channel_id=1, source_target_pairs={{0,1},{1,0},{2,3},{3,2},{4,5},{5,4},{6,7},{7,6},{8,9},{9,8},{10,11... | collective-permute-start | bytes 786440 | tf_op jit(solution)/shard_map/ppermute | solution.py:373
  171.0 27.2 %collective-permute-start.21 = (bf16[8,64,1024]{2,1,0:T(8,128)(2,1)}, bf16[8,64,1024]{2,1,0:T(8,128)(2,1)}, u32[]{:S(2)}, u32[]{:S(2)}) collective-permute-start(bf16[8,64,1024]{2,1,0:T(8,128)(2,1)} %get-tuple-element.224), channel_id=1, source_target_pairs={{0,16},{16,0},{1,17},{17,1},{2,18},{18,2},{3,19},{19,3},{4,20},{20... | collective-permute-start | bytes 3145736 | tf_op jit(solution)/shard_map/ppermute | solution.py:373
  180.3 15.2 %collective-permute-start.23 = (bf16[256,1024]{1,0:T(8,128)(2,1)S(1)}, bf16[256,1024]{1,0:T(8,128)(2,1)S(1)}, u32[]{:S(2)}, u32[]{:S(2)}) collective-permute-start(bf16[256,1024]{1,0:T(8,128)(2,1)S(1)} %bitcast.83), channel_id=1, source_target_pairs={{0,1},{1,0},{2,3},{3,2},{4,5},{5,4},{6,7},{7,6},{8,9},{9,8},{10,11... | collective-permute-start | bytes 1572872 | tf_op jit(solution)/shard_map/ppermute | solution.py:373
  183.6 18.8 %collective-permute-start.27 = (bf16[2,128,128]{2,1,0:T(8,128)(2,1)S(1)}, bf16[2,128,128]{2,1,0:T(8,128)(2,1)S(1)}, u32[]{:S(2)}, u32[]{:S(2)}) collective-permute-start(bf16[2,128,128]{2,1,0:T(8,128)(2,1)S(1)} %get-tuple-element.239), channel_id=1, source_target_pairs={{0,2},{2,0},{4,6},{6,4},{8,10},{10,8},{12,14},{14,12},{1,3},{3,1},... | collective-permute-start | bytes 196616 | tf_op jit(solution)/shard_map/ppermute | solution.py:373
  184.4 19.7 %collective-permute-start.28 = (bf16[2,128,128]{2,1,0:T(8,128)(2,1)S(1)}, bf16[2,128,128]{2,1,0:T(8,128)(2,1)S(1)}, u32[]{:S(2)}, u32[]{:S(2)}) collective-permute-start(bf16[2,128,128]{2,1,0:T(8,128)(2,1)S(1)} %get-tuple-element.240), channel_id=1, source_target_pairs={{0,4},{2,6},{4,0},{6,2},{8,12},{10,14},{12,8},{14,10},{1,5},{3,7},... | collective-permute-start | bytes 196616 | tf_op jit(solution)/shard_map/ppermute | solution.py:373
  200.9 30.9 %collective-permute-start.31 = (bf16[2,128,128]{2,1,0:T(8,128)(2,1)S(1)}, bf16[2,128,128]{2,1,0:T(8,128)(2,1)S(1)}, u32[]{:S(2)}, u32[]{:S(2)}) collective-permute-start(bf16[2,128,128]{2,1,0:T(8,128)(2,1)S(1)} %get-tuple-element.243), channel_id=1, source_target_pairs={{0,10},{2,8},{4,14},{6,12},{8,2},{10,0},{12,6},{14,4},{1,11},{3,9}... | collective-permute-start | bytes 196616 | tf_op jit(solution)/shard_map/ppermute | solution.py:373
  202.4 31.5 %collective-permute-start.32 = (bf16[2,128,128]{2,1,0:T(8,128)(2,1)S(1)}, bf16[2,128,128]{2,1,0:T(8,128)(2,1)S(1)}, u32[]{:S(2)}, u32[]{:S(2)}) collective-permute-start(bf16[2,128,128]{2,1,0:T(8,128)(2,1)S(1)} %get-tuple-element.244), channel_id=1, source_target_pairs={{0,12},{2,14},{4,8},{6,10},{8,4},{10,6},{12,0},{14,2},{1,13},{3,15... | collective-permute-start | bytes 196616 | tf_op jit(solution)/shard_map/ppermute | solution.py:373
  204.1 29.8 %collective-permute-start.33 = (bf16[2,128,128]{2,1,0:T(8,128)(2,1)S(1)}, bf16[2,128,128]{2,1,0:T(8,128)(2,1)S(1)}, u32[]{:S(2)}, u32[]{:S(2)}) collective-permute-start(bf16[2,128,128]{2,1,0:T(8,128)(2,1)S(1)} %get-tuple-element.245), channel_id=1, source_target_pairs={{0,14},{2,12},{4,10},{6,8},{8,6},{10,4},{12,2},{14,0},{1,15},{3,13... | collective-permute-start | bytes 196616 | tf_op jit(solution)/shard_map/ppermute | solution.py:373
  209.7 58.2 %collective-permute-start.40 = (bf16[8,64,1024]{2,1,0:T(8,128)(2,1)}, bf16[8,64,1024]{2,1,0:T(8,128)(2,1)}, u32[]{:S(2)}, u32[]{:S(2)}) collective-permute-start(bf16[8,64,1024]{2,1,0:T(8,128)(2,1)} %get-tuple-element.269), channel_id=1, source_target_pairs={{0,8},{2,10},{4,12},{6,14},{8,0},{10,2},{12,4},{14,6},{1,9},{3,11}... | collective-permute-start | bytes 3145736 | tf_op jit(solution)/shard_map/ppermute | solution.py:373
  209.7 86.2 %collective-permute-start.26 = (bf16[4,64,1024]{2,1,0:T(8,128)(2,1)}, bf16[4,64,1024]{2,1,0:T(8,128)(2,1)}, u32[]{:S(2)}, u32[]{:S(2)}) collective-permute-start(bf16[4,64,1024]{2,1,0:T(8,128)(2,1)} %get-tuple-element.487), channel_id=1, source_target_pairs={{0,4},{2,6},{4,0},{6,2},{8,12},{10,14},{12,8},{14,10},{1,5},{3,7},... | collective-permute-start | bytes 1572872 | tf_op jit(solution)/shard_map/ppermute | solution.py:373
  231.8 34.2 %collective-permute-start.36 = (bf16[8,512,128]{2,1,0:T(8,128)(2,1)}, bf16[8,512,128]{2,1,0:T(8,128)(2,1)}, u32[]{:S(2)}, u32[]{:S(2)}) collective-permute-start(bf16[8,512,128]{2,1,0:T(8,128)(2,1)} %get-tuple-element.262), channel_id=1, source_target_pairs={{0,2},{2,0},{4,6},{6,4},{8,10},{10,8},{12,14},{14,12},{1,3},{3,1},... | collective-permute-start | bytes 3145736 | tf_op jit(solution)/shard_map/ppermute | solution.py:373
  233.9 57.6 %collective-permute-start.37 = (bf16[8,32,1024]{2,1,0:T(8,128)(2,1)}, bf16[8,32,1024]{2,1,0:T(8,128)(2,1)}, u32[]{:S(2)}, u32[]{:S(2)}) collective-permute-start(bf16[8,32,1024]{2,1,0:T(8,128)(2,1)} %get-tuple-element.265), channel_id=1, source_target_pairs={{0,2},{2,0},{4,6},{6,4},{8,10},{10,8},{12,14},{14,12},{1,3},{3,1},... | collective-permute-start | bytes 1572872 | tf_op jit(solution)/shard_map/ppermute | solution.py:373
  261.3 27.6 %collective-permute-start.39 = (bf16[8,512,128]{2,1,0:T(8,128)(2,1)}, bf16[8,512,128]{2,1,0:T(8,128)(2,1)S(1)}, u32[]{:S(2)}, u32[]{:S(2)}) collective-permute-start(bf16[8,512,128]{2,1,0:T(8,128)(2,1)} %copy-done.8), channel_id=1, source_target_pairs={{0,4},{2,6},{4,0},{6,2},{8,12},{10,14},{12,8},{14,10},{1,5},{3,7},... | collective-permute-start | bytes 3145736 | tf_op jit(solution)/shard_map/ppermute | solution.py:373
  266.0 23.1 %collective-permute-start.38 = (f32[12288]{0:T(1024)}, f32[12288]{0:T(1024)S(1)}, u32[]{:S(2)}, u32[]{:S(2)}) collective-permute-start(f32[12288]{0:T(1024)} %constant_dynamic-update-slice_fusion.85), channel_id=1, source_target_pairs={{0,1},{1,0},{2,3},{3,2},{4,5},{5,4},{6,7},{7,6},{8,9},{9,8},{10,11... | collective-permute-start | bytes 147464 | tf_op jit(solution)/shard_map/ppermute | solution.py:373
  267.9 25.9 %collective-permute-start.35 = (bf16[3,256,128]{2,1,0:T(8,128)(2,1)S(1)}, bf16[3,256,128]{2,1,0:T(8,128)(2,1)S(1)}, u32[]{:S(2)}, u32[]{:S(2)}) collective-permute-start(bf16[3,256,128]{2,1,0:T(8,128)(2,1)S(1)} %select_convert_fusion.1), channel_id=1, source_target_pairs={{0,16},{16,0},{1,17},{17,1},{2,18},{18,2},{3,19},{19,3},{4,20},{20... | collective-permute-start | bytes 589832 | tf_op jit(solution)/shard_map/ppermute | solution.py:373
  291.5 14.9 %collective-permute-start.45 = (bf16[4,512,128]{2,1,0:T(8,128)(2,1)S(1)}, bf16[4,512,128]{2,1,0:T(8,128)(2,1)S(1)}, u32[]{:S(2)}, u32[]{:S(2)}) collective-permute-start(bf16[4,512,128]{2,1,0:T(8,128)(2,1)S(1)} %get-tuple-element.484), channel_id=1, source_target_pairs={{0,16},{16,0},{1,17},{17,1},{2,18},{18,2},{3,19},{19,3},{4,20},{20... | collective-permute-start | bytes 1572872 | tf_op jit(solution)/shard_map/ppermute | solution.py:373
  293.8 14.9 %collective-permute-start.46 = (bf16[4,64,1024]{2,1,0:T(8,128)(2,1)S(1)}, bf16[4,64,1024]{2,1,0:T(8,128)(2,1)S(1)}, u32[]{:S(2)}, u32[]{:S(2)}) collective-permute-start(bf16[4,64,1024]{2,1,0:T(8,128)(2,1)S(1)} %get-tuple-element.482), channel_id=1, source_target_pairs={{0,2},{2,0},{4,6},{6,4},{8,10},{10,8},{12,14},{14,12},{1,3},{3,1},... | collective-permute-start | bytes 1572872 | tf_op jit(solution)/shard_map/ppermute | solution.py:373
  294.6 19.7 %collective-permute-start.48 = (bf16[1,3,256,128]{3,2,1,0:T(8,128)(2,1)S(1)}, bf16[1,3,256,128]{3,2,1,0:T(8,128)(2,1)S(1)}, u32[]{:S(2)}, u32[]{:S(2)}) collective-permute-start(bf16[1,3,256,128]{3,2,1,0:T(8,128)(2,1)S(1)} %fusion.37), channel_id=1, source_target_pairs={{0,8},{2,10},{4,12},{6,14},{8,0},{10,2},{12,4},{14,6},{1,9},{3,11}... | collective-permute-start | bytes 589832 | tf_op jit(solution)/shard_map/ppermute | solution.py:373
  297.2 30.9 %collective-permute-start.41 = (bf16[2,64,1024]{2,1,0:T(8,128)(2,1)S(1)}, bf16[2,64,1024]{2,1,0:T(8,128)(2,1)S(1)}, u32[]{:S(2)}, u32[]{:S(2)}) collective-permute-start(bf16[2,64,1024]{2,1,0:T(8,128)(2,1)S(1)} %get-tuple-element.507), channel_id=1, source_target_pairs={{0,2},{2,0},{4,6},{6,4},{8,10},{10,8},{12,14},{14,12},{1,3},{3,1},... | collective-permute-start | bytes 786440 | tf_op jit(solution)/shard_map/ppermute | solution.py:373
  298.1 16.0 %collective-permute-start.43 = (bf16[4,32,1024]{2,1,0:T(8,128)(2,1)S(1)}, bf16[4,32,1024]{2,1,0:T(8,128)(2,1)S(1)}, u32[]{:S(2)}, u32[]{:S(2)}) collective-permute-start(bf16[4,32,1024]{2,1,0:T(8,128)(2,1)S(1)} %get-tuple-element.504), channel_id=1, source_target_pairs={{0,16},{16,0},{1,17},{17,1},{2,18},{18,2},{3,19},{19,3},{4,20},{20... | collective-permute-start | bytes 786440 | tf_op jit(solution)/shard_map/ppermute | solution.py:373
  306.3 17.9 %collective-permute-start.50 = (bf16[4,512,128]{2,1,0:T(8,128)(2,1)S(1)}, bf16[4,512,128]{2,1,0:T(8,128)(2,1)S(1)}, u32[]{:S(2)}, u32[]{:S(2)}) collective-permute-start(bf16[4,512,128]{2,1,0:T(8,128)(2,1)S(1)} %get-tuple-element.480), channel_id=1, source_target_pairs={{0,2},{2,0},{4,6},{6,4},{8,10},{10,8},{12,14},{14,12},{1,3},{3,1},... | collective-permute-start | bytes 1572872 | tf_op jit(solution)/shard_map/ppermute | solution.py:373
  313.3 25.4 %collective-permute-start.53 = (f32[12288]{0:T(1024)S(1)}, f32[12288]{0:T(1024)S(1)}, u32[]{:S(2)}, u32[]{:S(2)}) collective-permute-start(f32[12288]{0:T(1024)S(1)} %add.330), channel_id=1, source_target_pairs={{0,2},{2,0},{4,6},{6,4},{8,10},{10,8},{12,14},{14,12},{1,3},{3,1},... | collective-permute-start | bytes 147464 | tf_op jit(solution)/shard_map/ppermute | solution.py:373
  314.2 12.9 %collective-permute-start.47 = (bf16[2,32,1024]{2,1,0:T(8,128)(2,1)S(1)}, bf16[2,32,1024]{2,1,0:T(8,128)(2,1)S(1)}, u32[]{:S(2)}, u32[]{:S(2)}) collective-permute-start(bf16[2,32,1024]{2,1,0:T(8,128)(2,1)S(1)} %get-tuple-element.547), channel_id=1, source_target_pairs={{0,4},{2,6},{4,0},{6,2},{8,12},{10,14},{12,8},{14,10},{1,5},{3,7},... | collective-permute-start | bytes 393224 | tf_op jit(solution)/shard_map/ppermute | solution.py:373
  324.2 18.9 %collective-permute-start.58 = (bf16[2,3,256,128]{3,2,1,0:T(8,128)(2,1)S(1)}, bf16[2,3,256,128]{3,2,1,0:T(8,128)(2,1)S(1)}, u32[]{:S(2)}, u32[]{:S(2)}) collective-permute-start(bf16[2,3,256,128]{3,2,1,0:T(8,128)(2,1)S(1)} %constant_dynamic-update-slice_fusion.25), channel_id=1, source_target_pairs={{0,4},{2,6},{4,0},{6,2},{8,12},{10,14},{12,8},{14,10},{1,5},{3,7},... | collective-permute-start | bytes 1179656 | tf_op jit(solution)/shard_map/ppermute | solution.py:373
  324.9 13.7 %collective-permute-start.52 = (bf16[2,512,128]{2,1,0:T(8,128)(2,1)S(1)}, bf16[2,512,128]{2,1,0:T(8,128)(2,1)S(1)}, u32[]{:S(2)}, u32[]{:S(2)}) collective-permute-start(bf16[2,512,128]{2,1,0:T(8,128)(2,1)S(1)} %get-tuple-element.500), channel_id=1, source_target_pairs={{0,8},{2,10},{4,12},{6,14},{8,0},{10,2},{12,4},{14,6},{1,9},{3,11}... | collective-permute-start | bytes 786440 | tf_op jit(solution)/shard_map/ppermute | solution.py:373
  327.1 12.4 %collective-permute-start.55 = (bf16[2,512,128]{2,1,0:T(8,128)(2,1)S(1)}, bf16[2,512,128]{2,1,0:T(8,128)(2,1)S(1)}, u32[]{:S(2)}, u32[]{:S(2)}) collective-permute-start(bf16[2,512,128]{2,1,0:T(8,128)(2,1)S(1)} %get-tuple-element.498), channel_id=1, source_target_pairs={{0,16},{16,0},{1,17},{17,1},{2,18},{18,2},{3,19},{19,3},{4,20},{20... | collective-permute-start | bytes 786440 | tf_op jit(solution)/shard_map/ppermute | solution.py:373
  328.1 25.4 %collective-permute-start.51 = (bf16[1,64,1024]{2,1,0:T(8,128)(2,1)S(1)}, bf16[1,64,1024]{2,1,0:T(8,128)(2,1)S(1)}, u32[]{:S(2)}, u32[]{:S(2)}) collective-permute-start(bf16[1,64,1024]{2,1,0:T(8,128)(2,1)S(1)} %get-tuple-element.545), channel_id=1, source_target_pairs={{0,8},{2,10},{4,12},{6,14},{8,0},{10,2},{12,4},{14,6},{1,9},{3,11}... | collective-permute-start | bytes 393224 | tf_op jit(solution)/shard_map/ppermute | solution.py:373
  338.7 14.1 %collective-permute-start.54 = (f32[12288]{0:T(1024)S(1)}, f32[12288]{0:T(1024)S(1)}, u32[]{:S(2)}, u32[]{:S(2)}) collective-permute-start(f32[12288]{0:T(1024)S(1)} %add.342), channel_id=1, source_target_pairs={{0,16},{16,0},{1,17},{17,1},{2,18},{18,2},{3,19},{19,3},{4,20},{20... | collective-permute-start | bytes 147464 | tf_op jit(solution)/shard_map/ppermute | solution.py:373
  343.1 12.3 %collective-permute-start.60 = (bf16[1,512,128]{2,1,0:T(8,128)(2,1)S(1)}, bf16[1,512,128]{2,1,0:T(8,128)(2,1)S(1)}, u32[]{:S(2)}, u32[]{:S(2)}) collective-permute-start(bf16[1,512,128]{2,1,0:T(8,128)(2,1)S(1)} %get-tuple-element.540), channel_id=1, source_target_pairs={{0,4},{2,6},{4,0},{6,2},{8,12},{10,14},{12,8},{14,10},{1,5},{3,7},... | collective-permute-start | bytes 393224 | tf_op jit(solution)/shard_map/ppermute | solution.py:373
  353.6 19.1 %collective-permute-start.75 = (bf16[4,3,256,128]{3,2,1,0:T(8,128)(2,1)S(1)}, bf16[4,3,256,128]{3,2,1,0:T(8,128)(2,1)S(1)}, u32[]{:S(2)}, u32[]{:S(2)}) collective-permute-start(bf16[4,3,256,128]{3,2,1,0:T(8,128)(2,1)S(1)} %constant_dynamic-update-slice_fusion.27), channel_id=1, source_target_pairs={{0,2},{2,0},{4,6},{6,4},{8,10},{10,8},{12,14},{14,12},{1,3},{3,1},... | collective-permute-start | bytes 2359304 | tf_op jit(solution)/shard_map/ppermute | solution.py:373
  358.5 11.8 %collective-permute-start.65 = (bf16[1,512,128]{2,1,0:T(8,128)(2,1)S(1)}, bf16[1,512,128]{2,1,0:T(8,128)(2,1)S(1)}, u32[]{:S(2)}, u32[]{:S(2)}) collective-permute-start(bf16[1,512,128]{2,1,0:T(8,128)(2,1)S(1)} %add_convert_fusion.25), channel_id=1, source_target_pairs={{0,4},{2,6},{4,0},{6,2},{8,12},{10,14},{12,8},{14,10},{1,5},{3,7},... | collective-permute-start | bytes 393224 | tf_op jit(solution)/shard_map/ppermute | solution.py:373
  359.2 15.2 %collective-permute-start.74 = (bf16[1,512,128]{2,1,0:T(8,128)(2,1)S(1)}, bf16[1,512,128]{2,1,0:T(8,128)(2,1)S(1)}, u32[]{:S(2)}, u32[]{:S(2)}) collective-permute-start(bf16[1,512,128]{2,1,0:T(8,128)(2,1)S(1)} %add_convert_fusion.24), channel_id=1, source_target_pairs={{0,8},{2,10},{4,12},{6,14},{8,0},{10,2},{12,4},{14,6},{1,9},{3,11}... | collective-permute-start | bytes 393224 | tf_op jit(solution)/shard_map/ppermute | solution.py:373
  363.3 12.4 %collective-permute-start.73 = (bf16[2,64,1024]{2,1,0:T(8,128)(2,1)S(1)}, bf16[2,64,1024]{2,1,0:T(8,128)(2,1)S(1)}, u32[]{:S(2)}, u32[]{:S(2)}) collective-permute-start(bf16[2,64,1024]{2,1,0:T(8,128)(2,1)S(1)} %constant_dynamic-update-slice_fusion.29), channel_id=1, source_target_pairs={{0,16},{16,0},{1,17},{17,1},{2,18},{18,2},{3,19},{19,3},{4,20},{20... | collective-permute-start | bytes 786440 | tf_op jit(solution)/shard_map/ppermute | solution.py:373
  372.6 13.2 %collective-permute-start.67 = (bf16[2,128,384]{2,1,0:T(8,128)(2,1)S(1)}, bf16[2,128,384]{2,1,0:T(8,128)(2,1)S(1)}, u32[]{:S(2)}, u32[]{:S(2)}) collective-permute-start(bf16[2,128,384]{2,1,0:T(8,128)(2,1)S(1)} %copy-done.40), channel_id=1, source_target_pairs={{0,4},{2,6},{4,0},{6,2},{8,12},{10,14},{12,8},{14,10},{1,5},{3,7},... | collective-permute-start | bytes 589832 | tf_op jit(solution)/shard_map/ppermute | solution.py:373
  372.7 15.8 %collective-permute-start.68 = (bf16[2,128,384]{2,1,0:T(8,128)(2,1)S(1)}, bf16[2,128,384]{2,1,0:T(8,128)(2,1)S(1)}, u32[]{:S(2)}, u32[]{:S(2)}) collective-permute-start(bf16[2,128,384]{2,1,0:T(8,128)(2,1)S(1)} %copy-done.39), channel_id=1, source_target_pairs={{0,6},{2,4},{4,2},{6,0},{8,14},{10,12},{12,10},{14,8},{1,7},{3,5},... | collective-permute-start | bytes 589832 | tf_op jit(solution)/shard_map/ppermute | solution.py:373
  374.5 14.9 %collective-permute-start.69 = (bf16[2,128,384]{2,1,0:T(8,128)(2,1)S(1)}, bf16[2,128,384]{2,1,0:T(8,128)(2,1)S(1)}, u32[]{:S(2)}, u32[]{:S(2)}) collective-permute-start(bf16[2,128,384]{2,1,0:T(8,128)(2,1)S(1)} %copy-done.38), channel_id=1, source_target_pairs={{0,8},{2,10},{4,12},{6,14},{8,0},{10,2},{12,4},{14,6},{1,9},{3,11}... | collective-permute-start | bytes 589832 | tf_op jit(solution)/shard_map/ppermute | solution.py:373
  375.7 25.6 %collective-permute-start.70 = (bf16[2,128,384]{2,1,0:T(8,128)(2,1)S(1)}, bf16[2,128,384]{2,1,0:T(8,128)(2,1)S(1)}, u32[]{:S(2)}, u32[]{:S(2)}) collective-permute-start(bf16[2,128,384]{2,1,0:T(8,128)(2,1)S(1)} %copy-done.37), channel_id=1, source_target_pairs={{0,10},{2,8},{4,14},{6,12},{8,2},{10,0},{12,6},{14,4},{1,11},{3,9}... | collective-permute-start | bytes 589832 | tf_op jit(solution)/shard_map/ppermute | solution.py:373
  382.1 19.3 %collective-permute-start.71 = (bf16[2,128,384]{2,1,0:T(8,128)(2,1)S(1)}, bf16[2,128,384]{2,1,0:T(8,128)(2,1)S(1)}, u32[]{:S(2)}, u32[]{:S(2)}) collective-permute-start(bf16[2,128,384]{2,1,0:T(8,128)(2,1)S(1)} %copy-done.36), channel_id=1, source_target_pairs={{0,12},{2,14},{4,8},{6,10},{8,4},{10,6},{12,0},{14,2},{1,13},{3,15... | collective-permute-start | bytes 589832 | tf_op jit(solution)/shard_map/ppermute | solution.py:373
  385.8 19.6 %collective-permute-start.72 = (bf16[2,128,384]{2,1,0:T(8,128)(2,1)S(1)}, bf16[2,128,384]{2,1,0:T(8,128)(2,1)S(1)}, u32[]{:S(2)}, u32[]{:S(2)}) collective-permute-start(bf16[2,128,384]{2,1,0:T(8,128)(2,1)S(1)} %pad_maximum_fusion.9), channel_id=1, source_target_pairs={{0,14},{2,12},{4,10},{6,8},{8,6},{10,4},{12,2},{14,0},{1,15},{3,13... | collective-permute-start | bytes 589832 | tf_op jit(solution)/shard_map/ppermute | solution.py:373
  388.5 20.9 %collective-permute-start.64 = (bf16[2,64,1024]{2,1,0:T(8,128)(2,1)S(1)}, bf16[2,64,1024]{2,1,0:T(8,128)(2,1)S(1)}, u32[]{:S(2)}, u32[]{:S(2)}) collective-permute-start(bf16[2,64,1024]{2,1,0:T(8,128)(2,1)S(1)} %constant_dynamic-update-slice_fusion.33), channel_id=1, source_target_pairs={{0,2},{2,0},{4,6},{6,4},{8,10},{10,8},{12,14},{14,12},{1,3},{3,1},... | collective-permute-start | bytes 786440 | tf_op jit(solution)/shard_map/ppermute | solution.py:373
  389.4 20.1 %collective-permute-start.78 = (bf16[2,32,1024]{2,1,0:T(8,128)(2,1)S(1)}, bf16[2,32,1024]{2,1,0:T(8,128)(2,1)S(1)}, u32[]{:S(2)}, u32[]{:S(2)}) collective-permute-start(bf16[2,32,1024]{2,1,0:T(8,128)(2,1)S(1)} %constant_dynamic-update-slice_fusion.31), channel_id=1, source_target_pairs={{0,4},{2,6},{4,0},{6,2},{8,12},{10,14},{12,8},{14,10},{1,5},{3,7},... | collective-permute-start | bytes 393224 | tf_op jit(solution)/shard_map/ppermute | solution.py:373
  401.3 45.6 %collective-permute-start.81 = (bf16[2,512,128]{2,1,0:T(8,128)(2,1)S(1)}, bf16[2,512,128]{2,1,0:T(8,128)(2,1)S(1)}, u32[]{:S(2)}, u32[]{:S(2)}) collective-permute-start(bf16[2,512,128]{2,1,0:T(8,128)(2,1)S(1)} %constant_dynamic-update-slice_fusion.35), channel_id=1, source_target_pairs={{0,8},{2,10},{4,12},{6,14},{8,0},{10,2},{12,4},{14,6},{1,9},{3,11}... | collective-permute-start | bytes 786440 | tf_op jit(solution)/shard_map/ppermute | solution.py:373
  401.3 45.4 %collective-permute-start.76 = (bf16[2,512,128]{2,1,0:T(8,128)(2,1)S(1)}, bf16[2,512,128]{2,1,0:T(8,128)(2,1)S(1)}, u32[]{:S(2)}, u32[]{:S(2)}) collective-permute-start(bf16[2,512,128]{2,1,0:T(8,128)(2,1)S(1)} %constant_dynamic-update-slice_fusion.39), channel_id=1, source_target_pairs={{0,16},{16,0},{1,17},{17,1},{2,18},{18,2},{3,19},{19,3},{4,20},{20... | collective-permute-start | bytes 786440 | tf_op jit(solution)/shard_map/ppermute | solution.py:373
  405.4 36.5 %collective-permute-start.77 = (bf16[8,3,256,128]{3,2,1,0:T(8,128)(2,1)S(1)}, bf16[8,3,256,128]{3,2,1,0:T(8,128)(2,1)S(1)}, u32[]{:S(2)}, u32[]{:S(2)}) collective-permute-start(bf16[8,3,256,128]{3,2,1,0:T(8,128)(2,1)S(1)} %constant_dynamic-update-slice_fusion.37.chunks_ref), channel_id=1, source_target_pairs={{0,16},{16,0},{1,17},{17,1},{2,18},{18,2},{3,19},{19,3},{4,20},{20... | collective-permute-start | bytes 4718600 | tf_op jit(solution)/shard_map/ppermute | solution.py:373
  409.4 37.4 %collective-permute-start.82 = (bf16[4,64,1024]{2,1,0:T(8,128)(2,1)S(1)}, bf16[4,64,1024]{2,1,0:T(8,128)(2,1)S(1)}, u32[]{:S(2)}, u32[]{:S(2)}) collective-permute-start(bf16[4,64,1024]{2,1,0:T(8,128)(2,1)S(1)} %constant_dynamic-update-slice_fusion.41), channel_id=1, source_target_pairs={{0,2},{2,0},{4,6},{6,4},{8,10},{10,8},{12,14},{14,12},{1,3},{3,1},... | collective-permute-start | bytes 1572872 | tf_op jit(solution)/shard_map/ppermute | solution.py:373
  409.5 39.6 %collective-permute-start.79 = (bf16[4,64,1024]{2,1,0:T(8,128)(2,1)S(1)}, bf16[4,64,1024]{2,1,0:T(8,128)(2,1)S(1)}, u32[]{:S(2)}, u32[]{:S(2)}) collective-permute-start(bf16[4,64,1024]{2,1,0:T(8,128)(2,1)S(1)} %constant_dynamic-update-slice_fusion.67), channel_id=1, source_target_pairs={{0,4},{2,6},{4,0},{6,2},{8,12},{10,14},{12,8},{14,10},{1,5},{3,7},... | collective-permute-start | bytes 1572872 | tf_op jit(solution)/shard_map/ppermute | solution.py:373
  446.8 13.0 %collective-permute-start.86 = (bf16[4,512,128]{2,1,0:T(8,128)(2,1)S(1)}, bf16[4,512,128]{2,1,0:T(8,128)(2,1)S(1)}, u32[]{:S(2)}, u32[]{:S(2)}) collective-permute-start(bf16[4,512,128]{2,1,0:T(8,128)(2,1)S(1)} %constant_dynamic-update-slice_fusion.71), channel_id=1, source_target_pairs={{0,2},{2,0},{4,6},{6,4},{8,10},{10,8},{12,14},{14,12},{1,3},{3,1},... | collective-permute-start | bytes 1572872 | tf_op jit(solution)/shard_map/ppermute | solution.py:373
  447.0 12.9 %collective-permute-start.85 = (bf16[4,512,128]{2,1,0:T(8,128)(2,1)S(1)}, bf16[4,512,128]{2,1,0:T(8,128)(2,1)S(1)}, u32[]{:S(2)}, u32[]{:S(2)}) collective-permute-start(bf16[4,512,128]{2,1,0:T(8,128)(2,1)S(1)} %constant_dynamic-update-slice_fusion.75), channel_id=1, source_target_pairs={{0,16},{16,0},{1,17},{17,1},{2,18},{18,2},{3,19},{19,3},{4,20},{20... | collective-permute-start | bytes 1572872 | tf_op jit(solution)/shard_map/ppermute | solution.py:373
  449.3 33.7 %collective-permute-start.83 = (bf16[8,64,1024]{2,1,0:T(8,128)(2,1)S(1)}, bf16[8,64,1024]{2,1,0:T(8,128)(2,1)S(1)}, u32[]{:S(2)}, u32[]{:S(2)}) collective-permute-start(bf16[8,64,1024]{2,1,0:T(8,128)(2,1)S(1)} %constant_dynamic-update-slice_fusion.79.chunks_ref), channel_id=1, source_target_pairs={{0,16},{16,0},{1,17},{17,1},{2,18},{18,2},{3,19},{19,3},{4,20},{20... | collective-permute-start | bytes 3145736 | tf_op jit(solution)/shard_map/ppermute | solution.py:373
  460.0 24.3 %collective-permute-start.89 = (bf16[8,512,128]{2,1,0:T(8,128)(2,1)S(1)}, bf16[8,512,128]{2,1,0:T(8,128)(2,1)S(1)}, u32[]{:S(2)}, u32[]{:S(2)}) collective-permute-start(bf16[8,512,128]{2,1,0:T(8,128)(2,1)S(1)} %constant_dynamic-update-slice_fusion.83.chunks_ref), channel_id=1, source_target_pairs={{0,2},{2,0},{4,6},{6,4},{8,10},{10,8},{12,14},{14,12},{1,3},{3,1},... | collective-permute-start | bytes 3145736 | tf_op jit(solution)/shard_map/ppermute | solution.py:373
  460.1 35.3 %collective-permute-start.88 = (bf16[8,64,1024]{2,1,0:T(8,128)(2,1)S(1)}, bf16[8,64,1024]{2,1,0:T(8,128)(2,1)S(1)}, u32[]{:S(2)}, u32[]{:S(2)}) collective-permute-start(bf16[8,64,1024]{2,1,0:T(8,128)(2,1)S(1)} %constant_dynamic-update-slice_fusion.73.chunks_ref), channel_id=1, source_target_pairs={{0,8},{2,10},{4,12},{6,14},{8,0},{10,2},{12,4},{14,6},{1,9},{3,11}... | collective-permute-start | bytes 3145736 | tf_op jit(solution)/shard_map/ppermute | solution.py:373
  469.8 27.1 %collective-permute-start.87 = (bf16[8,512,128]{2,1,0:T(8,128)(2,1)S(1)}, bf16[8,512,128]{2,1,0:T(8,128)(2,1)S(1)}, u32[]{:S(2)}, u32[]{:S(2)}) collective-permute-start(bf16[8,512,128]{2,1,0:T(8,128)(2,1)S(1)} %constant_dynamic-update-slice_fusion.81.chunks_ref), channel_id=1, source_target_pairs={{0,4},{2,6},{4,0},{6,2},{8,12},{10,14},{12,8},{14,10},{1,5},{3,7},... | collective-permute-start | bytes 3145736 | tf_op jit(solution)/shard_map/ppermute | solution.py:373
  (72 other events, 1050.5 us)

commit v4 on v3

--- a/solution.py
+++ b/solution.py
@@ -397,13 +397,12 @@
     return jnp.where(which == 0, low, high)
 
 
-def gather_blocks(block):
-    count = lax.axis_size("ctx")
+def gather_blocks(block, order):
     pieces = {0: block}
-    for bit in reversed(bits_below(count)):
+    for bit in order:
         for k in list(pieces):
             pieces[k ^ bit] = exchange(pieces[k], "ctx", bit)
-    return [pieces[k] for k in range(count)]
+    return [pieces[k] for k in range(len(pieces))]
 
 
 def swap_blocks(pieces):
@@ -628,12 +627,11 @@
 
 
 LINKS = {"x": ("dp", 1), "y": ("ctx", 1), "p": ("ctx", 2), "r": ("ctx", 4)}
-ORDERS = {"b0": "xpyr", "b1": "ryxp", "i0": "yxrp", "i1": "pyxr", "o": "yxpr", "q": "xypr", "v": "rpyx"}
+ORDERS = {"b0": "pyrx", "b1": "yprx", "i0": "xypr", "i1": "yxpr", "o": "rxpy", "q": "xypr", "v": "xypr", "T": "ypr"}
 EVENTS = (
-    "b0", "A", "q", "i0", "b1", "i1", "v", "o", "q", "b0", "v", "i0", "b1", "v",
-    "o", "q", "i1", "b1", "o", "b0", "i0", "v", "i1", "q", "b1", "o", "v", "b0",
-    "i0", "i1", "b1", "T", "o", "b0", "i0", "q", "i1", "b1", "K", "b0", "o", "q",
-    "i1", "b1", "i0", "o", "b0", "i1", "i0", "o", "b0", "i0", "b1", "i1",
+    "b", "A", "i", "q", "o", "b", "i", "q", "v", "o", "v", "b", "i", "v", "o", "q",
+    "b", "o", "v", "i", "T", "o", "q", "b", "v", "o", "i", "T", "o", "b", "i", "q",
+    "T", "i", "o", "b", "q", "T", "i", "b",
 )
 
 
@@ -681,6 +679,54 @@
                 self.put(self.value, False)
         else:
             self.value = self.put(arrived, True)
+        self.line.done(self)
+
+
+class Group:
+    def __init__(self, line, names, parts, put):
+        self.line, self.put, self.step = line, put, 1
+        self.orders = [hops(name) for name in names]
+        self.value = [keep for keep, send in parts]
+        self.arrived = [exchange(send, *o[0]) for (keep, send), o in zip(parts, self.orders)]
+
+    def advance(self):
+        arrived, value = self.line.after((self.arrived, self.value))
+        tail = self.orders[0][2:]
+        step = self.step
+        self.step += 1
+        if step == 1:
+            self.arrived = [
+                exchange(added(v[v.shape[0] // 2 :], a[v.shape[0] // 2 :]), *o[1])
+                for v, a, o in zip(value, arrived, self.orders)
+            ]
+            self.value = [
+                added(v[: v.shape[0] // 2], a[: v.shape[0] // 2]) for v, a in zip(value, arrived)
+            ]
+        elif step == 2:
+            total = jnp.stack([added(v, a) for v, a in zip(value, arrived)], axis=1)
+            self.value = total[:2]
+            self.arrived = exchange(total[2:], *tail[0])
+        elif step == 3:
+            self.value = added(value[:1], arrived[:1])
+            self.arrived = exchange(added(value[1:], arrived[1:]), *tail[1])
+        elif step == 4:
+            self.value = added(value, arrived)
+            self.arrived = exchange(self.value, *tail[1])
+        elif step == 5:
+            self.value = jnp.concatenate([value, arrived], axis=0)
+            self.arrived = exchange(self.value, *tail[0])
+        elif step == 6:
+            total = jnp.concatenate([value, arrived], axis=0)
+            self.value = [total[:, 0], total[:, 1]]
+            self.arrived = [exchange(v, *o[1]) for v, o in zip(self.value, self.orders)]
+        elif step == 7:
+            self.value = [jnp.concatenate([v, a], axis=0) for v, a in zip(value, arrived)]
+            self.arrived = [exchange(v, *o[0]) for v, o in zip(self.value, self.orders)]
+            for part, chunks in enumerate(self.value):
+                self.put(chunks, part, False)
+        else:
+            for part, chunks in enumerate(arrived):
+                self.value = self.put(chunks, part, True)
         self.line.done(self)
 
 
@@ -788,7 +834,13 @@
     pair = width // ctx_count
     flat = seqs * block_rows
 
-    token_pieces = gather_blocks(tokens)
+    cut = block_rows // 4
+    token_pieces = [
+        jnp.concatenate(pair_of, axis=1)
+        for pair_of in zip(
+            gather_blocks(tokens[:, :cut], (1, 4, 2)), gather_blocks(tokens[:, cut:], (4, 2, 1))
+        )
+    ]
 
     small = (
         bias_query, bias_value, attention_out_bias, gain_one, shift_one,
@@ -825,7 +877,9 @@
         ]
     )
     token_rows = jnp.concatenate(token_pieces, axis=1)
-    projected = lowered(project(token_rows, head_weight) + head_bias)
+    projected = jnp.concatenate(
+        [lowered(project(piece, head_weight) + head_bias) for piece in token_pieces], axis=1
+    )
     head_result, head_low, head_logs = attention_forward(projected)
 
     def row_blocks(values):
@@ -863,7 +917,7 @@
         return (rows, exchange(rows, "fsdp", 1))
 
     places = {name: place_of(hops(name)) for name in ORDERS}
-    count = 1 << len(hops("b0"))
+    count = 1 << len(hops("q"))
 
     active_pair = left_pair(active_low)
     normed_pair = left_pair(normed_low)
@@ -902,14 +956,17 @@
 
     whole = {"back": None, "in": None, "out": None, "qkv": None}
 
-    def placer(target, name, part, parts, by_rows):
-        def put(chunks, far):
+    def placer(target, names, by_rows):
+        def put(chunks, part, far):
             whole[target] = put_in_place(
-                places[name], chunks, far, whole[target], part, parts, by_rows, "place_" + target
+                places[names[part]], chunks, far, whole[target], part, len(names), by_rows,
+                "place_" + target,
             )
             return whole[target]
 
         return put
+
+    put_out = placer("out", ("o",), True)
 
     class Placed:
         def __init__(self, target):
@@ -925,13 +982,11 @@
 
     line = Line()
     chains = {
-        "b0": Reduction(line, "b0", *back_parts[0], placer("back", "b0", 0, 2, True)),
-        "b1": Reduction(line, "b1", *back_parts[1], placer("back", "b1", 1, 2, True)),
-        "i0": Reduction(line, "i0", *in_parts[0], placer("in", "i0", 0, 2, False)),
-        "i1": Reduction(line, "i1", *in_parts[1], placer("in", "i1", 1, 2, False)),
-        "o": Reduction(line, "o", *out_parts, placer("out", "o", 0, 1, True)),
+        "b": Group(line, ("b0", "b1"), back_parts, placer("back", ("b0", "b1"), True)),
+        "i": Group(line, ("i0", "i1"), in_parts, placer("in", ("i0", "i1"), False)),
+        "o": Reduction(line, "o", *out_parts, lambda chunks, far: put_out(chunks, 0, far)),
     }
-    targets = {"b0": "back", "b1": "back", "i0": "in", "i1": "in", "o": "out"}
+    targets = {"b": ("back", 9), "i": ("in", 9), "o": ("out", 8)}
     line.done(chains["o"])
     token_flat = token_rows.reshape(-1, width)
 
@@ -1014,32 +1069,45 @@
             )
             return whole["qkv"]
 
-    class TokenStart:
+    class Tokens:
+        def __init__(self):
+            self.step = 0
+
         def advance(self):
-            blocks = [row_blocks(part) for part in chains["A"].head_grads]
-            pieces = [jnp.concatenate([m[k] for m in blocks], axis=-1) for k in range(ctx_count)]
-            pieces = line.after(pieces)
-            self.value = pieces[0]
-            self.arrived = swap_blocks(pieces)[1:]
+            order = hops("T")
+            if self.step == 0:
+                blocks = [row_blocks(part) for part in chains["A"].head_grads]
+                pieces = line.after(
+                    [jnp.concatenate([m[k] for m in blocks], axis=-1) for k in range(ctx_count)]
+                )
+                held = {(0, k): piece for k, piece in enumerate(pieces)}
+            else:
+                bit = order[self.step - 1][1]
+                arrived, kept = line.after((self.arrived, self.value))
+                held = dict(zip(self.kept, kept))
+                for n, (source, target) in enumerate(self.sent):
+                    held[source ^ bit, target ^ bit] = arrived[n]
+            if self.step < len(order):
+                bit = order[self.step][1]
+                self.sent = [key for key in sorted(held) if key[1] & bit]
+                self.kept = [key for key in sorted(held) if not key[1] & bit]
+                self.arrived = exchange(jnp.stack([held[key] for key in self.sent]), *order[self.step])
+                self.value = [held[key] for key in self.kept]
+            else:
+                mixed = reorder([held[k, 0] for k in range(ctx_count)], ctx)
+                mixed_grad = jnp.concatenate(
+                    [m[..., t * pair : (t + 1) * pair] for t in range(3) for m in mixed], axis=-1
+                )
+                self.value = summed_grad + back_project(mixed_grad, qkv_full)
+            self.step += 1
             line.done(self)
 
-    class TokenEnd:
-        def advance(self):
-            start = chains["T"]
-            arrived, own = line.after((start.arrived, start.value))
-            mixed = reorder([own] + arrived, ctx)
-            mixed_grad = jnp.concatenate(
-                [m[..., t * pair : (t + 1) * pair] for t in range(3) for m in mixed], axis=-1
-            )
-            self.value = summed_grad + back_project(mixed_grad, qkv_full)
-            line.done(self)
-
-    chains.update(A=Attention(), v=Vectors(), q=QueryKeyValue(), T=TokenStart(), K=TokenEnd())
+    chains.update(A=Attention(), v=Vectors(), q=QueryKeyValue(), T=Tokens())
     for name in EVENTS:
         chain = chains[name]
         chain.advance()
-        if name in targets and chain.step == 8:
-            line.done(Placed(targets[name]))
+        if name in targets and chain.step == targets[name][1]:
+            line.done(Placed(targets[name][0]))
 
     reduced = []
     offset = 0
@@ -1047,7 +1115,7 @@
     for size in sizes:
         reduced.append(half_of(chains["v"].value[offset : offset + size], core, 0))
         offset += size
-    token_grad = chains["K"].value
+    token_grad = chains["T"].value
     qkv_grad, in_grad, back_grad, out_grad = (
         whole["qkv"], whole["in"], whole["back"], whole["out"]
     )

time: 508 us -> 473 us (0.931)
  waiting for transfers between devices: 185 us -> 139 us
  local copies, waits for them, and re-layouts: 29.4 us -> 66.1 us
  starting transfers between devices: 122 us -> 108 us
  Pallas kernels: 71.5 us -> 61.9 us
    ppermute x90 -> x85, waiting for transfers between devices: 185 us -> 139 us  [exchange(): return lax.ppermute(values, axis, [(i, i ^ bit) for i in range(count)])]
    ppermute x0 -> x14, local copies, waits for them, and re-layouts: none -> 25.5 us  [exchange(): return lax.ppermute(values, axis, [(i, i ^ bit) for i in range(count)])]
    ppermute x90 -> x85, starting transfers between devices: 122 us -> 108 us  [exchange(): return lax.ppermute(values, axis, [(i, i ^ bit) for i in range(count)])]
    pallas_call x5, Pallas kernels: 28 us -> 17.9 us  [pair_grad(): pl.pallas_call(partial(grad_kernel, by_rows=by_rows), grid_spec=pltpu.Pre...]
    concatenate x1, local copies, waits for them, and re-layouts: 0.83 us -> 10 us  [on_device(): token_rows = jnp.concatenate(token_pieces, axis=1)]
    dot_general x4 -> x11, matrix products: 17.7 us -> 15.2 us  [project(): jnp.einsum('ugj,jn->ugn', left_operand_rows, right_operand_matrix, prefer...]
    convert_element_type x24 -> x16, other arithmetic: 21.7 us -> 19.6 us  [lowered(): return values.astype(jnp.bfloat16)]
    unnamed x163 -> x153, local copies, waits for them, and re-layouts: 24.3 us -> 23.4 us
  transfers between devices with their start and end apart: 90 -> 85, of which waited for: 31 -> 29; matrix products, arithmetic and copies ran while one was open for 22% -> 31% of each run, Pallas kernels for 14% -> 13%
where the time goes in v4:
time: 473 us; the launch traced here: 465 us
  waiting for transfers between devices  139 us (29%)
  starting transfers between devices  108 us (23%)
  local copies, waits for them, and re-layouts  66.1 us (14%)
  Pallas kernels  61.9 us (13%)
  other arithmetic  47.3 us (10%)
  matrix products  40.4 us (9%)
    ppermute x85, waiting for transfers between devices, exchange(): return lax.ppermute(values, axis, [(i, i ^ bit) for i in range(count)])  139 us
    ppermute x85, starting transfers between devices, exchange(): return lax.ppermute(values, axis, [(i, i ^ bit) for i in range(count)])  108 us
    ppermute x14, local copies, waits for them, and re-layouts, exchange(): return lax.ppermute(values, axis, [(i, i ^ bit) for i in range(count)])  25.5 us
    unnamed x153, local copies, waits for them, and re-layouts  23.4 us
    convert_element_type x16, other arithmetic, lowered(): return values.astype(jnp.bfloat16)  19.6 us
    dot_general x4, matrix products, back_project(): jnp.einsum('wkb,fb->wkf', gradient_row_block, right_operand_matrix, prefe...  19.3 us
    pallas_call x5, Pallas kernels, pair_grad(): pl.pallas_call(partial(grad_kernel, by_rows=by_rows), grid_spec=pltpu.Pre...  17.9 us
    dot_general x11, matrix products, project(): jnp.einsum('ugj,jn->ugn', left_operand_rows, right_operand_matrix, prefer...  15.2 us
  transfers between devices with their start and end apart: 85, of which 29 were waited for; matrix products, arithmetic and copies ran while one was open for 31% of the time, Pallas kernels for 13%

profile of v4, /device:TPU:0, one launch (start us, length us, event | category | flops | bytes accessed | tf_op | source)
XLA Modules:
  0.0 464.8 jit_solution(5407489814406777586)
XLA Ops:
  15.8 3.0 collective-permute-start.3
  22.5 2.0 copy.38
  28.7 3.0 collective-permute-start.9
  31.8 2.3 broadcast_select_fusion.4
  43.1 3.3 collective-permute-done.6
  46.4 6.4 %collective-permute-done.9 = bf16[2,96,1024]{2,1,0:T(8,128)(2,1)S(1)} collective-permute-done((bf16[2,96,1024]{2,1,0:T(8,128)(2,1)}, bf16[2,96,1024]{2,1,0:T(8,128)(2,1)S(1)}, u32[]{:S(2)}, u32[]{:S(2)}) %collective-permute-start.9) | collective-permute-done | bytes 393248 | tf_op jit(solution)/shard_map/ppermute | solution.py:373
  54.9 7.4 %collective-permute-start.10 = (bf16[2,32,1024]{2,1,0:T(8,128)(2,1)}, bf16[2,32,1024]{2,1,0:T(8,128)(2,1)S(1)}, u32[]{:S(2)}, u32[]{:S(2)}) collective-permute-start(bf16[2,32,1024]{2,1,0:T(8,128)(2,1)} %collective-permute-done.2), channel_id=1, source_target_pairs={{0,8},{2,10},{4,12},{6,14},{8,0},{10,2},{12,4},{14,6},{1,9},{3,11}... | collective-permute-start | bytes 393224 | tf_op jit(solution)/shard_map/ppermute | solution.py:373
  62.7 3.3 collective-permute-done.10
  66.0 8.0 %collective-permute-start.12 = (bf16[2,32,1024]{2,1,0:T(8,128)(2,1)S(1)}, bf16[2,32,1024]{2,1,0:T(8,128)(2,1)S(1)}, u32[]{:S(2)}, u32[]{:S(2)}) collective-permute-start(bf16[2,32,1024]{2,1,0:T(8,128)(2,1)S(1)} %collective-permute-done.8), channel_id=1, source_target_pairs={{0,4},{2,6},{4,0},{6,2},{8,12},{10,14},{12,8},{14,10},{1,5},{3,7},... | collective-permute-start | bytes 393224 | tf_op jit(solution)/shard_map/ppermute | solution.py:373
  75.5 2.8 collective-permute-done.12
  80.1 4.4 collective-permute-done.15
  85.7 11.5 %attention_forward.1 = (f32[2,1024,128]{2,1,0:T(8,128)S(1)}, bf16[2,1024,128]{2,1,0:T(8,128)(2,1)S(1)}, f32[2,1024,128]{2,1,0:T(8,128)S(1)}) custom-call(bf16[2,1024,384]{2,1,0:T(8,128)(2,1)S(1)} %fusion.39.query_ref.key_ref.value_ref, bf16[2,1024,384]{2,1,0:T(8,128)(2,1)S(1)} %fusion.39.query_ref.key_ref.value_ref, ...), custom_call_target="tpu_custom_call" | custom-call | tf_op jit(solution)/shard_map/attention_forward/pallas_call | solution.py:452
  100.0 2.2 collective-permute-start.20
  116.9 2.1 copy.42
  119.0 2.0 copy.46
  121.0 2.0 copy.44
  123.0 2.0 copy.48
  125.0 2.0 copy.50
  127.0 3.3 collective-permute-start.19
  132.1 2.6 collective-permute-start.17
  134.7 3.0 broadcast_select_fusion.9
  138.7 10.0 %concatenate.209 = bf16[2,1024,1024]{1,2,0:T(8,128)(2,1)} concatenate(bf16[2,128,1024]{1,2,0:T(8,128)(2,1)} %copy.38, bf16[2,32,1024]{1,2,0:T(8,128)(2,1)} %copy.39, bf16[2,96,1024]{1,2,0:T(8,128)(2,1)} %copy.40, bf16[2,32,1024]{1,2,0:T(8,128)(2,1)} %copy.41, bf16[2,96,1024]{1,2,0:T(8,128)(2,1)} %copy.42, bf16[2,32,1024]{1,2,0:T(8,128)(2,1)} %copy.43, ...), dimensions={1} | concatenate | bytes 8388608 | tf_op jit(solution)/shard_map/concatenate | solution.py:879
  151.3 2.5 fusion.103
  155.0 3.8 broadcast_select_fusion.3
  158.8 4.6 fusion.45
  163.5 10.5 %multiply_convert_fusion = (bf16[2,128,4096]{2,1,0:T(8,128)(2,1)S(1)}, f32[2,128,4096]{2,1,0:T(8,128)}) fusion(f32[2,128,4096]{2,1,0:T(8,128)S(1)} %get-tuple-element.604, u8[128,4096]{1,0:T(8,128)(4,1)S(1)} %get-tuple-element.410, u8[128,4096]{1,0:T(8,128)(4,1)S(1)} %get-tuple-element.409), kind=kLoop, calls=%fused_computation.25 | loop fusion | flops 73400320 | bytes 11534336 | tf_op jit(solution)/shard_map/convert_element_type | solution.py:31
  174.9 2.6 fusion.104
  182.2 9.4 %add_convert_fusion = bf16[2,128,4096]{2,1,0:T(8,128)(2,1)S(1)} fusion(f32[2,128,4096]{2,1,0:T(8,128)} %get-tuple-element.446, bf16[2,128,1024]{2,1,0:T(8,128)(2,1)S(1)} %get-tuple-element.432, bf16[2048,1024]{1,0:T(8,128)(2,1)} %copy-done.21, bf16[2048,1024]{1,0:T(8,128)(2,1)} %copy-done.20, f32[2,128,4096]{2,1,0:T(8,128)} %copy-done.24), kind=kOutput, calls=%fused_computation.24 | convolution fusion | flops 2178940928 | bytes 19398656 | tf_op jit(solution)/shard_map/wkb,fb->wkf/dot_general | solution.py:51
  191.6 3.3 grad_back.2
  194.9 2.8 grad_back.3
  197.7 6.3 %multiply_reduce_fusion = (f32[1024]{0:T(1024)S(1)}, f32[2,128]{1,0:T(2,128)S(1)}, f32[1024]{0:T(1024)S(1)}, f32[2,128,1024]{2,1,0:T(8,128)S(1)}) fusion(f32[2,128,1024]{2,1,0:T(8,128)S(1)} %get-tuple-element.603, f32[2,128]{1,0:T(2,128)S(1)} %fusion.78, f32[2,128]{1,0:T(2,128)S(1)} %broadcast_multiply_fusion.1, f32[1024]{0:T(1024)S(1)} %get-tuple-element.608, ...), kind=kOutput, calls=%fused_computation.97 | convolution fusion | flops 2168715008 | bytes 14179328 | tf_op jit(solution)/shard_map/wkb,fb->wkf/dot_general | solution.py:51
  209.6 4.6 grad_in.2
  215.2 4.6 grad_in.3
  223.3 2.6 grad_out.1
  225.9 5.7 %collective-permute-done.40 = bf16[8,64,1024]{2,1,0:T(8,128)(2,1)} collective-permute-done((bf16[8,64,1024]{2,1,0:T(8,128)(2,1)}, bf16[8,64,1024]{2,1,0:T(8,128)(2,1)}, u32[]{:S(2)}, u32[]{:S(2)}) %collective-permute-start.40) | collective-permute-done | bytes 1048608 | tf_op jit(solution)/shard_map/ppermute | solution.py:373
  231.7 3.3 collective-permute-start.37
  234.9 2.6 add_convert_fusion.6
  238.8 3.1 collective-permute-start.39
  246.8 2.3 collective-permute-start.48
  249.3 14.3 %attention_backward.1 = (bf16[2,1024,128]{2,1,0:T(8,128)(2,1)S(1)}, bf16[2,1024,128]{2,1,0:T(8,128)(2,1)S(1)}, bf16[2,1024,128]{2,1,0:T(8,128)(2,1)S(1)}) custom-call(bf16[2,1024,384]{2,1,0:T(8,128)(2,1)S(1)} %fusion.39.query_ref.key_ref.value_ref, bf16[2,1024,384]{2,1,0:T(8,128)(2,1)S(1)} %fusion.39.query_ref.key_ref.value_ref, ...), custom_call_target="tpu_custom_call" | custom-call | tf_op jit(solution)/shard_map/attention_backward/pallas_call | solution.py:531
  267.6 3.4 convolution_bitcast_fusion.2
  277.9 2.2 collective-permute-done.46
  283.3 6.9 %collective-permute-done.43 = bf16[4,512,128]{2,1,0:T(8,128)(2,1)S(1)} collective-permute-done((bf16[4,512,128]{2,1,0:T(8,128)(2,1)S(1)}, bf16[4,512,128]{2,1,0:T(8,128)(2,1)S(1)}, u32[]{:S(2)}, u32[]{:S(2)}) %collective-permute-start.43) | collective-permute-done | bytes 524320 | tf_op jit(solution)/shard_map/ppermute | solution.py:373
  292.1 3.0 collective-permute-done.50
  302.0 8.4 %collective-permute-done.51 = bf16[2,2,64,1024]{3,2,0,1:T(8,128)(2,1)S(1)} collective-permute-done((bf16[2,2,64,1024]{3,2,0,1:T(8,128)(2,1)S(1)}, bf16[2,2,64,1024]{3,2,0,1:T(8,128)(2,1)S(1)}, u32[]{:S(2)}, u32[]{:S(2)}) %collective-permute-start.51) | collective-permute-done | bytes 524320 | tf_op jit(solution)/shard_map/ppermute | solution.py:373
  312.1 8.7 %collective-permute-done.49 = bf16[2,2,512,128]{3,2,0,1:T(8,128)(2,1)S(1)} collective-permute-done((bf16[2,2,512,128]{3,2,0,1:T(8,128)(2,1)S(1)}, bf16[2,2,512,128]{3,2,0,1:T(8,128)(2,1)S(1)}, u32[]{:S(2)}, u32[]{:S(2)}) %collective-permute-start.49) | collective-permute-done | bytes 524320 | tf_op jit(solution)/shard_map/ppermute | solution.py:373
  321.0 2.3 collective-permute-start.57
  324.5 2.6 collective-permute-start.59
  329.3 2.1 collective-permute-start.63
  332.5 2.1 collective-permute-start.62
  335.3 9.5 %collective-permute-done.65 = bf16[2,3,256,128]{3,2,1,0:T(8,128)(2,1)S(1)} collective-permute-done((bf16[2,3,256,128]{3,2,1,0:T(8,128)(2,1)S(1)}, bf16[2,3,256,128]{3,2,1,0:T(8,128)(2,1)S(1)}, u32[]{:S(2)}, u32[]{:S(2)}) %collective-permute-start.65) | collective-permute-done | bytes 393248 | tf_op jit(solution)/shard_map/ppermute | solution.py:373
  344.9 2.1 collective-permute-start.74
  349.7 2.5 collective-permute-start.68
  352.2 13.0 %collective-permute-done.69 = bf16[4,2,128,384]{3,2,1,0:T(8,128)(2,1)S(1)} collective-permute-done((bf16[4,2,128,384]{3,2,1,0:T(8,128)(2,1)S(1)}, bf16[4,2,128,384]{3,2,1,0:T(8,128)(2,1)S(1)}, u32[]{:S(2)}, u32[]{:S(2)}) %collective-permute-start.69) | collective-permute-done | bytes 786464 | tf_op jit(solution)/shard_map/ppermute | solution.py:373
  369.7 9.1 %collective-permute-start.72 = (bf16[4,512,128]{2,1,0:T(8,128)(2,1)S(1)}, bf16[4,512,128]{2,1,0:T(8,128)(2,1)S(1)}, u32[]{:S(2)}, u32[]{:S(2)}) collective-permute-start(bf16[4,512,128]{2,1,0:T(8,128)(2,1)S(1)} %get-tuple-element.377), channel_id=1, source_target_pairs={{0,2},{2,0},{4,6},{6,4},{8,10},{10,8},{12,14},{14,12},{1,3},{3,1},... | collective-permute-start | bytes 1572872 | tf_op jit(solution)/shard_map/ppermute | solution.py:373
  378.9 3.0 collective-permute-start.73
  384.0 2.3 place_qkv.2.rest_0_
  388.2 5.1 %collective-permute-done.72 = bf16[4,512,128]{2,1,0:T(8,128)(2,1)S(1)} collective-permute-done((bf16[4,512,128]{2,1,0:T(8,128)(2,1)S(1)}, bf16[4,512,128]{2,1,0:T(8,128)(2,1)S(1)}, u32[]{:S(2)}, u32[]{:S(2)}) %collective-permute-start.72) | collective-permute-done | bytes 524320 | tf_op jit(solution)/shard_map/ppermute | solution.py:373
  394.7 3.8 collective-permute-start.78
  400.2 34.3 %collective-permute-done.82.chunks_ref = bf16[8,32,1024]{2,1,0:T(8,128)(2,1)S(1)} collective-permute-done((bf16[8,32,1024]{2,1,0:T(8,128)(2,1)S(1)}, bf16[8,32,1024]{2,1,0:T(8,128)(2,1)S(1)}, u32[]{:S(2)}, u32[]{:S(2)}) %collective-permute-start.82) | collective-permute-done | bytes 524320 | tf_op jit(solution)/shard_map/ppermute | solution.py:373
  440.3 2.3 collective-permute-start.84
  442.6 2.3 place_qkv.3
  448.0 2.8 fusion.16
  454.9 6.9 %collective-permute-done.84.chunks_ref = bf16[8,64,1024]{2,1,0:T(8,128)(2,1)S(1)} collective-permute-done((bf16[8,64,1024]{2,1,0:T(8,128)(2,1)S(1)}, bf16[8,64,1024]{2,1,0:T(8,128)(2,1)S(1)}, u32[]{:S(2)}, u32[]{:S(2)}) %collective-permute-start.84) | collective-permute-done | bytes 1048608 | tf_op jit(solution)/shard_map/ppermute | solution.py:373
  (441 shorter events, 143.9 us)
Async XLA Ops:
  0.6 28.1 %collective-permute-start = (bf16[512,3072]{1,0:T(8,128)(2,1)}, bf16[512,3072]{1,0:T(8,128)(2,1)S(1)}, u32[]{:S(2)}, u32[]{:S(2)}) collective-permute-start(bf16[512,3072]{1,0:T(8,128)(2,1)} %param.16), channel_id=1, source_target_pairs={{0,1},{1,0},{2,3},{3,2},{4,5},{5,4},{6,7},{7,6},{8,9},{9,8},{10,11... | collective-permute-start | bytes 9437192 | tf_op jit(solution)/shard_map/ppermute | solution.py:373
  15.8 20.8 %collective-permute-start.3 = (bf16[2,96,1024]{2,1,0:T(8,128)(2,1)}, bf16[2,96,1024]{2,1,0:T(8,128)(2,1)S(1)}, u32[]{:S(2)}, u32[]{:S(2)}) collective-permute-start(bf16[2,96,1024]{2,1,0:T(8,128)(2,1)} %slice.517), channel_id=1, source_target_pairs={{0,2},{2,0},{4,6},{6,4},{8,10},{10,8},{12,14},{14,12},{1,3},{3,1},... | collective-permute-start | bytes 1179656 | tf_op jit(solution)/shard_map/ppermute | solution.py:373
  18.8 18.0 %collective-permute-start.5 = (bf16[2,96,1024]{2,1,0:T(8,128)(2,1)}, bf16[2,96,1024]{2,1,0:T(8,128)(2,1)}, u32[]{:S(2)}, u32[]{:S(2)}) collective-permute-start(bf16[2,96,1024]{2,1,0:T(8,128)(2,1)} %slice.517), channel_id=1, source_target_pairs={{0,4},{2,6},{4,0},{6,2},{8,12},{10,14},{12,8},{14,10},{1,5},{3,7},... | collective-permute-start | bytes 1179656 | tf_op jit(solution)/shard_map/ppermute | solution.py:373
  21.9 14.7 %collective-permute-start.2 = (bf16[2,32,1024]{2,1,0:T(8,128)(2,1)}, bf16[2,32,1024]{2,1,0:T(8,128)(2,1)}, u32[]{:S(2)}, u32[]{:S(2)}) collective-permute-start(bf16[2,32,1024]{2,1,0:T(8,128)(2,1)} %slice.516), channel_id=1, source_target_pairs={{0,2},{2,0},{4,6},{6,4},{8,10},{10,8},{12,14},{14,12},{1,3},{3,1},... | collective-permute-start | bytes 393224 | tf_op jit(solution)/shard_map/ppermute | solution.py:373
  24.5 15.5 %collective-permute-start.4 = (bf16[2,32,1024]{2,1,0:T(8,128)(2,1)}, bf16[2,32,1024]{2,1,0:T(8,128)(2,1)S(1)}, u32[]{:S(2)}, u32[]{:S(2)}) collective-permute-start(bf16[2,32,1024]{2,1,0:T(8,128)(2,1)} %slice.516), channel_id=1, source_target_pairs={{0,4},{2,6},{4,0},{6,2},{8,12},{10,14},{12,8},{14,10},{1,5},{3,7},... | collective-permute-start | bytes 393224 | tf_op jit(solution)/shard_map/ppermute | solution.py:373
  28.7 24.1 %collective-permute-start.9 = (bf16[2,96,1024]{2,1,0:T(8,128)(2,1)}, bf16[2,96,1024]{2,1,0:T(8,128)(2,1)S(1)}, u32[]{:S(2)}, u32[]{:S(2)}) collective-permute-start(bf16[2,96,1024]{2,1,0:T(8,128)(2,1)} %slice.517), channel_id=1, source_target_pairs={{0,8},{2,10},{4,12},{6,14},{8,0},{10,2},{12,4},{14,6},{1,9},{3,11}... | collective-permute-start | bytes 1179656 | tf_op jit(solution)/shard_map/ppermute | solution.py:373
  36.7 18.2 %collective-permute-start.8 = (bf16[2,32,1024]{2,1,0:T(8,128)(2,1)}, bf16[2,32,1024]{2,1,0:T(8,128)(2,1)S(1)}, u32[]{:S(2)}, u32[]{:S(2)}) collective-permute-start(bf16[2,32,1024]{2,1,0:T(8,128)(2,1)} %slice.516), channel_id=1, source_target_pairs={{0,8},{2,10},{4,12},{6,14},{8,0},{10,2},{12,4},{14,6},{1,9},{3,11}... | collective-permute-start | bytes 393224 | tf_op jit(solution)/shard_map/ppermute | solution.py:373
  36.7 90.4 %collective-permute-start.23 = (bf16[512,1024]{1,0:T(8,128)(2,1)}, bf16[512,1024]{1,0:T(8,128)(2,1)}, u32[]{:S(2)}, u32[]{:S(2)}) collective-permute-start(bf16[512,1024]{1,0:T(8,128)(2,1)} %param.19), channel_id=1, source_target_pairs={{0,1},{1,0},{2,3},{3,2},{4,5},{5,4},{6,7},{7,6},{8,9},{9,8},{10,11... | collective-permute-start | bytes 3145736 | tf_op jit(solution)/shard_map/ppermute | solution.py:373
  36.8 17.6 %collective-permute-start.7 = (bf16[2,96,1024]{2,1,0:T(8,128)(2,1)}, bf16[2,96,1024]{2,1,0:T(8,128)(2,1)S(1)}, u32[]{:S(2)}, u32[]{:S(2)}) collective-permute-start(bf16[2,96,1024]{2,1,0:T(8,128)(2,1)} %collective-permute-done.5), channel_id=1, source_target_pairs={{0,2},{2,0},{4,6},{6,4},{8,10},{10,8},{12,14},{14,12},{1,3},{3,1},... | collective-permute-start | bytes 1179656 | tf_op jit(solution)/shard_map/ppermute | solution.py:373
  46.4 108.6 %collective-permute-start.24 = (bf16[512,4096]{1,0:T(8,128)(2,1)}, bf16[512,4096]{1,0:T(8,128)(2,1)}, u32[]{:S(2)}, u32[]{:S(2)}) collective-permute-start(bf16[512,4096]{1,0:T(8,128)(2,1)} %param.23), channel_id=1, source_target_pairs={{0,1},{1,0},{2,3},{3,2},{4,5},{5,4},{6,7},{7,6},{8,9},{9,8},{10,11... | collective-permute-start | bytes 12582920 | tf_op jit(solution)/shard_map/ppermute | solution.py:373
  52.8 21.1 %collective-permute-start.11 = (bf16[2,96,1024]{2,1,0:T(8,128)(2,1)S(1)}, bf16[2,96,1024]{2,1,0:T(8,128)(2,1)S(1)}, u32[]{:S(2)}, u32[]{:S(2)}) collective-permute-start(bf16[2,96,1024]{2,1,0:T(8,128)(2,1)S(1)} %collective-permute-done.9), channel_id=1, source_target_pairs={{0,2},{2,0},{4,6},{6,4},{8,10},{10,8},{12,14},{14,12},{1,3},{3,1},... | collective-permute-start | bytes 1179656 | tf_op jit(solution)/shard_map/ppermute | solution.py:373
  54.4 19.7 %collective-permute-start.13 = (bf16[2,96,1024]{2,1,0:T(8,128)(2,1)S(1)}, bf16[2,96,1024]{2,1,0:T(8,128)(2,1)S(1)}, u32[]{:S(2)}, u32[]{:S(2)}) collective-permute-start(bf16[2,96,1024]{2,1,0:T(8,128)(2,1)S(1)} %collective-permute-done.9), channel_id=1, source_target_pairs={{0,4},{2,6},{4,0},{6,2},{8,12},{10,14},{12,8},{14,10},{1,5},{3,7},... | collective-permute-start | bytes 1179656 | tf_op jit(solution)/shard_map/ppermute | solution.py:373
  99.1 28.0 %collective-permute-start.22 = (bf16[2,128,128]{2,1,0:T(8,128)(2,1)}, bf16[2,128,128]{2,1,0:T(8,128)(2,1)}, u32[]{:S(2)}, u32[]{:S(2)}) collective-permute-start(bf16[2,128,128]{2,1,0:T(8,128)(2,1)} %get-tuple-element.548), channel_id=1, source_target_pairs={{0,2},{2,0},{4,6},{6,4},{8,10},{10,8},{12,14},{14,12},{1,3},{3,1},... | collective-permute-start | bytes 196616 | tf_op jit(solution)/shard_map/ppermute | solution.py:373
  100.0 30.4 %collective-permute-start.20 = (bf16[2,128,128]{2,1,0:T(8,128)(2,1)}, bf16[2,128,128]{2,1,0:T(8,128)(2,1)}, u32[]{:S(2)}, u32[]{:S(2)}) collective-permute-start(bf16[2,128,128]{2,1,0:T(8,128)(2,1)} %get-tuple-element.550), channel_id=1, source_target_pairs={{0,6},{2,4},{4,2},{6,0},{8,14},{10,12},{12,10},{14,8},{1,7},{3,5},... | collective-permute-start | bytes 196616 | tf_op jit(solution)/shard_map/ppermute | solution.py:373
  102.2 29.9 %collective-permute-start.21 = (bf16[2,128,128]{2,1,0:T(8,128)(2,1)}, bf16[2,128,128]{2,1,0:T(8,128)(2,1)}, u32[]{:S(2)}, u32[]{:S(2)}) collective-permute-start(bf16[2,128,128]{2,1,0:T(8,128)(2,1)} %get-tuple-element.549), channel_id=1, source_target_pairs={{0,4},{2,6},{4,0},{6,2},{8,12},{10,14},{12,8},{14,10},{1,5},{3,7},... | collective-permute-start | bytes 196616 | tf_op jit(solution)/shard_map/ppermute | solution.py:373
  127.0 21.7 %collective-permute-start.18 = (bf16[2,128,128]{2,1,0:T(8,128)(2,1)}, bf16[2,128,128]{2,1,0:T(8,128)(2,1)}, u32[]{:S(2)}, u32[]{:S(2)}) collective-permute-start(bf16[2,128,128]{2,1,0:T(8,128)(2,1)} %get-tuple-element.552), channel_id=1, source_target_pairs={{0,10},{2,8},{4,14},{6,12},{8,2},{10,0},{12,6},{14,4},{1,11},{3,9}... | collective-permute-start | bytes 196616 | tf_op jit(solution)/shard_map/ppermute | solution.py:373
  127.0 21.8 %collective-permute-start.19 = (bf16[2,128,128]{2,1,0:T(8,128)(2,1)}, bf16[2,128,128]{2,1,0:T(8,128)(2,1)}, u32[]{:S(2)}, u32[]{:S(2)}) collective-permute-start(bf16[2,128,128]{2,1,0:T(8,128)(2,1)} %get-tuple-element.551), channel_id=1, source_target_pairs={{0,8},{2,10},{4,12},{6,14},{8,0},{10,2},{12,4},{14,6},{1,9},{3,11}... | collective-permute-start | bytes 196616 | tf_op jit(solution)/shard_map/ppermute | solution.py:373
  130.3 18.5 %collective-permute-start.16 = (bf16[2,128,128]{2,1,0:T(8,128)(2,1)}, bf16[2,128,128]{2,1,0:T(8,128)(2,1)}, u32[]{:S(2)}, u32[]{:S(2)}) collective-permute-start(bf16[2,128,128]{2,1,0:T(8,128)(2,1)} %get-tuple-element.553), channel_id=1, source_target_pairs={{0,14},{2,12},{4,10},{6,8},{8,6},{10,4},{12,2},{14,0},{1,15},{3,13... | collective-permute-start | bytes 196616 | tf_op jit(solution)/shard_map/ppermute | solution.py:373
  132.1 16.8 %collective-permute-start.17 = (bf16[2,128,128]{2,1,0:T(8,128)(2,1)}, bf16[2,128,128]{2,1,0:T(8,128)(2,1)}, u32[]{:S(2)}, u32[]{:S(2)}) collective-permute-start(bf16[2,128,128]{2,1,0:T(8,128)(2,1)} %get-tuple-element.547), channel_id=1, source_target_pairs={{0,12},{2,14},{4,8},{6,10},{8,4},{10,6},{12,0},{14,2},{1,13},{3,15... | collective-permute-start | bytes 196616 | tf_op jit(solution)/shard_map/ppermute | solution.py:373
  148.7 25.2 %collective-permute-start.25 = (bf16[2048,1024]{1,0:T(8,128)(2,1)}, bf16[2048,1024]{1,0:T(8,128)(2,1)S(1)}, u32[]{:S(2)}, u32[]{:S(2)}) collective-permute-start(bf16[2048,1024]{1,0:T(8,128)(2,1)} %param.25), channel_id=1, source_target_pairs={{0,1},{1,0},{2,3},{3,2},{4,5},{5,4},{6,7},{7,6},{8,9},{9,8},{10,11... | collective-permute-start | bytes 12582920 | tf_op jit(solution)/shard_map/ppermute | solution.py:373
  154.4 54.1 %collective-permute-start.29 = (bf16[256,512]{1,0:T(8,128)(2,1)S(1)}, bf16[256,512]{1,0:T(8,128)(2,1)S(1)}, u32[]{:S(2)}, u32[]{:S(2)}) collective-permute-start(bf16[256,512]{1,0:T(8,128)(2,1)S(1)} %get-tuple-element.545), channel_id=1, source_target_pairs={{0,1},{1,0},{2,3},{3,2},{4,5},{5,4},{6,7},{7,6},{8,9},{9,8},{10,11... | collective-permute-start | bytes 786440 | tf_op jit(solution)/shard_map/ppermute | solution.py:373
  204.8 15.0 %collective-permute-start.28 = (bf16[256,1024]{1,0:T(8,128)(2,1)S(1)}, bf16[256,1024]{1,0:T(8,128)(2,1)S(1)}, u32[]{:S(2)}, u32[]{:S(2)}) collective-permute-start(bf16[256,1024]{1,0:T(8,128)(2,1)S(1)} %bitcast.137), channel_id=1, source_target_pairs={{0,1},{1,0},{2,3},{3,2},{4,5},{5,4},{6,7},{7,6},{8,9},{9,8},{10,11... | collective-permute-start | bytes 1572872 | tf_op jit(solution)/shard_map/ppermute | solution.py:373
  205.3 26.3 %collective-permute-start.40 = (bf16[8,64,1024]{2,1,0:T(8,128)(2,1)}, bf16[8,64,1024]{2,1,0:T(8,128)(2,1)}, u32[]{:S(2)}, u32[]{:S(2)}) collective-permute-start(bf16[8,64,1024]{2,1,0:T(8,128)(2,1)} %get-tuple-element.236), channel_id=1, source_target_pairs={{0,4},{2,6},{4,0},{6,2},{8,12},{10,14},{12,8},{14,10},{1,5},{3,7},... | collective-permute-start | bytes 3145736 | tf_op jit(solution)/shard_map/ppermute | solution.py:373
  205.3 26.3 %collective-permute-start.41 = (bf16[8,64,1024]{2,1,0:T(8,128)(2,1)S(1)}, bf16[8,64,1024]{2,1,0:T(8,128)(2,1)S(1)}, u32[]{:S(2)}, u32[]{:S(2)}) collective-permute-start(bf16[8,64,1024]{2,1,0:T(8,128)(2,1)S(1)} %get-tuple-element.237), channel_id=1, source_target_pairs={{0,2},{2,0},{4,6},{6,4},{8,10},{10,8},{12,14},{14,12},{1,3},{3,1},... | collective-permute-start | bytes 3145736 | tf_op jit(solution)/shard_map/ppermute | solution.py:373
  219.8 17.8 %collective-permute-start.33 = (bf16[2,128,128]{2,1,0:T(8,128)(2,1)S(1)}, bf16[2,128,128]{2,1,0:T(8,128)(2,1)S(1)}, u32[]{:S(2)}, u32[]{:S(2)}) collective-permute-start(bf16[2,128,128]{2,1,0:T(8,128)(2,1)S(1)} %get-tuple-element.229), channel_id=1, source_target_pairs={{0,2},{2,0},{4,6},{6,4},{8,10},{10,8},{12,14},{14,12},{1,3},{3,1},... | collective-permute-start | bytes 196616 | tf_op jit(solution)/shard_map/ppermute | solution.py:373
  220.7 18.1 %collective-permute-start.34 = (bf16[2,128,128]{2,1,0:T(8,128)(2,1)S(1)}, bf16[2,128,128]{2,1,0:T(8,128)(2,1)S(1)}, u32[]{:S(2)}, u32[]{:S(2)}) collective-permute-start(bf16[2,128,128]{2,1,0:T(8,128)(2,1)S(1)} %get-tuple-element.230), channel_id=1, source_target_pairs={{0,4},{2,6},{4,0},{6,2},{8,12},{10,14},{12,8},{14,10},{1,5},{3,7},... | collective-permute-start | bytes 196616 | tf_op jit(solution)/shard_map/ppermute | solution.py:373
  222.2 21.1 %collective-permute-start.35 = (bf16[2,128,128]{2,1,0:T(8,128)(2,1)S(1)}, bf16[2,128,128]{2,1,0:T(8,128)(2,1)S(1)}, u32[]{:S(2)}, u32[]{:S(2)}) collective-permute-start(bf16[2,128,128]{2,1,0:T(8,128)(2,1)S(1)} %get-tuple-element.231), channel_id=1, source_target_pairs={{0,6},{2,4},{4,2},{6,0},{8,14},{10,12},{12,10},{14,8},{1,7},{3,5},... | collective-permute-start | bytes 196616 | tf_op jit(solution)/shard_map/ppermute | solution.py:373
  231.7 14.1 %collective-permute-start.37 = (bf16[2,128,128]{2,1,0:T(8,128)(2,1)S(1)}, bf16[2,128,128]{2,1,0:T(8,128)(2,1)S(1)}, u32[]{:S(2)}, u32[]{:S(2)}) collective-permute-start(bf16[2,128,128]{2,1,0:T(8,128)(2,1)S(1)} %get-tuple-element.233), channel_id=1, source_target_pairs={{0,10},{2,8},{4,14},{6,12},{8,2},{10,0},{12,6},{14,4},{1,11},{3,9}... | collective-permute-start | bytes 196616 | tf_op jit(solution)/shard_map/ppermute | solution.py:373
  243.3 28.1 %collective-permute-start.31 = (bf16[8,512,128]{2,1,0:T(8,128)(2,1)}, bf16[8,512,128]{2,1,0:T(8,128)(2,1)}, u32[]{:S(2)}, u32[]{:S(2)}) collective-permute-start(bf16[8,512,128]{2,1,0:T(8,128)(2,1)} %get-tuple-element.224), channel_id=1, source_target_pairs={{0,16},{16,0},{1,17},{17,1},{2,18},{18,2},{3,19},{19,3},{4,20},{20... | collective-permute-start | bytes 3145736 | tf_op jit(solution)/shard_map/ppermute | solution.py:373
  244.8 26.7 %collective-permute-start.32 = (bf16[8,512,128]{2,1,0:T(8,128)(2,1)}, bf16[8,512,128]{2,1,0:T(8,128)(2,1)}, u32[]{:S(2)}, u32[]{:S(2)}) collective-permute-start(bf16[8,512,128]{2,1,0:T(8,128)(2,1)} %get-tuple-element.225), channel_id=1, source_target_pairs={{0,2},{2,0},{4,6},{6,4},{8,10},{10,8},{12,14},{14,12},{1,3},{3,1},... | collective-permute-start | bytes 3145736 | tf_op jit(solution)/shard_map/ppermute | solution.py:373
  245.7 34.4 %collective-permute-start.46 = (bf16[4,64,1024]{2,1,0:T(8,128)(2,1)}, bf16[4,64,1024]{2,1,0:T(8,128)(2,1)}, u32[]{:S(2)}, u32[]{:S(2)}) collective-permute-start(bf16[4,64,1024]{2,1,0:T(8,128)(2,1)} %get-tuple-element.468), channel_id=1, source_target_pairs={{0,2},{2,0},{4,6},{6,4},{8,10},{10,8},{12,14},{14,12},{1,3},{3,1},... | collective-permute-start | bytes 1572872 | tf_op jit(solution)/shard_map/ppermute | solution.py:373
  246.8 33.3 %collective-permute-start.47 = (bf16[4,64,1024]{2,1,0:T(8,128)(2,1)}, bf16[4,64,1024]{2,1,0:T(8,128)(2,1)}, u32[]{:S(2)}, u32[]{:S(2)}) collective-permute-start(bf16[4,64,1024]{2,1,0:T(8,128)(2,1)} %get-tuple-element.466), channel_id=1, source_target_pairs={{0,4},{2,6},{4,0},{6,2},{8,12},{10,14},{12,8},{14,10},{1,5},{3,7},... | collective-permute-start | bytes 1572872 | tf_op jit(solution)/shard_map/ppermute | solution.py:373
  246.8 29.2 %collective-permute-start.48 = (bf16[8,32,1024]{2,1,0:T(8,128)(2,1)}, bf16[8,32,1024]{2,1,0:T(8,128)(2,1)}, u32[]{:S(2)}, u32[]{:S(2)}) collective-permute-start(bf16[8,32,1024]{2,1,0:T(8,128)(2,1)} %get-tuple-element.269), channel_id=1, source_target_pairs={{0,8},{2,10},{4,12},{6,14},{8,0},{10,2},{12,4},{14,6},{1,9},{3,11}... | collective-permute-start | bytes 1572872 | tf_op jit(solution)/shard_map/ppermute | solution.py:373
  271.5 24.9 %collective-permute-start.52 = (f32[12288]{0:T(1024)S(1)}, f32[12288]{0:T(1024)S(1)}, u32[]{:S(2)}, u32[]{:S(2)}) collective-permute-start(f32[12288]{0:T(1024)S(1)} %constant_dynamic-update-slice_fusion.69), channel_id=1, source_target_pairs={{0,1},{1,0},{2,3},{3,2},{4,5},{5,4},{6,7},{7,6},{8,9},{9,8},{10,11... | collective-permute-start | bytes 147464 | tf_op jit(solution)/shard_map/ppermute | solution.py:373
  275.4 14.8 %collective-permute-start.43 = (bf16[4,512,128]{2,1,0:T(8,128)(2,1)S(1)}, bf16[4,512,128]{2,1,0:T(8,128)(2,1)S(1)}, u32[]{:S(2)}, u32[]{:S(2)}) collective-permute-start(bf16[4,512,128]{2,1,0:T(8,128)(2,1)S(1)} %get-tuple-element.473), channel_id=1, source_target_pairs={{0,2},{2,0},{4,6},{6,4},{8,10},{10,8},{12,14},{14,12},{1,3},{3,1},... | collective-permute-start | bytes 1572872 | tf_op jit(solution)/shard_map/ppermute | solution.py:373
  276.0 14.9 %collective-permute-start.44 = (bf16[4,512,128]{2,1,0:T(8,128)(2,1)S(1)}, bf16[4,512,128]{2,1,0:T(8,128)(2,1)S(1)}, u32[]{:S(2)}, u32[]{:S(2)}) collective-permute-start(bf16[4,512,128]{2,1,0:T(8,128)(2,1)S(1)} %get-tuple-element.471), channel_id=1, source_target_pairs={{0,16},{16,0},{1,17},{17,1},{2,18},{18,2},{3,19},{19,3},{4,20},{20... | collective-permute-start | bytes 1572872 | tf_op jit(solution)/shard_map/ppermute | solution.py:373
  280.1 15.0 %collective-permute-start.50 = (bf16[3,256,128]{2,1,0:T(8,128)(2,1)S(1)}, bf16[3,256,128]{2,1,0:T(8,128)(2,1)S(1)}, u32[]{:S(2)}, u32[]{:S(2)}) collective-permute-start(bf16[3,256,128]{2,1,0:T(8,128)(2,1)S(1)} %select_convert_fusion.1), channel_id=1, source_target_pairs={{0,16},{16,0},{1,17},{17,1},{2,18},{18,2},{3,19},{19,3},{4,20},{20... | collective-permute-start | bytes 589832 | tf_op jit(solution)/shard_map/ppermute | solution.py:373
  283.3 27.1 %collective-permute-start.51 = (bf16[2,2,64,1024]{3,2,0,1:T(8,128)(2,1)S(1)}, bf16[2,2,64,1024]{3,2,0,1:T(8,128)(2,1)S(1)}, u32[]{:S(2)}, u32[]{:S(2)}) collective-permute-start(bf16[2,2,64,1024]{3,2,0,1:T(8,128)(2,1)S(1)} %get-tuple-element.494), channel_id=1, source_target_pairs={{0,8},{2,10},{4,12},{6,14},{8,0},{10,2},{12,4},{14,6},{1,9},{3,11}... | collective-permute-start | bytes 1572872 | tf_op jit(solution)/shard_map/ppermute | solution.py:373
  291.3 29.5 %collective-permute-start.49 = (bf16[2,2,512,128]{3,2,0,1:T(8,128)(2,1)S(1)}, bf16[2,2,512,128]{3,2,0,1:T(8,128)(2,1)S(1)}, u32[]{:S(2)}, u32[]{:S(2)}) collective-permute-start(bf16[2,2,512,128]{3,2,0,1:T(8,128)(2,1)S(1)} %get-tuple-element.497), channel_id=1, source_target_pairs={{0,4},{2,6},{4,0},{6,2},{8,12},{10,14},{12,8},{14,10},{1,5},{3,7},... | collective-permute-start | bytes 1572872 | tf_op jit(solution)/shard_map/ppermute | solution.py:373
  295.2 31.9 %collective-permute-start.60 = (bf16[1,3,256,128]{3,2,1,0:T(8,128)(2,1)S(1)}, bf16[1,3,256,128]{3,2,1,0:T(8,128)(2,1)S(1)}, u32[]{:S(2)}, u32[]{:S(2)}) collective-permute-start(bf16[1,3,256,128]{3,2,1,0:T(8,128)(2,1)S(1)} %fusion.77), channel_id=1, source_target_pairs={{0,8},{2,10},{4,12},{6,14},{8,0},{10,2},{12,4},{14,6},{1,9},{3,11}... | collective-permute-start | bytes 589832 | tf_op jit(solution)/shard_map/ppermute | solution.py:373
  300.0 24.5 %collective-permute-start.58 = (bf16[2,32,1024]{2,1,0:T(8,128)(2,1)S(1)}, bf16[2,32,1024]{2,1,0:T(8,128)(2,1)S(1)}, u32[]{:S(2)}, u32[]{:S(2)}) collective-permute-start(bf16[2,32,1024]{2,1,0:T(8,128)(2,1)S(1)} %get-tuple-element.536), channel_id=1, source_target_pairs={{0,4},{2,6},{4,0},{6,2},{8,12},{10,14},{12,8},{14,10},{1,5},{3,7},... | collective-permute-start | bytes 393224 | tf_op jit(solution)/shard_map/ppermute | solution.py:373
  301.0 20.0 %collective-permute-start.56 = (f32[12288]{0:T(1024)S(1)}, f32[12288]{0:T(1024)S(1)}, u32[]{:S(2)}, u32[]{:S(2)}) collective-permute-start(f32[12288]{0:T(1024)S(1)} %add.351), channel_id=1, source_target_pairs={{0,2},{2,0},{4,6},{6,4},{8,10},{10,8},{12,14},{14,12},{1,3},{3,1},... | collective-permute-start | bytes 147464 | tf_op jit(solution)/shard_map/ppermute | solution.py:373
  310.6 16.6 %collective-permute-start.61 = (bf16[1,2,64,1024]{3,2,0,1:T(8,128)(2,1)S(1)}, bf16[1,2,64,1024]{3,2,0,1:T(8,128)(2,1)S(1)}, u32[]{:S(2)}, u32[]{:S(2)}) collective-permute-start(bf16[1,2,64,1024]{3,2,0,1:T(8,128)(2,1)S(1)} %get-tuple-element.488), channel_id=1, source_target_pairs={{0,16},{16,0},{1,17},{17,1},{2,18},{18,2},{3,19},{19,3},{4,20},{20... | collective-permute-start | bytes 786440 | tf_op jit(solution)/shard_map/ppermute | solution.py:373
  327.1 17.7 %collective-permute-start.65 = (bf16[2,3,256,128]{3,2,1,0:T(8,128)(2,1)S(1)}, bf16[2,3,256,128]{3,2,1,0:T(8,128)(2,1)S(1)}, u32[]{:S(2)}, u32[]{:S(2)}) collective-permute-start(bf16[2,3,256,128]{3,2,1,0:T(8,128)(2,1)S(1)} %constant_dynamic-update-slice_fusion.17), channel_id=1, source_target_pairs={{0,4},{2,6},{4,0},{6,2},{8,12},{10,14},{12,8},{14,10},{1,5},{3,7},... | collective-permute-start | bytes 1179656 | tf_op jit(solution)/shard_map/ppermute | solution.py:373
  327.3 17.6 %collective-permute-start.67 = (bf16[1,2,64,1024]{3,2,0,1:T(8,128)(2,1)S(1)}, bf16[1,2,64,1024]{3,2,0,1:T(8,128)(2,1)S(1)}, u32[]{:S(2)}, u32[]{:S(2)}) collective-permute-start(bf16[1,2,64,1024]{3,2,0,1:T(8,128)(2,1)S(1)} %add_convert_fusion.17), channel_id=1, source_target_pairs={{0,16},{16,0},{1,17},{17,1},{2,18},{18,2},{3,19},{19,3},{4,20},{20... | collective-permute-start | bytes 786440 | tf_op jit(solution)/shard_map/ppermute | solution.py:373
  331.4 15.6 %collective-permute-start.66 = (f32[12288]{0:T(1024)S(1)}, f32[12288]{0:T(1024)S(1)}, u32[]{:S(2)}, u32[]{:S(2)}) collective-permute-start(f32[12288]{0:T(1024)S(1)} %add.362), channel_id=1, source_target_pairs={{0,8},{2,10},{4,12},{6,14},{8,0},{10,2},{12,4},{14,6},{1,9},{3,11}... | collective-permute-start | bytes 147464 | tf_op jit(solution)/shard_map/ppermute | solution.py:373
  332.5 17.2 %collective-permute-start.62 = (bf16[1,2,512,128]{3,2,0,1:T(8,128)(2,1)S(1)}, bf16[1,2,512,128]{3,2,0,1:T(8,128)(2,1)S(1)}, u32[]{:S(2)}, u32[]{:S(2)}) collective-permute-start(bf16[1,2,512,128]{3,2,0,1:T(8,128)(2,1)S(1)} %add_convert_fusion.16), channel_id=1, source_target_pairs={{0,8},{2,10},{4,12},{6,14},{8,0},{10,2},{12,4},{14,6},{1,9},{3,11}... | collective-permute-start | bytes 786440 | tf_op jit(solution)/shard_map/ppermute | solution.py:373
  344.8 20.5 %collective-permute-start.69 = (bf16[4,2,128,384]{3,2,1,0:T(8,128)(2,1)S(1)}, bf16[4,2,128,384]{3,2,1,0:T(8,128)(2,1)S(1)}, u32[]{:S(2)}, u32[]{:S(2)}) collective-permute-start(bf16[4,2,128,384]{3,2,1,0:T(8,128)(2,1)S(1)} %pad_maximum_fusion.2), channel_id=1, source_target_pairs={{0,2},{2,0},{4,6},{6,4},{8,10},{10,8},{12,14},{14,12},{1,3},{3,1},... | collective-permute-start | bytes 2359304 | tf_op jit(solution)/shard_map/ppermute | solution.py:373
  344.9 37.2 %collective-permute-start.74 = (bf16[4,3,256,128]{3,2,1,0:T(8,128)(2,1)S(1)}, bf16[4,3,256,128]{3,2,1,0:T(8,128)(2,1)S(1)}, u32[]{:S(2)}, u32[]{:S(2)}) collective-permute-start(bf16[4,3,256,128]{3,2,1,0:T(8,128)(2,1)S(1)} %constant_dynamic-update-slice_fusion.21), channel_id=1, source_target_pairs={{0,2},{2,0},{4,6},{6,4},{8,10},{10,8},{12,14},{14,12},{1,3},{3,1},... | collective-permute-start | bytes 2359304 | tf_op jit(solution)/shard_map/ppermute | solution.py:373
  347.0 20.2 %collective-permute-start.70 = (bf16[2,2,64,1024]{3,2,0,1:T(8,128)(2,1)S(1)}, bf16[2,2,64,1024]{3,2,0,1:T(8,128)(2,1)S(1)}, u32[]{:S(2)}, u32[]{:S(2)}) collective-permute-start(bf16[2,2,64,1024]{3,2,0,1:T(8,128)(2,1)S(1)} %constant_dynamic-update-slice_fusion.23), channel_id=1, source_target_pairs={{0,8},{2,10},{4,12},{6,14},{8,0},{10,2},{12,4},{14,6},{1,9},{3,11}... | collective-permute-start | bytes 1572872 | tf_op jit(solution)/shard_map/ppermute | solution.py:373
  347.4 17.9 %collective-permute-start.71 = (bf16[4,32,1024]{2,1,0:T(8,128)(2,1)S(1)}, bf16[4,32,1024]{2,1,0:T(8,128)(2,1)S(1)}, u32[]{:S(2)}, u32[]{:S(2)}) collective-permute-start(bf16[4,32,1024]{2,1,0:T(8,128)(2,1)S(1)} %constant_dynamic-update-slice_fusion.25), channel_id=1, source_target_pairs={{0,16},{16,0},{1,17},{17,1},{2,18},{18,2},{3,19},{19,3},{4,20},{20... | collective-permute-start | bytes 786440 | tf_op jit(solution)/shard_map/ppermute | solution.py:373
  349.7 19.6 %collective-permute-start.68 = (bf16[2,2,512,128]{3,2,0,1:T(8,128)(2,1)S(1)}, bf16[2,2,512,128]{3,2,0,1:T(8,128)(2,1)S(1)}, u32[]{:S(2)}, u32[]{:S(2)}) collective-permute-start(bf16[2,2,512,128]{3,2,0,1:T(8,128)(2,1)S(1)} %constant_dynamic-update-slice_fusion.27), channel_id=1, source_target_pairs={{0,4},{2,6},{4,0},{6,2},{8,12},{10,14},{12,8},{14,10},{1,5},{3,7},... | collective-permute-start | bytes 1572872 | tf_op jit(solution)/shard_map/ppermute | solution.py:373
  369.4 17.8 %collective-permute-start.75 = (bf16[4,2,128,384]{3,2,1,0:T(8,128)(2,1)S(1)}, bf16[4,2,128,384]{3,2,1,0:T(8,128)(2,1)S(1)}, u32[]{:S(2)}, u32[]{:S(2)}) collective-permute-start(bf16[4,2,128,384]{3,2,1,0:T(8,128)(2,1)S(1)} %pad_maximum_fusion.3), channel_id=1, source_target_pairs={{0,4},{2,6},{4,0},{6,2},{8,12},{10,14},{12,8},{14,10},{1,5},{3,7},... | collective-permute-start | bytes 2359304 | tf_op jit(solution)/shard_map/ppermute | solution.py:373
  369.7 23.6 %collective-permute-start.72 = (bf16[4,512,128]{2,1,0:T(8,128)(2,1)S(1)}, bf16[4,512,128]{2,1,0:T(8,128)(2,1)S(1)}, u32[]{:S(2)}, u32[]{:S(2)}) collective-permute-start(bf16[4,512,128]{2,1,0:T(8,128)(2,1)S(1)} %get-tuple-element.377), channel_id=1, source_target_pairs={{0,2},{2,0},{4,6},{6,4},{8,10},{10,8},{12,14},{14,12},{1,3},{3,1},... | collective-permute-start | bytes 1572872 | tf_op jit(solution)/shard_map/ppermute | solution.py:373
  378.9 15.9 %collective-permute-start.73 = (bf16[4,512,128]{2,1,0:T(8,128)(2,1)S(1)}, bf16[4,512,128]{2,1,0:T(8,128)(2,1)S(1)}, u32[]{:S(2)}, u32[]{:S(2)}) collective-permute-start(bf16[4,512,128]{2,1,0:T(8,128)(2,1)S(1)} %get-tuple-element.379), channel_id=1, source_target_pairs={{0,16},{16,0},{1,17},{17,1},{2,18},{18,2},{3,19},{19,3},{4,20},{20... | collective-permute-start | bytes 1572872 | tf_op jit(solution)/shard_map/ppermute | solution.py:373
  382.3 58.0 %collective-permute-start.79 = (bf16[8,3,256,128]{3,2,1,0:T(8,128)(2,1)S(1)}, bf16[8,3,256,128]{3,2,1,0:T(8,128)(2,1)S(1)}, u32[]{:S(2)}, u32[]{:S(2)}) collective-permute-start(bf16[8,3,256,128]{3,2,1,0:T(8,128)(2,1)S(1)} %constant_dynamic-update-slice_fusion.35.chunks_ref), channel_id=1, source_target_pairs={{0,16},{16,0},{1,17},{17,1},{2,18},{18,2},{3,19},{19,3},{4,20},{20... | collective-permute-start | bytes 4718600 | tf_op jit(solution)/shard_map/ppermute | solution.py:373
  383.0 52.8 %collective-permute-start.80 = (bf16[4,64,1024]{2,1,0:T(8,128)(2,1)S(1)}, bf16[4,64,1024]{2,1,0:T(8,128)(2,1)S(1)}, u32[]{:S(2)}, u32[]{:S(2)}) collective-permute-start(bf16[4,64,1024]{2,1,0:T(8,128)(2,1)S(1)} %get-tuple-element.390), channel_id=1, source_target_pairs={{0,2},{2,0},{4,6},{6,4},{8,10},{10,8},{12,14},{14,12},{1,3},{3,1},... | collective-permute-start | bytes 1572872 | tf_op jit(solution)/shard_map/ppermute | solution.py:373
  387.2 48.6 %collective-permute-start.81 = (bf16[4,64,1024]{2,1,0:T(8,128)(2,1)S(1)}, bf16[4,64,1024]{2,1,0:T(8,128)(2,1)S(1)}, u32[]{:S(2)}, u32[]{:S(2)}) collective-permute-start(bf16[4,64,1024]{2,1,0:T(8,128)(2,1)S(1)} %get-tuple-element.392), channel_id=1, source_target_pairs={{0,4},{2,6},{4,0},{6,2},{8,12},{10,14},{12,8},{14,10},{1,5},{3,7},... | collective-permute-start | bytes 1572872 | tf_op jit(solution)/shard_map/ppermute | solution.py:373
  393.3 41.2 %collective-permute-start.82 = (bf16[8,32,1024]{2,1,0:T(8,128)(2,1)S(1)}, bf16[8,32,1024]{2,1,0:T(8,128)(2,1)S(1)}, u32[]{:S(2)}, u32[]{:S(2)}) collective-permute-start(bf16[8,32,1024]{2,1,0:T(8,128)(2,1)S(1)} %constant_dynamic-update-slice_fusion.29.chunks_ref), channel_id=1, source_target_pairs={{0,8},{2,10},{4,12},{6,14},{8,0},{10,2},{12,4},{14,6},{1,9},{3,11}... | collective-permute-start | bytes 1572872 | tf_op jit(solution)/shard_map/ppermute | solution.py:373
  394.7 50.1 %collective-permute-start.78 = (bf16[4,2,128,384]{3,2,1,0:T(8,128)(2,1)S(1)}, bf16[4,2,128,384]{3,2,1,0:T(8,128)(2,1)S(1)}, u32[]{:S(2)}, u32[]{:S(2)}) collective-permute-start(bf16[4,2,128,384]{3,2,1,0:T(8,128)(2,1)S(1)} %pad_maximum_fusion.4), channel_id=1, source_target_pairs={{0,8},{2,10},{4,12},{6,14},{8,0},{10,2},{12,4},{14,6},{1,9},{3,11}... | collective-permute-start | bytes 2359304 | tf_op jit(solution)/shard_map/ppermute | solution.py:373
  434.5 16.2 %collective-permute-start.76 = (bf16[8,512,128]{2,1,0:T(8,128)(2,1)S(1)}, bf16[8,512,128]{2,1,0:T(8,128)(2,1)S(1)}, u32[]{:S(2)}, u32[]{:S(2)}) collective-permute-start(bf16[8,512,128]{2,1,0:T(8,128)(2,1)S(1)} %constant_dynamic-update-slice_fusion.37.chunks_ref), channel_id=1, source_target_pairs={{0,16},{16,0},{1,17},{17,1},{2,18},{18,2},{3,19},{19,3},{4,20},{20... | collective-permute-start | bytes 3145736 | tf_op jit(solution)/shard_map/ppermute | solution.py:373
  435.8 15.0 %collective-permute-start.77 = (bf16[8,512,128]{2,1,0:T(8,128)(2,1)S(1)}, bf16[8,512,128]{2,1,0:T(8,128)(2,1)S(1)}, u32[]{:S(2)}, u32[]{:S(2)}) collective-permute-start(bf16[8,512,128]{2,1,0:T(8,128)(2,1)S(1)} %constant_dynamic-update-slice_fusion.39.chunks_ref), channel_id=1, source_target_pairs={{0,2},{2,0},{4,6},{6,4},{8,10},{10,8},{12,14},{14,12},{1,3},{3,1},... | collective-permute-start | bytes 3145736 | tf_op jit(solution)/shard_map/ppermute | solution.py:373
  435.9 19.1 %collective-permute-start.83 = (bf16[8,64,1024]{2,1,0:T(8,128)(2,1)S(1)}, bf16[8,64,1024]{2,1,0:T(8,128)(2,1)S(1)}, u32[]{:S(2)}, u32[]{:S(2)}) collective-permute-start(bf16[8,64,1024]{2,1,0:T(8,128)(2,1)S(1)} %constant_dynamic-update-slice_fusion.41.chunks_ref), channel_id=1, source_target_pairs={{0,4},{2,6},{4,0},{6,2},{8,12},{10,14},{12,8},{14,10},{1,5},{3,7},... | collective-permute-start | bytes 3145736 | tf_op jit(solution)/shard_map/ppermute | solution.py:373
  440.3 21.5 %collective-permute-start.84 = (bf16[8,64,1024]{2,1,0:T(8,128)(2,1)S(1)}, bf16[8,64,1024]{2,1,0:T(8,128)(2,1)S(1)}, u32[]{:S(2)}, u32[]{:S(2)}) collective-permute-start(bf16[8,64,1024]{2,1,0:T(8,128)(2,1)S(1)} %constant_dynamic-update-slice_fusion.43.chunks_ref), channel_id=1, source_target_pairs={{0,2},{2,0},{4,6},{6,4},{8,10},{10,8},{12,14},{14,12},{1,3},{3,1},... | collective-permute-start | bytes 3145736 | tf_op jit(solution)/shard_map/ppermute | solution.py:373
  (67 other events, 600.5 us)
